TPU v7x, 32 devices: a whole 2x2x4 slice. The times are simulated.
32 devices in a mesh: section: 2 (over y), dp: 16 (over z, x, core).
Axes of the slice: x: 2, y: 2, z: 4, core: 2. Of those that a mesh axis runs over, the one named last changes fastest.
Arguments:
- inputs: bfloat16 [256, 64, 768], P('dp'), may hold values from -6 to 6
- cotangent: bfloat16 [2, 256, 64, 768], P('section', 'dp'), may hold values from -6 to 6
- images: bfloat16 [16, 576, 768], P('dp', 'section'), may hold values from -6 to 6
- seg_ids: int32 [256, 64], P('dp'), may hold values from 0 to 1, as said below
- row_block: int32 [256], P('dp'), may hold values from 0 to 15, as said below
- seg_image: int32 [256, 2], P('dp'), may hold values from 0 to 1, as said below
- ln1_gain: float32 [2, 768], P('section'), may hold values from 0.5 to 1.5
- ln1_bias: float32 [2, 768], P('section'), may hold values from -3 to 3
- w_qkv: bfloat16 [2, 768, 2304], P('section'), may hold values from -0.21875 to 0.21875
- w_out: bfloat16 [2, 768, 768], P('section'), may hold values from -0.875 to 0.875
- ln2_gain: float32 [2, 768], P('section'), may hold values from 0.5 to 1.5
- ln2_bias: float32 [2, 768], P('section'), may hold values from -3 to 3
- w_up: bfloat16 [2, 768, 3072], P('section'), may hold values from -0.21875 to 0.21875
- b_up: float32 [2, 3072], P('section'), may hold values from -3 to 3
- w_down: bfloat16 [2, 3072, 768], P('section'), may hold values from -0.109375 to 0.109375
- b_down: float32 [2, 768], P('section'), may hold values from -3 to 3
- lnc_gain: float32 [768], replicated, may hold values from 0.5 to 1.5
- lnc_bias: float32 [768], replicated, may hold values from -3 to 3
- wq_cross: bfloat16 [768, 768], replicated, may hold values from -0.21875 to 0.21875
- wkv_cross: bfloat16 [768, 1536], replicated, may hold values from -0.21875 to 0.21875
- wo_cross: bfloat16 [768, 768], replicated, may hold values from -3 to 3
Outputs:
- activations: float32 [2, 256, 64, 768], P('section', 'dp')
- back_grads: float32 [2, 256, 64, 768], P('section', 'dp')
- image_grad: float32 [16, 576, 768], P('dp', 'section')
- grad_ln1_gain: float32 [2, 768], P('section', 'dp')
- grad_ln1_bias: float32 [2, 768], P('section', 'dp')
- grad_w_qkv: float32 [2, 768, 2304], P('section', 'dp')
- grad_w_out: float32 [2, 768, 768], P('section', 'dp')
- grad_ln2_gain: float32 [2, 768], P('section', 'dp')
- grad_ln2_bias: float32 [2, 768], P('section', 'dp')
- grad_w_up: float32 [2, 768, 3072], P('section', 'dp')
- grad_b_up: float32 [2, 3072], P('section', 'dp')
- grad_w_down: float32 [2, 3072, 768], P('section', 'dp')
- grad_b_down: float32 [2, 768], P('section', 'dp')
- grad_lnc_gain: float32 [768], P('dp')
- grad_lnc_bias: float32 [768], P('dp')
- grad_wq_cross: float32 [768, 768], P('dp')
- grad_wkv_cross: float32 [768, 1536], P('dp')
- grad_wo_cross: float32 [768, 768], P('dp')
Inputs may be any that keep to these rules, and one draw needn't show every extreme that they name: `seg_ids`: in every row caption 0 holds the first positions and caption 1 the rest; each caption has 16 to 48 positions, and row 0's first caption has exactly 48. `row_block`: for row r it is r // 16 - 1 or that number itself, modulo 16; the first row of each group of 16 rows takes the former, the last row the latter. Caption j of row r describes image (row_block[r] + seg_image[r, j]) modulo 16; in the first row of each group of 16 rows caption 0 takes 0, in the last row caption 1 takes 1.
All inputs are finite; a program needn't handle non-finite values.
Results may differ from a plain program's by a relative error of at most 0.025.
Values may be sent and summed in bfloat16 or wider, within the bound.
A program may use at most 640 MiB of HBM per device.

v0:
```python
from functools import partial

import jax
import jax.numpy as jnp
from jax import lax
from jax.sharding import PartitionSpec as P

H = 12
HD = 64
MICRO = 2


EPS = 1e-05
MASKED = -1e30


def with_halo(x, sides, width):
    for axis, dim in sides:
        size, length = (lax.axis_size(axis), x.shape[dim])
        up = [(i, (i + 1) % size) for i in range(size)]
        down = [(j, i) for i, j in up]
        last = lax.slice_in_dim(x, length - width, length, axis=dim)
        first = lax.slice_in_dim(x, 0, width, axis=dim)
        before = lax.ppermute(last, axis, up)
        after = lax.ppermute(first, axis, down)
        x = jnp.concatenate([before, x, after], axis=dim)
    return x


def passed_along(block, axis, distance):
    devices = range(lax.axis_size(axis))
    route = [(i - distance, i) for i in devices if i - distance in devices]
    return lax.ppermute(block, axis, route)


def norm_apply(stream, gain_vec, bias_vec):
    middle = jnp.mean(stream, -1, keepdims=True)
    centred = stream - middle
    spread = jnp.mean(centred * centred, -1, keepdims=True)
    return centred * lax.rsqrt(spread + EPS) * gain_vec + bias_vec


def matmul(left_in, right_in):
    return jnp.einsum("...d,de->...e", left_in, right_in, preferred_element_type=jnp.float32)


def matmul_back(gradient, weight):
    return jnp.einsum("...e,de->...d", gradient, weight, preferred_element_type=jnp.float32)


def outer_sum(left_in, right_in):
    return jnp.einsum("rtd,rte->de", left_in, right_in, preferred_element_type=jnp.float32)


def column_sum(gradient):
    return jnp.sum(gradient.astype(jnp.float32), (0, 1))


def attend(queries, key_rows, value_rows, allowed):
    factor = HD ** (-0.5)
    scores = (
        jnp.einsum("rqhd,rkhd->rhqk", queries, key_rows, preferred_element_type=jnp.float32)
        * factor
    )
    scores = jnp.where(allowed[:, None], scores, MASKED)
    highest = jnp.max(scores, -1, keepdims=True)
    expo = jnp.exp(scores - highest)
    attn_probs = expo / jnp.sum(expo, -1, keepdims=True)
    mixed_out = jnp.einsum(
        "rhqk,rkhd->rqhd",
        attn_probs.astype(jnp.bfloat16),
        value_rows,
        preferred_element_type=jnp.float32,
    )
    return (mixed_out, attn_probs)


def attend_back(queries, key_rows, value_rows, attn_probs, grad_mixed):
    factor = HD ** (-0.5)
    grad_probs = jnp.einsum(
        "rqhd,rkhd->rhqk", grad_mixed, value_rows, preferred_element_type=jnp.float32
    )
    grad_scores = attn_probs * (grad_probs - jnp.sum(attn_probs * grad_probs, -1, keepdims=True))
    narrow = grad_scores.astype(jnp.bfloat16)
    grad_q = (
        jnp.einsum("rhqk,rkhd->rqhd", narrow, key_rows, preferred_element_type=jnp.float32) * factor
    )
    grad_k = (
        jnp.einsum("rhqk,rqhd->rkhd", narrow, queries, preferred_element_type=jnp.float32) * factor
    )
    grad_v = jnp.einsum(
        "rhqk,rqhd->rkhd",
        attn_probs.astype(jnp.bfloat16),
        grad_mixed,
        preferred_element_type=jnp.float32,
    )
    return (grad_q, grad_k, grad_v)


def zero_grads(weights, cross_parts):
    layer_zero = tuple((jnp.zeros(weight.shape, jnp.float32) for weight in weights))
    cross_zero = tuple((jnp.zeros(weight.shape, jnp.float32) for weight in cross_parts[2:]))
    pool_zero = jnp.zeros(cross_parts[0].shape, jnp.float32)
    return (layer_zero, cross_zero, pool_zero)


def layer_forward(hidden, seg_rows, weights, cross_parts, with_cross):
    (
        gain_one,
        bias_one,
        w_triple,
        w_mix,
        gain_two,
        bias_two,
        w_expand,
        b_expand,
        w_reduce,
        b_reduce,
    ) = weights
    row_count, seq_len = seg_rows.shape
    stored = {}
    normed = norm_apply(hidden, gain_one, bias_one).astype(jnp.bfloat16)
    triple = matmul(normed, w_triple).astype(jnp.bfloat16).reshape(row_count, seq_len, 3, H, HD)
    positions = jnp.arange(seq_len)
    allowed = (seg_rows[:, :, None] == seg_rows[:, None, :]) & (
        positions[:, None] >= positions[None, :]
    )[None]
    mixed_out, attn_probs = attend(triple[:, :, 0], triple[:, :, 1], triple[:, :, 2], allowed)
    mixed_out = mixed_out.reshape(row_count, seq_len, H * HD).astype(jnp.bfloat16)
    hidden_two = hidden + matmul(mixed_out, w_mix)
    stored["hidden"] = hidden
    stored["normed"] = normed
    stored["triple"] = triple
    stored["attn_probs"] = attn_probs
    stored["mixed_out"] = mixed_out
    stored["hidden_two"] = hidden_two
    hidden_three = hidden_two
    if with_cross:
        image_pool, slot_ids, cross_gain, cross_bias, w_query, w_back = cross_parts
        cross_in = norm_apply(hidden_two, cross_gain, cross_bias).astype(jnp.bfloat16)
        queries = matmul(cross_in, w_query).astype(jnp.bfloat16).reshape(row_count, seq_len, H, HD)
        chosen = image_pool[slot_ids].reshape(
            row_count, slot_ids.shape[1] * image_pool.shape[1], 2, H, HD
        )
        owners = jnp.arange(chosen.shape[1]) // image_pool.shape[1]
        cross_allowed = seg_rows[:, :, None] == owners[None, None, :]
        cross_mixed, cross_probs = attend(queries, chosen[:, :, 0], chosen[:, :, 1], cross_allowed)
        cross_mixed = cross_mixed.reshape(row_count, seq_len, H * HD).astype(jnp.bfloat16)
        hidden_three = hidden_two + matmul(cross_mixed, w_back)
        stored["cross_in"] = cross_in
        stored["queries"] = queries
        stored["chosen"] = chosen
        stored["cross_probs"] = cross_probs
        stored["cross_mixed"] = cross_mixed
    ffn_in = norm_apply(hidden_three, gain_two, bias_two).astype(jnp.bfloat16)
    pre_act = matmul(ffn_in, w_expand) + b_expand
    active = jax.nn.gelu(pre_act, approximate=False).astype(jnp.bfloat16)
    result = hidden_three + matmul(active, w_reduce) + b_reduce
    stored["hidden_three"] = hidden_three
    stored["ffn_in"] = ffn_in
    stored["pre_act"] = pre_act
    stored["active"] = active
    return (result, stored)


def layer_backward(stored, grad_out, weights, cross_parts, with_cross):
    (
        gain_one,
        bias_one,
        w_triple,
        w_mix,
        gain_two,
        bias_two,
        w_expand,
        b_expand,
        w_reduce,
        b_reduce,
    ) = weights
    row_count, seq_len = (grad_out.shape[0], grad_out.shape[1])
    low_out = grad_out.astype(jnp.bfloat16)
    d_reduce = outer_sum(stored["active"], low_out)
    d_breduce = column_sum(low_out)
    grad_active = matmul_back(low_out, w_reduce)
    _, gelu_pull = jax.vjp(partial(jax.nn.gelu, approximate=False), stored["pre_act"])
    low_pre = gelu_pull(grad_active)[0].astype(jnp.bfloat16)
    d_expand = outer_sum(stored["ffn_in"], low_pre)
    d_bexpand = column_sum(low_pre)
    grad_ffn = matmul_back(low_pre, w_expand)
    _, norm_pull = jax.vjp(norm_apply, stored["hidden_three"], gain_two, bias_two)
    part_three, d_gain_two, d_bias_two = norm_pull(grad_ffn)
    grad_three = grad_out + part_three
    grad_two = grad_three
    _, cross_grads, pool_grad = zero_grads(weights, cross_parts)
    if with_cross:
        image_pool, slot_ids, cross_gain, cross_bias, w_query, w_back = cross_parts
        low_three = grad_three.astype(jnp.bfloat16)
        d_back = outer_sum(stored["cross_mixed"], low_three)
        grad_cmix = (
            matmul_back(low_three, w_back).astype(jnp.bfloat16).reshape(row_count, seq_len, H, HD)
        )
        chosen = stored["chosen"]
        grad_q, grad_k, grad_v = attend_back(
            stored["queries"], chosen[:, :, 0], chosen[:, :, 1], stored["cross_probs"], grad_cmix
        )
        low_query = grad_q.reshape(row_count, seq_len, H * HD).astype(jnp.bfloat16)
        d_query = outer_sum(stored["cross_in"], low_query)
        grad_cin = matmul_back(low_query, w_query)
        _, cross_pull = jax.vjp(norm_apply, stored["hidden_two"], cross_gain, cross_bias)
        part_two, d_cgain, d_cbias = cross_pull(grad_cin)
        grad_two = grad_three + part_two
        pair_grad = jnp.stack([grad_k, grad_v], 2).reshape(row_count * slot_ids.shape[1], -1)
        one_hot = (
            slot_ids.reshape(-1)[:, None] == jnp.arange(image_pool.shape[0])[None, :]
        ).astype(jnp.float32)
        pool_grad = jnp.einsum(
            "ni,nc->ic", one_hot, pair_grad, precision=lax.Precision.HIGHEST
        ).reshape(image_pool.shape)
        cross_grads = (d_cgain, d_cbias, d_query, d_back)
    low_two = grad_two.astype(jnp.bfloat16)
    d_mix = outer_sum(stored["mixed_out"], low_two)
    grad_mix = matmul_back(low_two, w_mix).astype(jnp.bfloat16).reshape(row_count, seq_len, H, HD)
    triple = stored["triple"]
    grad_q, grad_k, grad_v = attend_back(
        triple[:, :, 0], triple[:, :, 1], triple[:, :, 2], stored["attn_probs"], grad_mix
    )
    low_triple = jnp.stack([grad_q, grad_k, grad_v], 2).reshape(row_count, seq_len, 3 * H * HD)
    low_triple = low_triple.astype(jnp.bfloat16)
    d_triple = outer_sum(stored["normed"], low_triple)
    grad_normed = matmul_back(low_triple, w_triple)
    _, first_pull = jax.vjp(norm_apply, stored["hidden"], gain_one, bias_one)
    part_one, d_gain_one, d_bias_one = first_pull(grad_normed)
    grad_in = grad_two + part_one
    layer_grads = (
        d_gain_one,
        d_bias_one,
        d_triple,
        d_mix,
        d_gain_two,
        d_bias_two,
        d_expand,
        d_bexpand,
        d_reduce,
        d_breduce,
    )
    return (grad_in, layer_grads, cross_grads, pool_grad)


def per_device(
    inputs,
    cotangent,
    images,
    seg_ids,
    row_block,
    seg_image,
    ln1_gain,
    ln1_bias,
    w_qkv,
    w_out,
    ln2_gain,
    ln2_bias,
    w_up,
    b_up,
    w_down,
    b_down,
    lnc_gain,
    lnc_bias,
    wq_cross,
    wkv_cross,
    wo_cross,
):
    is_upper = lax.axis_index("section") == 1
    dp_index = lax.axis_index("dp")
    dp_count = lax.axis_size("dp")
    weights = (
        ln1_gain[0],
        ln1_bias[0],
        w_qkv[0],
        w_out[0],
        ln2_gain[0],
        ln2_bias[0],
        w_up[0],
        b_up[0],
        w_down[0],
        b_down[0],
    )
    image_count = images.shape[0]
    half_len = images.shape[1]
    half_pairs = matmul(images, wkv_cross).astype(jnp.bfloat16)
    beside_all = with_halo(half_pairs, (("dp", 0),), image_count)
    lifted = passed_along(beside_all, "section", 1)
    image_pool = jnp.concatenate([lifted, beside_all], 1)
    slot_all = (row_block[:, None] + seg_image - dp_index + 1) % dp_count
    rows_mb = inputs.shape[0] // MICRO

    def part_rows(array, micro_index):
        return array[micro_index * rows_mb : (micro_index + 1) * rows_mb]

    def cross_of(micro_index):
        return (
            image_pool,
            part_rows(slot_all, micro_index),
            lnc_gain,
            lnc_bias,
            wq_cross,
            wo_cross,
        )

    received = jnp.zeros((rows_mb,) + inputs.shape[1:], jnp.bfloat16)
    section_inputs = []
    section_outputs = []
    for moment in range(MICRO + 1):
        low_index = min(moment, MICRO - 1)
        high_index = max(moment - 1, 0)
        hidden = jnp.where(is_upper, received, part_rows(inputs, low_index)).astype(jnp.float32)
        seg_rows = jnp.where(
            is_upper, part_rows(seg_ids, high_index), part_rows(seg_ids, low_index)
        )
        cross_parts = cross_of(high_index)

        def upper_forward():
            return layer_forward(hidden, seg_rows, weights, cross_parts, True)[0]

        def lower_forward():
            return layer_forward(hidden, seg_rows, weights, cross_parts, False)[0]

        def spare_forward():
            return jnp.zeros_like(hidden)

        if moment == 0:
            result = lax.cond(is_upper, spare_forward, lower_forward)
        elif moment == MICRO:
            result = lax.cond(is_upper, upper_forward, spare_forward)
        else:
            result = lax.cond(is_upper, upper_forward, lower_forward)
        section_inputs.append(hidden)
        section_outputs.append(result)
        if moment < MICRO:
            received = passed_along(result.astype(jnp.bfloat16), "section", 1)
    layer_total, cross_total, pool_total = zero_grads(weights, cross_of(0))
    returned = jnp.zeros((rows_mb,) + inputs.shape[1:], jnp.bfloat16)
    own_cotangent = cotangent[0].astype(jnp.float32)
    upper_rows = [None] * MICRO
    lower_rows = [None] * MICRO
    for moment in range(MICRO + 1):
        high_index = max(MICRO - 1 - moment, 0)
        low_index = min(MICRO - moment, MICRO - 1)
        hidden = jnp.where(is_upper, section_inputs[high_index + 1], section_inputs[low_index])
        seg_rows = jnp.where(
            is_upper, part_rows(seg_ids, high_index), part_rows(seg_ids, low_index)
        )
        cross_parts = cross_of(high_index)
        grad_out = jnp.where(
            is_upper,
            part_rows(own_cotangent, high_index),
            part_rows(own_cotangent, low_index) + returned.astype(jnp.float32),
        )

        def upper_backward():
            stored = layer_forward(hidden, seg_rows, weights, cross_parts, True)[1]
            return layer_backward(stored, grad_out, weights, cross_parts, True)

        def lower_backward():
            stored = layer_forward(hidden, seg_rows, weights, cross_parts, False)[1]
            return layer_backward(stored, grad_out, weights, cross_parts, False)

        def spare_backward():
            layer_zero, cross_zero, pool_zero = zero_grads(weights, cross_parts)
            return (jnp.zeros_like(hidden), layer_zero, cross_zero, pool_zero)

        if moment == 0:
            outcome = lax.cond(is_upper, upper_backward, spare_backward)
        elif moment == MICRO:
            outcome = lax.cond(is_upper, spare_backward, lower_backward)
        else:
            outcome = lax.cond(is_upper, upper_backward, lower_backward)
        grad_in, layer_grads, cross_grads, pool_grad = outcome
        layer_total = jax.tree.map(jnp.add, layer_total, layer_grads)
        cross_total = jax.tree.map(jnp.add, cross_total, cross_grads)
        pool_total = pool_total + pool_grad
        if moment < MICRO:
            upper_rows[high_index] = grad_in
        if moment > 0:
            lower_rows[low_index] = grad_in
        if moment < MICRO:
            returned = passed_along(grad_in.astype(jnp.bfloat16), "section", -1)
    pool_low = pool_total.astype(jnp.bfloat16)
    dropped = passed_along(pool_low[:, :half_len], "section", -1)
    own_part = jnp.where(is_upper, pool_low[:, half_len:], dropped)
    edge_grads = jnp.concatenate([own_part[:image_count], own_part[2 * image_count :]], 0)
    beside_all = with_halo(edge_grads, (("dp", 0),), image_count)
    summed = (
        own_part[image_count : 2 * image_count].astype(jnp.float32)
        + beside_all[:image_count].astype(jnp.float32)
        + beside_all[3 * image_count :].astype(jnp.float32)
    )
    key_grad = summed.astype(jnp.bfloat16)
    image_grad = jnp.einsum("ite,de->itd", key_grad, wkv_cross, preferred_element_type=jnp.float32)
    d_pairs = jnp.einsum("itd,ite->de", images, key_grad, preferred_element_type=jnp.float32)
    activations = jnp.concatenate(
        [
            jnp.where(is_upper, section_outputs[micro_index + 1], section_outputs[micro_index])
            for micro_index in range(MICRO)
        ],
        0,
    )[None]
    back_grads = jnp.concatenate(
        [
            jnp.where(is_upper, upper_rows[micro_index], lower_rows[micro_index])
            for micro_index in range(MICRO)
        ],
        0,
    )[None]
    layer_sum = (
        lax.psum_scatter(layer_total[0][None], "dp", scatter_dimension=1, tiled=True),
        lax.psum_scatter(layer_total[1][None], "dp", scatter_dimension=1, tiled=True),
        lax.psum_scatter(layer_total[2][None], "dp", scatter_dimension=1, tiled=True),
        lax.psum_scatter(layer_total[3][None], "dp", scatter_dimension=1, tiled=True),
        lax.psum_scatter(layer_total[4][None], "dp", scatter_dimension=1, tiled=True),
        lax.psum_scatter(layer_total[5][None], "dp", scatter_dimension=1, tiled=True),
        lax.psum_scatter(layer_total[6][None], "dp", scatter_dimension=1, tiled=True),
        lax.psum_scatter(layer_total[7][None], "dp", scatter_dimension=1, tiled=True),
        lax.psum_scatter(layer_total[8][None], "dp", scatter_dimension=1, tiled=True),
        lax.psum_scatter(layer_total[9][None], "dp", scatter_dimension=1, tiled=True),
    )
    cross_part = (
        lax.psum_scatter(cross_total[0], "dp", scatter_dimension=0, tiled=True),
        lax.psum_scatter(cross_total[1], "dp", scatter_dimension=0, tiled=True),
        lax.psum_scatter(cross_total[2], "dp", scatter_dimension=0, tiled=True),
        lax.psum_scatter(d_pairs, "dp", scatter_dimension=0, tiled=True),
        lax.psum_scatter(cross_total[3], "dp", scatter_dimension=0, tiled=True),
    )
    cross_sum = (
        lax.psum(cross_part[0].astype(jnp.bfloat16), "section").astype(jnp.float32),
        lax.psum(cross_part[1].astype(jnp.bfloat16), "section").astype(jnp.float32),
        lax.psum(cross_part[2].astype(jnp.bfloat16), "section").astype(jnp.float32),
        lax.psum(cross_part[3].astype(jnp.bfloat16), "section").astype(jnp.float32),
        lax.psum(cross_part[4].astype(jnp.bfloat16), "section").astype(jnp.float32),
    )
    return (
        activations,
        back_grads,
        image_grad,
        layer_sum[0],
        layer_sum[1],
        layer_sum[2],
        layer_sum[3],
        layer_sum[4],
        layer_sum[5],
        layer_sum[6],
        layer_sum[7],
        layer_sum[8],
        layer_sum[9],
        cross_sum[0],
        cross_sum[1],
        cross_sum[2],
        cross_sum[3],
        cross_sum[4],
    )


def solution(mesh):
    placed = (
        P("dp", None, None),
        P("section", "dp", None, None),
        P("dp", "section", None),
        P("dp", None),
        P("dp"),
        P("dp", None),
        P("section", None),
        P("section", None),
        P("section", None, None),
        P("section", None, None),
        P("section", None),
        P("section", None),
        P("section", None, None),
        P("section", None),
        P("section", None, None),
        P("section", None),
        P(),
        P(),
        P(),
        P(),
        P(),
    )
    return jax.shard_map(
        per_device,
        mesh=mesh,
        in_specs=placed,
        out_specs=(
            P("section", "dp", None, None),
            P("section", "dp", None, None),
            P("dp", "section", None),
            P("section", "dp"),
            P("section", "dp"),
            P("section", "dp", None),
            P("section", "dp", None),
            P("section", "dp"),
            P("section", "dp"),
            P("section", "dp", None),
            P("section", "dp"),
            P("section", "dp", None),
            P("section", "dp"),
            P("dp"),
            P("dp"),
            P("dp", None),
            P("dp", None),
            P("dp", None),
        ),
        check_vma=False,
    )
```

profile of v0, /device:TPU:0, one launch (start us, length us, event | category | flops | bytes accessed | tf_op | source)
XLA Modules:
  0.0 3116.5 jit_solution(2680269349803676793)
XLA Ops:
  42.0 66.6 %conditional.6 = (f32[8,64,768]{2,1,0:T(8,128)}) conditional(s32[]{:T(128)} %convert_element_type.564, (f32[8,64,768]{2,1,0:T(8,128)}, f32[1,768]{1,0:T(1,128)S(1)}, f32[1,768]{1,0:T(1,128)S(1)}, bf16[768,2304]{1,0:T(8,128)(2,1)}, s32[8,64]{1,0:T(8,128)}, /*index=5*/bf16[768,768]{1,0:T(8,128)(2,1)S(1)}, f32[1,768]{1,0:T(1,128)S(1)}, ...), branch_computations={%region_0.7_spmd, %region_7.8_spmd} | conditional | flops 7494767616 | bytes 103423264 | solution.py:330
  90.0 18.2 add_add_fusion
  114.7 14.0 collective-permute-done
  135.9 77.3 %conditional.7 = (f32[8,64,768]{2,1,0:T(8,128)}) conditional(s32[]{:T(128)} %convert_element_type.564, (f32[8,64,768]{2,1,0:T(8,128)}, f32[1,768]{1,0:T(1,128)S(1)}, f32[1,768]{1,0:T(1,128)S(1)}, bf16[768,2304]{1,0:T(8,128)(2,1)}, s32[8,64]{1,0:T(8,128)S(1)}, /*index=5*/bf16[768,768]{1,0:T(8,128)(2,1)S(1)}, f32[1,768]{1,0:T(1,128)S(1)}, ...), branch_computations={%region_8.15_spmd, %region_15.26_spmd} | conditional | flops 10562453504 | bytes 437377984 | solution.py:334
  182.9 18.2 add_add_fusion.1
  214.8 178.5 %collective-permute-start.4 = (bf16[8,64,768]{2,1,0:T(8,128)(2,1)S(1)}, bf16[8,64,768]{2,1,0:T(8,128)(2,1)S(1)}, u32[]{:S(2)}, u32[]{:S(2)}) collective-permute-start(bf16[8,64,768]{2,1,0:T(8,128)(2,1)S(1)} %convert_element_type.570), channel_id=1, source_target_pairs={{0,16},{1,17},{2,18},{3,19},{4,20},{5,21},{6,22},{7,23},{8,24},{9,... | collective-permute-start | bytes 2359304 | tf_op jit(solution)/shard_map/ppermute | solution.py:33
  396.4 14.3 collective-permute-done.4
  412.0 30.7 conditional.9
  446.1 742.6 %collective-permute-done.5 = bf16[8,64,768]{2,1,0:T(8,128)(2,1)S(1)} collective-permute-done((bf16[8,64,768]{2,1,0:T(8,128)(2,1)S(1)}, bf16[8,64,768]{2,1,0:T(8,128)(2,1)S(1)}, u32[]{:S(2)}, u32[]{:S(2)}) %collective-permute-start.5) | collective-permute-done | bytes 786464 | tf_op jit(solution)/shard_map/ppermute | solution.py:33
  1192.0 164.5 %conditional.10 = (f32[8,64,768]{2,1,0:T(8,128)}, f32[768]{0:T(1024)}, f32[768]{0:T(1024)}, f32[768,2304]{1,0:T(8,128)}, f32[768,768]{1,0:T(8,128)}, /*index=5*/...) conditional(s32[]{:T(128)} %convert_element_type.564, ...), branch_computations={%region_66.84_spmd, %region_84.111_spmd} | conditional | flops 29549268992 | bytes 1423976064 | solution.py:375
  1241.1 15.5 fusion.209
  1359.4 615.8 %collective-permute-done.6 = bf16[8,64,768]{2,1,0:T(8,128)(2,1)S(1)} collective-permute-done((bf16[8,64,768]{2,1,0:T(8,128)(2,1)S(1)}, bf16[8,64,768]{2,1,0:T(8,128)(2,1)S(1)}, u32[]{:S(2)}, u32[]{:S(2)}) %collective-permute-start.6) | collective-permute-done | bytes 786464 | tf_op jit(solution)/shard_map/ppermute | solution.py:33
  1976.4 144.6 %conditional.11 = (f32[8,64,768]{2,1,0:T(8,128)}, f32[768]{0:T(1024)}, f32[768]{0:T(1024)}, f32[768,2304]{1,0:T(8,128)}, f32[768,768]{1,0:T(8,128)}, /*index=5*/...) conditional(s32[]{:T(128)} %convert_element_type.564, ...), branch_computations={%region_111.129_spmd, %region_129.130_spmd} | conditional | flops 19837419520 | bytes 349339808 | solution.py:373
  2026.3 15.4 fusion.255
  2143.5 55.2 %collective-permute-done.7 = bf16[3,288,1536]{2,1,0:T(8,128)(2,1)} collective-permute-done((bf16[3,288,1536]{2,1,0:T(8,128)(2,1)}, bf16[3,288,1536]{2,1,0:T(8,128)(2,1)}, u32[]{:S(2)}, u32[]{:S(2)}) %collective-permute-start.7) | collective-permute-done | bytes 2654240 | tf_op jit(solution)/shard_map/ppermute | solution.py:33
  2254.1 76.9 %reduce-scatter.52.cloned.1.call-done = f32[48,1536]{1,0:T(8,128)} async-done(((f32[768,1536]{1,0:T(8,128)}), f32[48,1536]{1,0:T(8,128)}) %reduce-scatter.52.cloned.1.call-update) | async-done | bytes 294928
  2349.4 15.0 add_bitcast_fusion.1
  2389.0 30.5 all-reduce.2
  2419.6 238.0 %all-reduce.3 = (bf16[48]{0:T(256)(128)(2,1)S(1)}, bf16[48]{0:T(256)(128)(2,1)S(1)}) all-reduce(bf16[48]{0:T(256)(128)(2,1)S(1)} %dynamic-slice.7, bf16[48]{0:T(256)(128)(2,1)S(1)} %dynamic-slice.6), channel_id=1, replica_groups=mesh['section'=2,'dp'=16] {'section'}, use_global_device_ids=true, to_apply=%region_141.142 | all-reduce | flops 96 | bytes 384 | tf_op jit(solution)/shard_map/psum | solution.py:433
  2689.5 27.1 all-reduce.7.cloned.1.call-done
  2721.6 62.3 %reduce-scatter.30.cloned.1.call-done = f32[1,48,768]{2,1,0:T(8,128)} async-done(((f32[1,768,768]{2,1,0:T(8,128)}), f32[1,48,768]{2,1,0:T(8,128)}) %reduce-scatter.30.cloned.1.call-update) | async-done | bytes 147472 | tf_op jit(solution)/shard_map/reduce_scatter | solution.py:417
  2783.9 94.0 %reduce-scatter.28.cloned.1.call-done = f32[1,48,2304]{2,1,0:T(8,128)} async-done(((f32[1,768,2304]{2,1,0:T(8,128)}), f32[1,48,2304]{2,1,0:T(8,128)}) %reduce-scatter.28.cloned.1.call-update) | async-done | bytes 442384 | tf_op jit(solution)/shard_map/reduce_scatter | solution.py:416
  2877.9 115.7 %reduce-scatter.32.cloned.1.call-done = f32[1,48,3072]{2,1,0:T(8,128)} async-done(((f32[1,768,3072]{2,1,0:T(8,128)}), f32[1,48,3072]{2,1,0:T(8,128)}) %reduce-scatter.32.cloned.1.call-update) | async-done | bytes 589840 | tf_op jit(solution)/shard_map/reduce_scatter | solution.py:420
  2993.5 116.2 %reduce-scatter.34.cloned.1.call-done = f32[1,192,768]{2,1,0:T(8,128)} async-done(((f32[1,3072,768]{2,1,0:T(8,128)}), f32[1,192,768]{2,1,0:T(8,128)}) %reduce-scatter.34.cloned.1.call-update) | async-done | bytes 589840 | tf_op jit(solution)/shard_map/reduce_scatter | solution.py:422
  (529 shorter events, 611.0 us)
Async XLA Ops:
  7.2 2233.9 %reduce-scatter.36.cloned.1.call-start = ((), (), s32[]{:S(2)}) async-start(), calls=%async_computation.17 | async-start | bytes 2506752 | tf_op jit(solution)/shard_map/reduce_scatter | solution.py:428
  10.8 16.0 collective-permute-start.2
  16.3 15.3 collective-permute-start.1
  33.3 97.9 %collective-permute-start.3 = (bf16[3,288,1536]{2,1,0:T(8,128)(2,1)}, bf16[3,288,1536]{2,1,0:T(8,128)(2,1)}, u32[]{:S(2)}, u32[]{:S(2)}) collective-permute-start(bf16[3,288,1536]{2,1,0:T(8,128)(2,1)} %pad_maximum_fusion.6), channel_id=1, source_target_pairs={{0,16},{1,17},{2,18},{3,19},{4,20},{5,21},{6,22},{7,23},{8,24},{9,... | collective-permute-start | bytes 7962632 | tf_op jit(solution)/shard_map/ppermute | solution.py:33
  111.0 17.7 collective-permute-start
  214.8 195.9 %collective-permute-start.4 = (bf16[8,64,768]{2,1,0:T(8,128)(2,1)S(1)}, bf16[8,64,768]{2,1,0:T(8,128)(2,1)S(1)}, u32[]{:S(2)}, u32[]{:S(2)}) collective-permute-start(bf16[8,64,768]{2,1,0:T(8,128)(2,1)S(1)} %convert_element_type.570), channel_id=1, source_target_pairs={{0,16},{1,17},{2,18},{3,19},{4,20},{5,21},{6,22},{7,23},{8,24},{9,... | collective-permute-start | bytes 2359304 | tf_op jit(solution)/shard_map/ppermute | solution.py:33
  444.8 743.9 %collective-permute-start.5 = (bf16[8,64,768]{2,1,0:T(8,128)(2,1)S(1)}, bf16[8,64,768]{2,1,0:T(8,128)(2,1)S(1)}, u32[]{:S(2)}, u32[]{:S(2)}) collective-permute-start(bf16[8,64,768]{2,1,0:T(8,128)(2,1)S(1)} %convert_element_type.573), channel_id=1, source_target_pairs={{16,0},{17,1},{18,2},{19,3},{20,4},{21,5},{22,6},{23,7},{24,8},{25... | collective-permute-start | bytes 2359304 | tf_op jit(solution)/shard_map/ppermute | solution.py:33
  1358.1 617.1 %collective-permute-start.6 = (bf16[8,64,768]{2,1,0:T(8,128)(2,1)S(1)}, bf16[8,64,768]{2,1,0:T(8,128)(2,1)S(1)}, u32[]{:S(2)}, u32[]{:S(2)}) collective-permute-start(bf16[8,64,768]{2,1,0:T(8,128)(2,1)S(1)} %convert_element_type.575), channel_id=1, source_target_pairs={{16,0},{17,1},{18,2},{19,3},{20,4},{21,5},{22,6},{23,7},{24,8},{25... | collective-permute-start | bytes 2359304 | tf_op jit(solution)/shard_map/ppermute | solution.py:33
  2125.1 127.4 %reduce-scatter.38.cloned.1.call-start = ((), (), s32[]{:S(2)}) async-start(), calls=%async_computation.18 | async-start | bytes 2506752 | tf_op jit(solution)/shard_map/reduce_scatter | solution.py:430
  2138.0 60.6 %collective-permute-start.7 = (bf16[3,288,1536]{2,1,0:T(8,128)(2,1)}, bf16[3,288,1536]{2,1,0:T(8,128)(2,1)}, u32[]{:S(2)}, u32[]{:S(2)}) collective-permute-start(bf16[3,288,1536]{2,1,0:T(8,128)(2,1)} %slice.246), channel_id=1, source_target_pairs={{16,0},{17,1},{18,2},{19,3},{20,4},{21,5},{22,6},{23,7},{24,8},{25... | collective-permute-start | bytes 7962632 | tf_op jit(solution)/shard_map/ppermute | solution.py:33
  2143.4 187.6 %reduce-scatter.52.cloned.1.call-start = ((), (), s32[]{:S(2)}) async-start(), calls=%async_computation.25 | async-start | bytes 5013504
  2201.8 15.3 collective-permute-start.8
  2201.8 15.3 collective-permute-start.9
  2228.7 436.1 %reduce-scatter.40.cloned.1.call-start = ((), (), s32[]{:S(2)}) async-start(), calls=%async_computation.19 | async-start | bytes 417792
  2230.4 435.7 %reduce-scatter.42.cloned.1.call-start = ((), (), s32[]{:S(2)}) async-start(), calls=%async_computation.20 | async-start | bytes 417792
  2232.0 435.3 %reduce-scatter.44.cloned.1.call-start = ((), (), s32[]{:S(2)}) async-start(), calls=%async_computation.21 | async-start | bytes 417792
  2233.7 435.0 %reduce-scatter.46.cloned.1.call-start = ((), (), s32[]{:S(2)}) async-start(), calls=%async_computation.22 | async-start | bytes 417792
  2235.5 434.6 %reduce-scatter.50.cloned.1.call-start = ((), (), s32[]{:S(2)}) async-start(), calls=%async_computation.24 | async-start | bytes 417792
  2237.2 447.5 %reduce-scatter.48.cloned.1.call-start = ((), (), s32[]{:S(2)}) async-start(), calls=%async_computation.23 | async-start | bytes 1671168
  2241.0 475.5 %all-reduce.7.cloned.1.call-start = ((), (), s32[]{:S(2)}) async-start(), calls=%async_computation.26 | async-start | bytes 1081344 | tf_op jit(solution)/shard_map/psum | solution.py:436
  2332.9 450.9 %reduce-scatter.30.cloned.1.call-start = ((), (), s32[]{:S(2)}) async-start(), calls=%async_computation.14 | async-start | bytes 2506752 | tf_op jit(solution)/shard_map/reduce_scatter | solution.py:417
  2337.9 539.9 %reduce-scatter.28.cloned.1.call-start = ((), (), s32[]{:S(2)}) async-start(), calls=%async_computation.13 | async-start | bytes 7520256 | tf_op jit(solution)/shard_map/reduce_scatter | solution.py:416
  2349.3 644.2 %reduce-scatter.32.cloned.1.call-start = ((), (), s32[]{:S(2)}) async-start(), calls=%async_computation.15 | async-start | bytes 10027008 | tf_op jit(solution)/shard_map/reduce_scatter | solution.py:420
  2364.4 745.4 %reduce-scatter.34.cloned.1.call-start = ((), (), s32[]{:S(2)}) async-start(), calls=%async_computation.16 | async-start | bytes 10027008 | tf_op jit(solution)/shard_map/reduce_scatter | solution.py:422
  (124 other events, 2539.7 us)
Sparse Core Ops, SparseCore 0:
  2125.2 59.0 reduce-scatter.35
  2188.5 63.9 reduce-scatter.37
  2256.4 74.5 reduce-scatter.51
  2334.7 54.6 reduce-scatter.39
  2392.8 54.5 reduce-scatter.41
  2451.2 54.5 reduce-scatter.43
  2509.3 54.6 reduce-scatter.45
  2567.8 54.5 reduce-scatter.49
  2626.1 58.5 reduce-scatter.47
  2688.2 28.3 all-reduce.6
  2720.9 62.8 reduce-scatter.29
  2788.8 88.9 reduce-scatter.27
  2882.5 110.9 reduce-scatter.31
  2998.6 111.0 reduce-scatter.33
where the time goes:
time: 3150 us; the launch traced here: 3120 us
  waiting for transfers between devices  1980 us (63%)
  blocking collectives  269 us (9%)
  matrix products  213 us (7%)
  other arithmetic  205 us (7%)
  local copies, waits for them, and re-layouts  200 us (6%)
  starting transfers between devices  200 us (6%)
    ppermute x6, waiting for transfers between devices, passed_along(): return lax.ppermute(block, axis, route)  1440 us
    psum x1, blocking collectives, per_device(): lax.psum(cross_part[0].astype(jnp.bfloat16), 'section').astype(jnp.float32)  238 us
    ppermute x6, starting transfers between devices, passed_along(): return lax.ppermute(block, axis, route)  190 us
    reduce_scatter x1, waiting for transfers between devices, per_device(): lax.psum_scatter(layer_total[8][None], 'dp', scatter_dimension=1, tiled=T...  116 us
    reduce_scatter x1, waiting for transfers between devices, per_device(): lax.psum_scatter(layer_total[6][None], 'dp', scatter_dimension=1, tiled=T...  116 us
    reduce_scatter x1, waiting for transfers between devices, per_device(): lax.psum_scatter(layer_total[2][None], 'dp', scatter_dimension=1, tiled=T...  94 us
    unnamed x21, waiting for transfers between devices  90.5 us
    dot_general x15, matrix products, matmul(): jnp.einsum('...d,de->...e', left_in, right_in, preferred_element_type=jnp...  87.3 us
  transfers between devices with their start and end apart: 24, of which 16 were waited for; matrix products, arithmetic and copies ran while one was open for 6% of the time, Pallas kernels for 0%

commit v1 on v0

v1 whole, which is shorter than its diff:
```python
from functools import partial

import jax
import jax.numpy as jnp
from jax import lax
from jax.sharding import PartitionSpec as P

H = 12
HD = 64
MICRO = 2

EPS = 1e-05
MASKED = -1e30
SCALE = HD ** (-0.5)
F32 = jnp.float32
BF16 = jnp.bfloat16


def bf(x):
    return x.astype(BF16)


def run_on(flag, fn, *args):
    shapes = jax.eval_shape(fn, *args)

    def idle(*unused):
        return jax.tree.map(lambda s: jnp.zeros(s.shape, s.dtype), shapes)

    return lax.cond(flag, fn, idle, *args)


def norm_fwd(x, gain, bias):
    mean = jnp.mean(x, -1, keepdims=True)
    centred = x - mean
    var = jnp.mean(centred * centred, -1, keepdims=True)
    rstd = lax.rsqrt(var + EPS)
    xhat = centred * rstd
    return xhat * gain + bias, (xhat, rstd)


def norm_bwd(dy, saved, gain):
    xhat, rstd = saved
    lead = tuple(range(dy.ndim - 1))
    d_gain = jnp.sum(dy * xhat, lead)
    d_bias = jnp.sum(dy, lead)
    dxh = dy * gain
    dx = rstd * (
        dxh
        - jnp.mean(dxh, -1, keepdims=True)
        - xhat * jnp.mean(dxh * xhat, -1, keepdims=True)
    )
    return dx, d_gain, d_bias


def mm(a, w):
    return jnp.einsum("...d,de->...e", a, w, preferred_element_type=F32)


def mm_t(g, w):
    return jnp.einsum("...e,de->...d", g, w, preferred_element_type=F32)


def outer(a, b):
    return jnp.einsum("rtd,rte->de", a, b, preferred_element_type=F32)


def softmax_rows(s, axes):
    top = jnp.max(s, axes, keepdims=True)
    e = jnp.exp(s - top)
    return e / jnp.sum(e, axes, keepdims=True)


def self_fwd(h, seg, gain, bias, w_qkv, w_out):
    r, t = seg.shape
    y, nsave = norm_fwd(h, gain, bias)
    n = bf(y)
    trip = bf(mm(n, w_qkv)).reshape(r, t, 3, H, HD)
    q, k, v = trip[:, :, 0], trip[:, :, 1], trip[:, :, 2]
    pos = jnp.arange(t)
    allowed = (seg[:, :, None] == seg[:, None, :]) & (pos[:, None] >= pos[None, :])[None]
    s = jnp.einsum("rqhd,rkhd->rhqk", q, k, preferred_element_type=F32) * SCALE
    s = jnp.where(allowed[:, None], s, MASKED)
    p = softmax_rows(s, -1)
    o = bf(jnp.einsum("rhqk,rkhd->rqhd", bf(p), v, preferred_element_type=F32))
    o = o.reshape(r, t, H * HD)
    h2 = h + mm(o, w_out)
    saved = dict(nsave=nsave, n=n, q=q, k=k, v=v, p=p, o=o)
    return h2, saved


def self_bwd(dh2, sv, gain, w_qkv, w_out):
    r, t = dh2.shape[:2]
    g2 = bf(dh2)
    do = bf(mm_t(g2, w_out)).reshape(r, t, H, HD)
    p, q, k, v = sv["p"], sv["q"], sv["k"], sv["v"]
    dp = jnp.einsum("rqhd,rkhd->rhqk", do, v, preferred_element_type=F32)
    ds = bf(p * (dp - jnp.sum(p * dp, -1, keepdims=True)))
    dq = jnp.einsum("rhqk,rkhd->rqhd", ds, k, preferred_element_type=F32) * SCALE
    dk = jnp.einsum("rhqk,rqhd->rkhd", ds, q, preferred_element_type=F32) * SCALE
    dv = jnp.einsum("rhqk,rqhd->rkhd", bf(p), do, preferred_element_type=F32)
    dt = bf(jnp.stack([dq, dk, dv], 2)).reshape(r, t, 3 * H * HD)
    dn = mm_t(dt, w_qkv)
    dx, d_gain, d_bias = norm_bwd(dn, sv["nsave"], gain)
    pairs = dict(o=sv["o"], g2=g2, n=sv["n"], dt=dt)
    return dh2 + dx, (d_gain, d_bias), pairs


def cross_core_fwd(qc, pool_k, pool_v, pick):
    s = jnp.einsum("rqhd,pkhd->rhqpk", qc, pool_k, preferred_element_type=F32) * SCALE
    allowed = pick[:, :, None] == jnp.arange(pool_k.shape[0])[None, None, :]
    s = jnp.where(allowed[:, None, :, :, None], s, MASKED)
    p = softmax_rows(s, (-2, -1))
    oc = jnp.einsum("rhqpk,pkhd->rqhd", bf(p), pool_v, preferred_element_type=F32)
    return bf(oc), p


def cross_core_bwd(doc, qc, pool_k, pool_v, p):
    dp = jnp.einsum("rqhd,pkhd->rhqpk", doc, pool_v, preferred_element_type=F32)
    ds = bf(p * (dp - jnp.sum(p * dp, (-2, -1), keepdims=True)))
    dqc = jnp.einsum("rhqpk,pkhd->rqhd", ds, pool_k, preferred_element_type=F32) * SCALE
    dk = jnp.einsum("rhqpk,rqhd->pkhd", ds, qc, preferred_element_type=F32) * SCALE
    dv = jnp.einsum("rhqpk,rqhd->pkhd", bf(p), doc, preferred_element_type=F32)
    return dqc, dk, dv


def cross_fwd(h2, pick, pool_k, pool_v, gain, bias, wq, wo):
    r, t = pick.shape
    y, csave = norm_fwd(h2, gain, bias)
    c = bf(y)
    qc = bf(mm(c, wq)).reshape(r, t, H, HD)
    oc, p = cross_core_fwd(qc, pool_k, pool_v, pick)
    oc = oc.reshape(r, t, H * HD)
    h3 = h2 + mm(oc, wo)
    return h3, dict(csave=csave, c=c, qc=qc, p=p, oc=oc)


def cross_bwd(dh3, sv, pool_k, pool_v, gain, wq, wo):
    r, t = dh3.shape[:2]
    g3 = bf(dh3)
    doc = bf(mm_t(g3, wo)).reshape(r, t, H, HD)
    dqc, dk, dv = cross_core_bwd(doc, sv["qc"], pool_k, pool_v, sv["p"])
    dqc = bf(dqc.reshape(r, t, H * HD))
    dc = mm_t(dqc, wq)
    dx, d_gain, d_bias = norm_bwd(dc, sv["csave"], gain)
    pairs = dict(oc=sv["oc"], g3=g3, c=sv["c"], dqc=dqc)
    return dh3 + dx, (d_gain, d_bias), pairs, dk, dv


def gelu(z):
    return jax.nn.gelu(z, approximate=False)


def ffn_fwd(h3, gain, bias, w_up, b_up, w_down, b_down):
    y, usave = norm_fwd(h3, gain, bias)
    u = bf(y)
    z = mm(u, w_up) + b_up
    f = bf(gelu(z))
    out = h3 + (mm(f, w_down) + b_down)
    return out, dict(usave=usave, u=u, z=z, f=f)


def ffn_bwd(gout, sv, gain, w_up, w_down):
    gb = bf(gout)
    df = mm_t(gb, w_down)
    _, pull = jax.vjp(gelu, sv["z"])
    dz = bf(pull(df)[0])
    du = mm_t(dz, w_up)
    dx, d_gain, d_bias = norm_bwd(du, sv["usave"], gain)
    pairs = dict(f=sv["f"], gb=gb, u=sv["u"], dz=dz)
    return gout + dx, (d_gain, d_bias), pairs


def per_device(
    inputs,
    cotangent,
    images,
    seg_ids,
    row_block,
    seg_image,
    ln1_gain,
    ln1_bias,
    w_qkv,
    w_out,
    ln2_gain,
    ln2_bias,
    w_up,
    b_up,
    w_down,
    b_down,
    lnc_gain,
    lnc_bias,
    wq_cross,
    wkv_cross,
    wo_cross,
):
    up = lax.axis_index("section") == 1
    low = jnp.logical_not(up)
    dp_index = lax.axis_index("dp")
    n_dp = lax.axis_size("dp")
    rows = inputs.shape[0]
    rc = rows // MICRO
    g1, b1, wqkv, wout = ln1_gain[0], ln1_bias[0], w_qkv[0], w_out[0]
    g2, b2, wup, bup, wdown, bdown = ln2_gain[0], ln2_bias[0], w_up[0], b_up[0], w_down[0], b_down[0]
    n_img = n_dp * images.shape[0]

    first_half = lax.ppermute(images[0], "section", [(0, 1)])
    full_image = jnp.concatenate([first_half, images[0]], 0)

    def make_kv(img):
        return bf(mm(img, wkv_cross))

    kv_own = run_on(up, make_kv, full_image)
    ring_up = [(i, (i + 1) % n_dp) for i in range(n_dp)]
    ring_down = [((i + 1) % n_dp, i) for i in range(n_dp)]
    kv_prev = lax.ppermute(kv_own, "dp", ring_up)
    kv_next = lax.ppermute(kv_own, "dp", ring_down)
    pool = jnp.stack([kv_prev, kv_own, kv_next], 0)
    img_tok = pool.shape[1]
    pool = pool.reshape(3, img_tok, 2, H, HD)
    pool_k, pool_v = pool[:, :, 0], pool[:, :, 1]

    first_img = (row_block[:, None] + seg_image) % n_img
    slot = (first_img - dp_index + 1 + n_img) % n_img
    pick_all = jnp.where(seg_ids == 0, slot[:, :1], slot[:, 1:2])

    def chunk(a, m):
        return a[m * rc : (m + 1) * rc]

    x = inputs.astype(F32)

    def lower_fwd(hid, seg):
        h2, s_self = self_fwd(hid, seg, g1, b1, wqkv, wout)
        out, s_ffn = ffn_fwd(h2, g2, b2, wup, bup, wdown, bdown)
        return out, (s_self, s_ffn)

    def upper_fwd(sent, seg, pick, pk, pv):
        hid = sent.astype(F32)
        h2, s_self = self_fwd(hid, seg, g1, b1, wqkv, wout)
        h3, s_cross = cross_fwd(h2, pick, pk, pv, lnc_gain, lnc_bias, wq_cross, wo_cross)
        out, s_ffn = ffn_fwd(h3, g2, b2, wup, bup, wdown, bdown)
        return out, (s_self, s_cross, s_ffn)

    low_out, low_saved, sent = [], [], []
    for m in range(MICRO):
        out, saved = run_on(low, lower_fwd, chunk(x, m), chunk(seg_ids, m))
        low_out.append(out)
        low_saved.append(saved)
        sent.append(lax.ppermute(bf(out), "section", [(0, 1)]))
    up_out, up_saved = [], []
    for m in range(MICRO):
        out, saved = run_on(
            up, upper_fwd, sent[m], chunk(seg_ids, m), chunk(pick_all, m), pool_k, pool_v
        )
        up_out.append(out)
        up_saved.append(saved)

    cot = cotangent[0].astype(F32)

    def upper_bwd(gout, saved, pk, pv):
        s_self, s_cross, s_ffn = saved
        dh3, ln2g, pf = ffn_bwd(gout, s_ffn, g2, wup, wdown)
        dh2, lncg, pc, dk, dv = cross_bwd(dh3, s_cross, pk, pv, lnc_gain, wq_cross, wo_cross)
        dh, ln1g, ps = self_bwd(dh2, s_self, g1, wqkv, wout)
        return dh, (ln1g, ln2g, lncg), (ps, pf, pc), dk, dv

    up_grad, up_small, up_pairs = [], [], []
    returned = []
    pool_dk = pool_dv = None
    for m in range(MICRO):
        dh, small, pairs, dk, dv = run_on(up, upper_bwd, chunk(cot, m), up_saved[m], pool_k, pool_v)
        up_grad.append(dh)
        up_small.append(small)
        up_pairs.append(pairs)
        pool_dk = dk if pool_dk is None else pool_dk + dk
        pool_dv = dv if pool_dv is None else pool_dv + dv
        returned.append(lax.ppermute(bf(dh), "section", [(1, 0)]))

    def cat(name_path, pairs_list):
        return jnp.concatenate([name_path(p) for p in pairs_list], 0)

    def layer_weight_grads(pairs_list):
        ps = lambda i, k: cat(lambda p: p[i][k], pairs_list)
        d_wqkv = outer(ps(0, "n"), ps(0, "dt"))
        d_wout = outer(ps(0, "o"), ps(0, "g2"))
        d_wup = outer(ps(1, "u"), ps(1, "dz"))
        d_wdown = outer(ps(1, "f"), ps(1, "gb"))
        d_bup = jnp.sum(ps(1, "dz").astype(F32), (0, 1))
        d_bdown = jnp.sum(ps(1, "gb").astype(F32), (0, 1))
        return d_wqkv, d_wout, d_wup, d_bup, d_wdown, d_bdown

    def upper_wgrads(pairs_list):
        layer = layer_weight_grads(pairs_list)
        ps = lambda k: cat(lambda p: p[2][k], pairs_list)
        d_wq = outer(ps("c"), ps("dqc"))
        d_wo = outer(ps("oc"), ps("g3"))
        return layer, (d_wq, d_wo)

    up_w, cross_w = run_on(up, upper_wgrads, up_pairs)

    parts = bf(
        jnp.concatenate(
            [pool_dk.reshape(3, img_tok, H * HD), pool_dv.reshape(3, img_tok, H * HD)], -1
        )
    )
    from_next = lax.ppermute(parts[0], "dp", ring_down)
    from_prev = lax.ppermute(parts[2], "dp", ring_up)
    kv_grad = bf(parts[1].astype(F32) + from_next.astype(F32) + from_prev.astype(F32))

    def image_side(kvg, img):
        ig = jnp.einsum("te,de->td", kvg, wkv_cross, preferred_element_type=F32)
        dw = jnp.einsum("td,te->de", img, kvg, preferred_element_type=F32)
        return ig, dw

    image_grad_full, d_wkv = run_on(up, image_side, kv_grad, full_image)
    half = images.shape[1]
    ig_first = lax.ppermute(image_grad_full[:half], "section", [(1, 0)])
    image_grad = jnp.where(up, image_grad_full[half:], ig_first)[None]

    def lower_bwd(gout, saved):
        s_self, s_ffn = saved
        dh3, ln2g, pf = ffn_bwd(gout, s_ffn, g2, wup, wdown)
        dh, ln1g, ps = self_bwd(dh3, s_self, g1, wqkv, wout)
        return dh, (ln1g, ln2g), (ps, pf)

    low_grad, low_small, low_pairs = [], [], []
    for m in range(MICRO):
        gout = chunk(cot, m) + returned[m].astype(F32)
        dh, small, pairs = run_on(low, lower_bwd, gout, low_saved[m])
        low_grad.append(dh)
        low_small.append(small)
        low_pairs.append(pairs)

    low_w = run_on(low, layer_weight_grads, low_pairs)

    activations = jnp.where(
        up, jnp.concatenate(up_out, 0), jnp.concatenate(low_out, 0)
    )[None]
    back_grads = jnp.where(
        up, jnp.concatenate(up_grad, 0), jnp.concatenate(low_grad, 0)
    )[None]

    def tree_sum(xs):
        total = xs[0]
        for v in xs[1:]:
            total = jax.tree.map(jnp.add, total, v)
        return total

    up_sm = tree_sum(up_small)
    low_sm = tree_sum(low_small)
    ln1g = jax.tree.map(lambda a, b: jnp.where(up, a, b), up_sm[0], low_sm[0])
    ln2g = jax.tree.map(lambda a, b: jnp.where(up, a, b), up_sm[1], low_sm[1])
    lncg = up_sm[2]
    lw = jax.tree.map(lambda a, b: jnp.where(up, a, b), up_w, low_w)
    d_wqkv, d_wout, d_wup, d_bup, d_wdown, d_bdown = lw

    def rs(a, dim=0):
        return lax.psum_scatter(a, "dp", scatter_dimension=dim, tiled=True)

    def rs_cross(a):
        return lax.psum(jnp.where(up, rs(a), 0.0), "section")

    return (
        activations,
        back_grads,
        image_grad,
        rs(ln1g[0])[None],
        rs(ln1g[1])[None],
        rs(d_wqkv)[None],
        rs(d_wout)[None],
        rs(ln2g[0])[None],
        rs(ln2g[1])[None],
        rs(d_wup)[None],
        rs(d_bup)[None],
        rs(d_wdown)[None],
        rs(d_bdown)[None],
        rs_cross(lncg[0]),
        rs_cross(lncg[1]),
        rs_cross(cross_w[0]),
        rs_cross(d_wkv),
        rs_cross(cross_w[1]),
    )


def solution(mesh):
    placed = (
        P("dp", None, None),
        P("section", "dp", None, None),
        P("dp", "section", None),
        P("dp", None),
        P("dp"),
        P("dp", None),
        P("section", None),
        P("section", None),
        P("section", None, None),
        P("section", None, None),
        P("section", None),
        P("section", None),
        P("section", None, None),
        P("section", None),
        P("section", None, None),
        P("section", None),
        P(),
        P(),
        P(),
        P(),
        P(),
    )
    return jax.shard_map(
        per_device,
        mesh=mesh,
        in_specs=placed,
        out_specs=(
            P("section", "dp", None, None),
            P("section", "dp", None, None),
            P("dp", "section", None),
            P("section", "dp"),
            P("section", "dp"),
            P("section", "dp", None),
            P("section", "dp", None),
            P("section", "dp"),
            P("section", "dp"),
            P("section", "dp", None),
            P("section", "dp"),
            P("section", "dp", None),
            P("section", "dp"),
            P("dp"),
            P("dp"),
            P("dp", None),
            P("dp", None),
            P("dp", None),
        ),
        check_vma=False,
    )
```

time: 3150 us -> 1860 us (0.59)
  waiting for transfers between devices: 1980 us -> 1080 us
  starting transfers between devices: 200 us -> 21 us
  blocking collectives: 269 us -> 96.4 us
  other arithmetic: 205 us -> 120 us
  local copies, waits for them, and re-layouts: 200 us -> 278 us
    ppermute x10, waiting for transfers between devices: 1470 us -> 783 us  [the longest x2 756 us: per_device(): returned.append(lax.ppermute(bf(dh), 'section', [(1, 0)]))]
    psum x1, blocking collectives: 238 us -> 20.8 us  [rs_cross(): return lax.psum(jnp.where(up, rs(a), 0.0), 'section')]
    ppermute x10, starting transfers between devices: 200 us -> 20.7 us  [the longest x1 4.9 us: per_device(): first_half = lax.ppermute(images[0], 'section', [(0, 1)])]
    another operation x24 -> x98, local copies, waits for them, and re-layouts: 50.6 us -> 164 us
    reduce_scatter x6 -> x7, waiting for transfers between devices: 398 us -> 299 us  [rs(): return lax.psum_scatter(a, 'dp', scatter_dimension=dim, tiled=True)]
    unnamed x21 -> x8, waiting for transfers between devices: 90.5 us -> 0.13 us
    broadcast_in_dim x5 -> x1, other arithmetic: 48.4 us -> 2.22 us  [per_device(): image_grad = jnp.where(up, image_grad_full[half:], ig_first)[None]]
    unnamed x1, blocking collectives: 30.5 us -> 75.6 us
  transfers between devices with their start and end apart: 24 -> 18, of which waited for: 16 -> 7; matrix products, arithmetic and copies ran while one was open for 6% -> 27% of each run, Pallas kernels for 0% -> 0%
where the time goes in v1:
time: 1860 us; the launch traced here: 1850 us
  waiting for transfers between devices  1080 us (58%)
  local copies, waits for them, and re-layouts  278 us (15%)
  matrix products  202 us (11%)
  other arithmetic  120 us (6%)
  blocking collectives  96.4 us (5%)
  loops' own time  37.7 us (2%)
  starting transfers between devices  21 us (1%)
    ppermute x2, waiting for transfers between devices, per_device(): returned.append(lax.ppermute(bf(dh), 'section', [(1, 0)]))  756 us
    reduce_scatter x7, waiting for transfers between devices, rs(): return lax.psum_scatter(a, 'dp', scatter_dimension=dim, tiled=True)  299 us
    another operation x95, local copies, waits for them, and re-layouts  152 us
    unnamed x1, blocking collectives  75.6 us
    dot_general x8, matrix products, mm_t(): return jnp.einsum('...e,de->...d', g, w, preferred_element_type=F32)  66.5 us
    dot_general x8, matrix products, mm(): return jnp.einsum('...d,de->...e', a, w, preferred_element_type=F32)  65 us
    another operation x12, loops' own time, run_on(): return lax.cond(flag, fn, idle, *args)  37.7 us
  transfers between devices with their start and end apart: 18, of which 7 were waited for; matrix products, arithmetic and copies ran while one was open for 27% of the time, Pallas kernels for 0%

profile of v1, /device:TPU:0, one launch (start us, length us, event | category | flops | bytes accessed | tf_op | source)
XLA Modules:
  0.0 1854.3 jit_solution(4157537393169060356)
XLA Ops:
  31.0 71.7 %conditional.12 = (f32[8,64,768]{2,1,0:T(8,128)}, bf16[8,64,12,64]{3,1,2,0:T(8,128)(2,1)}, bf16[8,64,768]{2,1,0:T(8,128)(2,1)}, f32[8,64,768]{2,1,0:T(8,128)}, f...) conditional(s32[]{:T(128)} %convert_element_type.327, ...), branch_computations={%region_0.0_spmd, %region_1.8_spmd} | conditional | flops 7464489984 | bytes 121335072 | solution.py:29
  77.0 19.8 %fusion.69 = (bf16[8,64,3072]{2,1,0:T(8,128)(2,1)}, f32[8,64,3072]{2,1,0:T(8,128)}) fusion(f32[3072]{0:T(1024)S(1)} %bitcast.743, bf16[8,64,768]{2,1,0:T(8,128)(2,1)} %get-tuple-element.1802, bf16[768,3072]{1,0:T(8,128)(2,1)S(1)} %bitcast.708), kind=kOutput, calls=%fused_computation.87 | convolution fusion | flops 2519728128 | bytes 14954496 | tf_op jit(solution)/shard_map/cond/branch_1_fun/...d,de->...e/dot_general | solution.py:56
  107.3 71.9 %conditional.15 = (f32[8,64,768]{2,1,0:T(8,128)}, bf16[8,64,12,64]{3,1,2,0:T(8,128)(2,1)}, bf16[8,64,768]{2,1,0:T(8,128)(2,1)}, f32[8,64,768]{2,1,0:T(8,128)}, f...) conditional(s32[]{:T(128)} %convert_element_type.327, ...), branch_computations={%region_22.23_spmd, %region_23.30_spmd} | conditional | flops 7464489984 | bytes 121335072 | solution.py:29
  153.3 19.7 %fusion.155 = (bf16[8,64,3072]{2,1,0:T(8,128)(2,1)}, f32[8,64,3072]{2,1,0:T(8,128)}) fusion(f32[3072]{0:T(1024)S(1)} %bitcast.744, bf16[8,64,768]{2,1,0:T(8,128)(2,1)} %get-tuple-element.1730, bf16[768,3072]{1,0:T(8,128)(2,1)S(1)} %bitcast.710), kind=kOutput, calls=%fused_computation.230 | convolution fusion | flops 2519728128 | bytes 14954496 | tf_op jit(solution)/shard_map/cond/branch_1_fun/...d,de->...e/dot_general | solution.py:56
  199.2 49.5 %conditional.16 = (bf16[8,64,12,64]{3,1,2,0:T(8,128)(2,1)}, bf16[8,64,768]{2,1,0:T(8,128)(2,1)}, f32[8,64,768]{2,1,0:T(8,128)}, f32[8,64,1]{1,0,2:T(8,128)S(1)},...) conditional(s32[]{:T(128)} %convert_element_type.326, ...), branch_computations={%region_30.31_spmd, %region_31.42_spmd} | conditional | flops 11524041728 | bytes 352511328 | solution.py:29
  223.6 15.3 broadcast.1370
  249.4 26.6 %conditional.18 = (f32[8,64,768]{2,1,0:T(8,128)}, f32[768]{0:T(1024)S(1)}, f32[768]{0:T(1024)S(1)}, f32[768]{0:T(1024)S(1)}, f32[768]{0:T(1024)S(1)}, /*index=5*...) conditional(s32[]{:T(128)} %convert_element_type.326, ...), branch_computations={%region_58.59_spmd, %region_59.74_spmd} | conditional | flops 14295889920 | bytes 435386976 | solution.py:29
  276.6 49.6 %conditional.14 = (bf16[8,64,12,64]{3,1,2,0:T(8,128)(2,1)}, bf16[8,64,768]{2,1,0:T(8,128)(2,1)}, f32[8,64,768]{2,1,0:T(8,128)}, f32[8,64,1]{1,0,2:T(8,128)S(1)},...) conditional(s32[]{:T(128)} %convert_element_type.326, ...), branch_computations={%region_10.11_spmd, %region_11.0_spmd} | conditional | flops 11524041728 | bytes 352523648 | solution.py:29
  300.8 15.3 broadcast.1288
  326.8 30.6 %conditional.17 = (f32[8,64,768]{2,1,0:T(8,128)}, f32[768]{0:T(1024)}, f32[768]{0:T(1024)}, f32[768]{0:T(1024)}, f32[768]{0:T(1024)}, /*index=5*/f32[768]{0:T(10...) conditional(s32[]{:T(128)} %convert_element_type.326, ...), branch_computations={%region_42.43_spmd, %region_43.58_spmd} | conditional | flops 14295889920 | bytes 436517312 | solution.py:29
  357.4 23.2 %conditional.22 = (f32[768,2304]{1,0:T(8,128)}, f32[768,768]{1,0:T(8,128)}, f32[768,3072]{1,0:T(8,128)}, f32[3072]{0:T(1024)S(1)}, f32[3072,768]{1,0:T(8,128)}, ...) conditional(s32[]{:T(128)} %convert_element_type.326, () %tuple.134, ...), branch_computations={%region_100.101_spmd, %region_101.104_spmd} | conditional | flops 16931090432 | bytes 88095808 | solution.py:29
  406.8 16.7 collective-permute-done.8
  445.3 756.4 %collective-permute-done.6 = bf16[8,64,768]{2,1,0:T(8,128)(2,1)S(1)} collective-permute-done((bf16[8,64,768]{2,1,0:T(8,128)(2,1)S(1)}, bf16[8,64,768]{2,1,0:T(8,128)(2,1)S(1)}, u32[]{:S(2)}, u32[]{:S(2)}) %collective-permute-start.6) | collective-permute-done | bytes 786464 | tf_op jit(solution)/shard_map/ppermute | solution.py:276
  1203.0 75.9 %conditional.20 = (f32[768]{0:T(1024)S(1)}, f32[768]{0:T(1024)S(1)}, f32[768]{0:T(1024)S(1)}, f32[768]{0:T(1024)S(1)}, bf16[8,64,2304]{2,1,0:T(8,128)(2,1)}, /*i...) conditional(s32[]{:T(128)} %convert_element_type.327, ...), branch_computations={%region_85.86_spmd, %region_86.96_spmd} | conditional | flops 7580802048 | bytes 115728592 | solution.py:29
  1208.6 19.2 %fusion.373 = bf16[8,64,3072]{2,1,0:T(8,128)(2,1)} fusion(f32[8,64,3072]{2,1,0:T(8,128)} %get-tuple-element.585, bf16[8,64,768]{2,1,0:T(8,128)(2,1)} %get-tuple-element.1911, bf16[3072,768]{1,0:T(8,128)(2,1)} %get-tuple-element.586), kind=kOutput, calls=%fused_computation.589 | convolution fusion | flops 2529165312 | bytes 14942208 | tf_op jit(solution)/shard_map/cond/branch_1_fun/...e,de->...d/dot_general | solution.py:60
  1280.4 74.1 %conditional.19 = (f32[768]{0:T(1024)S(1)}, f32[768]{0:T(1024)S(1)}, f32[768]{0:T(1024)S(1)}, f32[768]{0:T(1024)S(1)}, bf16[8,64,2304]{2,1,0:T(8,128)(2,1)}, /*i...) conditional(s32[]{:T(128)} %convert_element_type.327, ...), branch_computations={%region_74.75_spmd, %region_75.85_spmd} | conditional | flops 7580802048 | bytes 109437112 | solution.py:29
  1284.0 20.0 %fusion.348 = bf16[8,64,3072]{2,1,0:T(8,128)(2,1)} fusion(f32[8,64,3072]{2,1,0:T(8,128)} %get-tuple-element.564, bf16[8,64,768]{2,1,0:T(8,128)(2,1)} %get-tuple-element.1979, bf16[3072,768]{1,0:T(8,128)(2,1)} %get-tuple-element.565), kind=kOutput, calls=%fused_computation.538 | convolution fusion | flops 2529165312 | bytes 14942208 | tf_op jit(solution)/shard_map/cond/branch_1_fun/...e,de->...d/dot_general | solution.py:60
  1354.5 39.9 %conditional.23 = (f32[768,2304]{1,0:T(8,128)}, f32[768,768]{1,0:T(8,128)S(1)}, f32[768,3072]{1,0:T(8,128)}, f32[3072]{0:T(1024)S(1)}, f32[3072,768]{1,0:T(8,128)}, /*index=5*/f32[768]{0:T(1024)S(1)}) conditional(s32[]{:T(128)} %convert_element_type.327, () %tuple.136, (bf16[8,64,768]{2,1,0:T(8,128)(2,1)}, bf16[8,64,768]{2,1,0:T(8,128)(2,1)}, ...), branch_computations={%region_104.105_spmd, %region_105.108_spmd} | conditional | flops 14512025600 | bytes 77085744 | solution.py:29
  1405.2 10.2 broadcast_select_fusion.1
  1429.4 75.6 %all-reduce.8 = (f32[768]{0:T(1024)S(1)}, f32[768]{0:T(1024)S(1)}, f32[768]{0:T(1024)S(1)}, f32[768]{0:T(1024)S(1)}, f32[3072]{0:T(1024)S(1)}, /*index=5*/f32[768]{0:T(1024)S(1)}, f32[768]{0:T(1024)S(1)}, f32[768]{0:T(1024)S(1)}) all-reduce(f32[768]{0:T(1024)S(1)} %get-tuple-element.1703, ...), channel_id=2, replica_groups=mesh['section'=2,'dp'=16] {'dp'}, use_global_device_ids=true, to_apply=%region_98.99.clone | all-reduce | flops 8448 | bytes 67584
  1508.4 20.8 %all-reduce.9 = (f32[48]{0:T(128)}, f32[48]{0:T(128)}) all-reduce(f32[48]{0:T(128)S(1)} %broadcast_select_fusion.10, f32[48]{0:T(128)S(1)} %broadcast_select_fusion.9), channel_id=1, replica_groups=mesh['section'=2,'dp'=16] {'section'}, use_global_device_ids=true, to_apply=%region_117.118 | all-reduce | flops 96 | bytes 768 | tf_op jit(solution)/shard_map/psum | solution.py:360
  1543.3 67.2 %reduce-scatter.8.cloned.1.call-done = f32[48,2304]{1,0:T(8,128)} async-done(((f32[768,2304]{1,0:T(8,128)}), f32[48,2304]{1,0:T(8,128)}) %reduce-scatter.8.cloned.1.call-update) | async-done | bytes 442384 | tf_op jit(solution)/shard_map/reduce_scatter | solution.py:357
  1610.5 115.5 %reduce-scatter.12.cloned.1.call-done = f32[48,3072]{1,0:T(8,128)} async-done(((f32[768,3072]{1,0:T(8,128)}), f32[48,3072]{1,0:T(8,128)}) %reduce-scatter.12.cloned.1.call-update) | async-done | bytes 589840 | tf_op jit(solution)/shard_map/reduce_scatter | solution.py:357
  1726.1 116.4 %reduce-scatter.14.cloned.1.call-done = f32[192,768]{1,0:T(8,128)} async-done(((f32[3072,768]{1,0:T(8,128)}), f32[192,768]{1,0:T(8,128)}) %reduce-scatter.14.cloned.1.call-update) | async-done | bytes 589840 | tf_op jit(solution)/shard_map/reduce_scatter | solution.py:357
  (461 shorter events, 517.4 us)
Async XLA Ops:
  7.2 1389.0 %reduce-scatter.16.cloned.1.call-start = ((), (), s32[]{:S(2)}) async-start(), calls=%async_computation.11 | async-start | bytes 2506752 | tf_op jit(solution)/shard_map/reduce_scatter | solution.py:357
  7.2 14.6 collective-permute-start.1
  25.5 161.0 %collective-permute-start.3 = (bf16[576,1536]{1,0:T(8,128)(2,1)}, bf16[576,1536]{1,0:T(8,128)(2,1)}, u32[]{:S(2)}, u32[]{:S(2)}) collective-permute-start(bf16[576,1536]{1,0:T(8,128)(2,1)} %get-tuple-element.818), channel_id=1, source_target_pairs={{1,0},{2,1},{3,2},{4,3},{5,4},{6,5},{7,6},{8,7},{9,8},{10,9},{11,1... | collective-permute-start | bytes 5308424 | tf_op jit(solution)/shard_map/ppermute | solution.py:216
  28.6 160.6 %collective-permute-start.2 = (bf16[576,1536]{1,0:T(8,128)(2,1)}, bf16[576,1536]{1,0:T(8,128)(2,1)}, u32[]{:S(2)}, u32[]{:S(2)}) collective-permute-start(bf16[576,1536]{1,0:T(8,128)(2,1)} %get-tuple-element.818), channel_id=1, source_target_pairs={{0,1},{1,2},{2,3},{3,4},{4,5},{5,6},{6,7},{7,8},{8,9},{9,10},{10,1... | collective-permute-start | bytes 5308424 | tf_op jit(solution)/shard_map/ppermute | solution.py:215
  105.1 170.9 %collective-permute-start = (bf16[8,64,768]{2,1,0:T(8,128)(2,1)}, bf16[8,64,768]{2,1,0:T(8,128)(2,1)}, u32[]{:S(2)}, u32[]{:S(2)}) collective-permute-start(bf16[8,64,768]{2,1,0:T(8,128)(2,1)} %convert_element_type.329), channel_id=1, source_target_pairs={{0,16},{1,17},{2,18},{3,19},{4,20},{5,21},{6,22},{7,23},{8,24},{9,... | collective-permute-start | bytes 2359304 | tf_op jit(solution)/shard_map/ppermute | solution.py:248
  181.8 17.4 collective-permute-start.4
  380.6 1016.3 %reduce-scatter.20.cloned.1.call-start = ((), (), s32[]{:S(2)}) async-start(), calls=%async_computation.13 | async-start | bytes 2506752 | tf_op jit(solution)/shard_map/reduce_scatter | solution.py:357
  382.0 1015.6 %reduce-scatter.18.cloned.1.call-start = ((), (), s32[]{:S(2)}) async-start(), calls=%async_computation.12 | async-start | bytes 5013504 | tf_op jit(solution)/shard_map/reduce_scatter | solution.py:357
  398.4 25.1 %collective-permute-start.8 = (bf16[576,1536]{1,0:T(8,128)(2,1)}, bf16[576,1536]{1,0:T(8,128)(2,1)}, u32[]{:S(2)}, u32[]{:S(2)}) collective-permute-start(bf16[576,1536]{1,0:T(8,128)(2,1)} %copy.285), channel_id=1, source_target_pairs={{0,1},{1,2},{2,3},{3,4},{4,5},{5,6},{6,7},{7,8},{8,9},{9,10},{10,1... | collective-permute-start | bytes 5308424 | tf_op jit(solution)/shard_map/ppermute | solution.py:306
  402.3 25.1 %collective-permute-start.7 = (bf16[576,1536]{1,0:T(8,128)(2,1)}, bf16[576,1536]{1,0:T(8,128)(2,1)}, u32[]{:S(2)}, u32[]{:S(2)}) collective-permute-start(bf16[576,1536]{1,0:T(8,128)(2,1)} %copy.283), channel_id=1, source_target_pairs={{1,0},{2,1},{3,2},{4,3},{5,4},{6,5},{7,6},{8,7},{9,8},{10,9},{11,1... | collective-permute-start | bytes 5308424 | tf_op jit(solution)/shard_map/ppermute | solution.py:305
  438.6 1104.7 %reduce-scatter.10.cloned.1.call-start = ((), (), s32[]{:S(2)}) async-start(), calls=%async_computation.8 | async-start | bytes 2506752 | tf_op jit(solution)/shard_map/reduce_scatter | solution.py:357
  438.6 764.3 %copy-start.4 = (f32[8,64,768]{2,1,0:T(8,128)S(1)}, f32[8,64,768]{2,1,0:T(8,128)}, u32[]{:S(2)}) copy-start(f32[8,64,768]{2,1,0:T(8,128)} %get-tuple-element.1693) | copy-start | bytes 4718596
  438.7 764.3 %copy-start.53 = (f32[8,64,1]{1,0,2:T(8,128)S(1)}, f32[8,64,1]{1,0,2:T(8,128)}, u32[]{:S(2)}) copy-start(f32[8,64,1]{1,0,2:T(8,128)} %copy-done.52) | copy-start | bytes 6148
  438.7 764.3 %copy-start.61 = (f32[8,64,1]{1,0,2:T(8,128)S(1)}, f32[8,64,1]{1,0,2:T(8,128)}, u32[]{:S(2)}) copy-start(f32[8,64,1]{1,0,2:T(8,128)} %copy-done.60) | copy-start | bytes 6148
  440.3 761.4 %collective-permute-start.6 = (bf16[8,64,768]{2,1,0:T(8,128)(2,1)S(1)}, bf16[8,64,768]{2,1,0:T(8,128)(2,1)S(1)}, u32[]{:S(2)}, u32[]{:S(2)}) collective-permute-start(bf16[8,64,768]{2,1,0:T(8,128)(2,1)S(1)} %convert_element_type.334), channel_id=1, source_target_pairs={{16,0},{17,1},{18,2},{19,3},{20,4},{21,5},{22,6},{23,7},{24,8},{25... | collective-permute-start | bytes 2359304 | tf_op jit(solution)/shard_map/ppermute | solution.py:276
  444.0 835.0 %collective-permute-start.5 = (bf16[8,64,768]{2,1,0:T(8,128)(2,1)}, bf16[8,64,768]{2,1,0:T(8,128)(2,1)}, u32[]{:S(2)}, u32[]{:S(2)}) collective-permute-start(bf16[8,64,768]{2,1,0:T(8,128)(2,1)} %convert_element_type.332), channel_id=1, source_target_pairs={{16,0},{17,1},{18,2},{19,3},{20,4},{21,5},{22,6},{23,7},{24,8},{25... | collective-permute-start | bytes 2359304 | tf_op jit(solution)/shard_map/ppermute | solution.py:276
  1203.0 77.3 %copy-start.2 = (f32[8,64,768]{2,1,0:T(8,128)S(1)}, f32[8,64,768]{2,1,0:T(8,128)}, u32[]{:S(2)}) copy-start(f32[8,64,768]{2,1,0:T(8,128)} %get-tuple-element.1692) | copy-start | bytes 4718596
  1203.0 77.3 %copy-start.51 = (f32[8,64,1]{1,0,2:T(8,128)S(1)}, f32[8,64,1]{1,0,2:T(8,128)}, u32[]{:S(2)}) copy-start(f32[8,64,1]{1,0,2:T(8,128)} %copy-done.50) | copy-start | bytes 6148
  1203.0 77.3 %copy-start.59 = (f32[8,64,1]{1,0,2:T(8,128)S(1)}, f32[8,64,1]{1,0,2:T(8,128)}, u32[]{:S(2)}) copy-start(f32[8,64,1]{1,0,2:T(8,128)} %copy-done.58) | copy-start | bytes 6148
  1396.2 147.2 %all-reduce.13.cloned.1.call-start = ((), (), s32[]{:S(2)}) async-start(), calls=%async_computation.14 | async-start | bytes 1179648 | tf_op jit(solution)/shard_map/psum | solution.py:360
  1398.4 212.2 %reduce-scatter.8.cloned.1.call-start = ((), (), s32[]{:S(2)}) async-start(), calls=%async_computation.7 | async-start | bytes 7520256 | tf_op jit(solution)/shard_map/reduce_scatter | solution.py:357
  1405.2 320.9 %reduce-scatter.12.cloned.1.call-start = ((), (), s32[]{:S(2)}) async-start(), calls=%async_computation.9 | async-start | bytes 10027008 | tf_op jit(solution)/shard_map/reduce_scatter | solution.py:357
  1415.4 427.0 %reduce-scatter.14.cloned.1.call-start = ((), (), s32[]{:S(2)}) async-start(), calls=%async_computation.10 | async-start | bytes 10027008 | tf_op jit(solution)/shard_map/reduce_scatter | solution.py:357
  1506.4 34.8 %collective-permute-start.9 = (f32[288,768]{1,0:T(8,128)S(1)}, f32[288,768]{1,0:T(8,128)S(1)}, u32[]{:S(2)}, u32[]{:S(2)}) collective-permute-start(f32[288,768]{1,0:T(8,128)S(1)} %slice.115), channel_id=1, source_target_pairs={{16,0},{17,1},{18,2},{19,3},{20,4},{21,5},{22,6},{23,7},{24,8},{25... | collective-permute-start | bytes 2654216 | tf_op jit(solution)/shard_map/ppermute | solution.py:316
  (76 other events, 581.0 us)
Sparse Core Ops, SparseCore 0:
  380.7 823.3 reduce-scatter.15
  1208.3 61.9 reduce-scatter.19
  1274.2 74.5 reduce-scatter.17
  1396.3 80.6 reduce-scatter.9
  1480.4 31.1 all-reduce.12
  1516.6 93.8 reduce-scatter.7
  1615.2 110.8 reduce-scatter.11
  1731.3 111.1 reduce-scatter.13

commit v2 on v1

--- a/solution.py
+++ b/solution.py
@@ -3,6 +3,8 @@
 import jax
 import jax.numpy as jnp
 from jax import lax
+from jax.experimental import pallas as pl
+from jax.experimental.pallas import tpu as pltpu
 from jax.sharding import PartitionSpec as P
 
 H = 12
@@ -105,45 +107,169 @@
     return dh2 + dx, (d_gain, d_bias), pairs
 
 
-def cross_core_fwd(qc, pool_k, pool_v, pick):
-    s = jnp.einsum("rqhd,pkhd->rhqpk", qc, pool_k, preferred_element_type=F32) * SCALE
-    allowed = pick[:, :, None] == jnp.arange(pool_k.shape[0])[None, None, :]
-    s = jnp.where(allowed[:, None, :, :, None], s, MASKED)
-    p = softmax_rows(s, (-2, -1))
-    oc = jnp.einsum("rhqpk,pkhd->rqhd", bf(p), pool_v, preferred_element_type=F32)
-    return bf(oc), p
-
-
-def cross_core_bwd(doc, qc, pool_k, pool_v, p):
-    dp = jnp.einsum("rqhd,pkhd->rhqpk", doc, pool_v, preferred_element_type=F32)
-    ds = bf(p * (dp - jnp.sum(p * dp, (-2, -1), keepdims=True)))
-    dqc = jnp.einsum("rhqpk,pkhd->rqhd", ds, pool_k, preferred_element_type=F32) * SCALE
-    dk = jnp.einsum("rhqpk,rqhd->pkhd", ds, qc, preferred_element_type=F32) * SCALE
-    dv = jnp.einsum("rhqpk,rqhd->pkhd", bf(p), doc, preferred_element_type=F32)
-    return dqc, dk, dv
-
-
-def cross_fwd(h2, pick, pool_k, pool_v, gain, bias, wq, wo):
-    r, t = pick.shape
+RB = 2
+
+
+def _dot_nt(a, b):
+    return lax.dot_general(a, b, (((1,), (1,)), ((), ())), preferred_element_type=F32)
+
+
+def _dot_tn(a, b):
+    return lax.dot_general(a, b, (((0,), (0,)), ((), ())), preferred_element_type=F32)
+
+
+def _dot(a, b):
+    return lax.dot_general(a, b, (((1,), (0,)), ((), ())), preferred_element_type=F32)
+
+
+def _probs(q, ka, kb, first):
+    sa = _dot_nt(q, ka) * SCALE
+    sb = _dot_nt(q, kb) * SCALE
+    s = jnp.where(first, sa, sb)
+    top = jnp.max(s, -1, keepdims=True)
+    e = jnp.exp(s - top)
+    return e / jnp.sum(e, -1, keepdims=True)
+
+
+def _fwd_kernel(slot_ref, cut_ref, q_ref, pool_ref, o_ref):
+    i = pl.program_id(0)
+    t = q_ref.shape[1]
+    d = H * HD
+    for j in range(RB):
+        r = i * RB + j
+        a = slot_ref[2 * r]
+        b = slot_ref[2 * r + 1]
+        first = lax.broadcasted_iota(jnp.int32, (t, 1), 0) < cut_ref[r]
+        for h in range(H):
+            cols = pl.ds(h * HD, HD)
+            vcols = pl.ds(d + h * HD, HD)
+            q = q_ref[j, :, cols]
+            p = _probs(q, pool_ref[a, :, cols], pool_ref[b, :, cols], first).astype(BF16)
+            zero = jnp.zeros_like(p)
+            o = _dot(jnp.where(first, p, zero), pool_ref[a, :, vcols]) + _dot(
+                jnp.where(first, zero, p), pool_ref[b, :, vcols]
+            )
+            o_ref[j, :, cols] = o.astype(o_ref.dtype)
+
+
+def _bwd_kernel(slot_ref, cut_ref, q_ref, do_ref, pool_ref, dq_ref, dpool_ref):
+    i = pl.program_id(0)
+    t = q_ref.shape[1]
+    d = H * HD
+
+    @pl.when(i == 0)
+    def _():
+        dpool_ref[...] = jnp.zeros_like(dpool_ref)
+
+    for j in range(RB):
+        r = i * RB + j
+        a = slot_ref[2 * r]
+        b = slot_ref[2 * r + 1]
+        first = lax.broadcasted_iota(jnp.int32, (t, 1), 0) < cut_ref[r]
+        for h in range(H):
+            cols = pl.ds(h * HD, HD)
+            vcols = pl.ds(d + h * HD, HD)
+            q = q_ref[j, :, cols]
+            do = do_ref[j, :, cols]
+            ka = pool_ref[a, :, cols]
+            kb = pool_ref[b, :, cols]
+            va = pool_ref[a, :, vcols]
+            vb = pool_ref[b, :, vcols]
+            p = _probs(q, ka, kb, first)
+            dp = jnp.where(first, _dot_nt(do, va), _dot_nt(do, vb))
+            ds = (p * (dp - jnp.sum(p * dp, -1, keepdims=True))).astype(BF16)
+            zero = jnp.zeros_like(ds)
+            dsa = jnp.where(first, ds, zero)
+            dsb = jnp.where(first, zero, ds)
+            dq = (_dot(dsa, ka) + _dot(dsb, kb)) * SCALE
+            dq_ref[j, :, cols] = dq.astype(dq_ref.dtype)
+            pb = p.astype(BF16)
+            pa_ = jnp.where(first, pb, zero)
+            pb_ = jnp.where(first, zero, pb)
+            dpool_ref[a, :, cols] += _dot_tn(dsa, q) * SCALE
+            dpool_ref[a, :, vcols] += _dot_tn(pa_, do)
+            dpool_ref[b, :, cols] += _dot_tn(dsb, q) * SCALE
+            dpool_ref[b, :, vcols] += _dot_tn(pb_, do)
+
+
+def cross_attention_fwd(qc, pool, slots, cuts):
+    r, t, d = qc.shape
+    spec = pltpu.PrefetchScalarGridSpec(
+        num_scalar_prefetch=2,
+        grid=(r // RB,),
+        in_specs=[
+            pl.BlockSpec((RB, t, d), lambda i, s, c: (i, 0, 0)),
+            pl.BlockSpec(pool.shape, lambda i, s, c: (0, 0, 0)),
+        ],
+        out_specs=pl.BlockSpec((RB, t, d), lambda i, s, c: (i, 0, 0)),
+    )
+    flops = r * H * 4 * 2 * t * pool.shape[1] * HD
+    return pl.pallas_call(
+        _fwd_kernel,
+        grid_spec=spec,
+        out_shape=jax.ShapeDtypeStruct((r, t, d), BF16),
+        compiler_params=pltpu.CompilerParams(
+            dimension_semantics=("arbitrary",), vmem_limit_bytes=48 * 1024 * 1024
+        ),
+        cost_estimate=pl.CostEstimate(
+            flops=flops,
+            transcendentals=r * H * t * 2 * pool.shape[1],
+            bytes_accessed=2 * qc.size * 2 + pool.size * 2,
+        ),
+    )(slots.reshape(-1), cuts, qc, pool)
+
+
+def cross_attention_bwd(qc, doc, pool, slots, cuts):
+    r, t, d = qc.shape
+    spec = pltpu.PrefetchScalarGridSpec(
+        num_scalar_prefetch=2,
+        grid=(r // RB,),
+        in_specs=[
+            pl.BlockSpec((RB, t, d), lambda i, s, c: (i, 0, 0)),
+            pl.BlockSpec((RB, t, d), lambda i, s, c: (i, 0, 0)),
+            pl.BlockSpec(pool.shape, lambda i, s, c: (0, 0, 0)),
+        ],
+        out_specs=[
+            pl.BlockSpec((RB, t, d), lambda i, s, c: (i, 0, 0)),
+            pl.BlockSpec(pool.shape, lambda i, s, c: (0, 0, 0)),
+        ],
+    )
+    flops = r * H * 10 * 2 * t * pool.shape[1] * HD
+    return pl.pallas_call(
+        _bwd_kernel,
+        grid_spec=spec,
+        out_shape=(
+            jax.ShapeDtypeStruct((r, t, d), BF16),
+            jax.ShapeDtypeStruct(pool.shape, F32),
+        ),
+        compiler_params=pltpu.CompilerParams(
+            dimension_semantics=("arbitrary",), vmem_limit_bytes=60 * 1024 * 1024
+        ),
+        cost_estimate=pl.CostEstimate(
+            flops=flops,
+            transcendentals=r * H * t * 2 * pool.shape[1],
+            bytes_accessed=3 * qc.size * 2 + pool.size * 2 + pool.size * 4,
+        ),
+    )(slots.reshape(-1), cuts, qc, doc, pool)
+
+
+def cross_fwd(h2, slots, cuts, pool, gain, bias, wq, wo):
     y, csave = norm_fwd(h2, gain, bias)
     c = bf(y)
-    qc = bf(mm(c, wq)).reshape(r, t, H, HD)
-    oc, p = cross_core_fwd(qc, pool_k, pool_v, pick)
-    oc = oc.reshape(r, t, H * HD)
+    qc = bf(mm(c, wq))
+    oc = cross_attention_fwd(qc, pool, slots, cuts)
     h3 = h2 + mm(oc, wo)
-    return h3, dict(csave=csave, c=c, qc=qc, p=p, oc=oc)
-
-
-def cross_bwd(dh3, sv, pool_k, pool_v, gain, wq, wo):
-    r, t = dh3.shape[:2]
+    return h3, dict(csave=csave, c=c, qc=qc, oc=oc)
+
+
+def cross_bwd(dh3, sv, slots, cuts, pool, gain, wq, wo):
     g3 = bf(dh3)
-    doc = bf(mm_t(g3, wo)).reshape(r, t, H, HD)
-    dqc, dk, dv = cross_core_bwd(doc, sv["qc"], pool_k, pool_v, sv["p"])
-    dqc = bf(dqc.reshape(r, t, H * HD))
+    doc = bf(mm_t(g3, wo))
+    dqc, dpool = cross_attention_bwd(sv["qc"], doc, pool, slots, cuts)
     dc = mm_t(dqc, wq)
     dx, d_gain, d_bias = norm_bwd(dc, sv["csave"], gain)
     pairs = dict(oc=sv["oc"], g3=g3, c=sv["c"], dqc=dqc)
-    return dh3 + dx, (d_gain, d_bias), pairs, dk, dv
+    return dh3 + dx, (d_gain, d_bias), pairs, dpool
 
 
 def gelu(z):
@@ -216,12 +342,10 @@
     kv_next = lax.ppermute(kv_own, "dp", ring_down)
     pool = jnp.stack([kv_prev, kv_own, kv_next], 0)
     img_tok = pool.shape[1]
-    pool = pool.reshape(3, img_tok, 2, H, HD)
-    pool_k, pool_v = pool[:, :, 0], pool[:, :, 1]
 
     first_img = (row_block[:, None] + seg_image) % n_img
     slot = (first_img - dp_index + 1 + n_img) % n_img
-    pick_all = jnp.where(seg_ids == 0, slot[:, :1], slot[:, 1:2])
+    cut_all = jnp.sum((seg_ids == 0).astype(jnp.int32), 1)
 
     def chunk(a, m):
         return a[m * rc : (m + 1) * rc]
@@ -233,10 +357,10 @@
         out, s_ffn = ffn_fwd(h2, g2, b2, wup, bup, wdown, bdown)
         return out, (s_self, s_ffn)
 
-    def upper_fwd(sent, seg, pick, pk, pv):
+    def upper_fwd(sent, seg, slots, cuts, pool):
         hid = sent.astype(F32)
         h2, s_self = self_fwd(hid, seg, g1, b1, wqkv, wout)
-        h3, s_cross = cross_fwd(h2, pick, pk, pv, lnc_gain, lnc_bias, wq_cross, wo_cross)
+        h3, s_cross = cross_fwd(h2, slots, cuts, pool, lnc_gain, lnc_bias, wq_cross, wo_cross)
         out, s_ffn = ffn_fwd(h3, g2, b2, wup, bup, wdown, bdown)
         return out, (s_self, s_cross, s_ffn)
 
@@ -249,30 +373,31 @@
     up_out, up_saved = [], []
     for m in range(MICRO):
         out, saved = run_on(
-            up, upper_fwd, sent[m], chunk(seg_ids, m), chunk(pick_all, m), pool_k, pool_v
+            up, upper_fwd, sent[m], chunk(seg_ids, m), chunk(slot, m), chunk(cut_all, m), pool
         )
         up_out.append(out)
         up_saved.append(saved)
 
     cot = cotangent[0].astype(F32)
 
-    def upper_bwd(gout, saved, pk, pv):
+    def upper_bwd(gout, saved, slots, cuts, pool):
         s_self, s_cross, s_ffn = saved
         dh3, ln2g, pf = ffn_bwd(gout, s_ffn, g2, wup, wdown)
-        dh2, lncg, pc, dk, dv = cross_bwd(dh3, s_cross, pk, pv, lnc_gain, wq_cross, wo_cross)
+        dh2, lncg, pc, dpool = cross_bwd(dh3, s_cross, slots, cuts, pool, lnc_gain, wq_cross, wo_cross)
         dh, ln1g, ps = self_bwd(dh2, s_self, g1, wqkv, wout)
-        return dh, (ln1g, ln2g, lncg), (ps, pf, pc), dk, dv
+        return dh, (ln1g, ln2g, lncg), (ps, pf, pc), dpool
 
     up_grad, up_small, up_pairs = [], [], []
     returned = []
-    pool_dk = pool_dv = None
+    pool_grad = None
     for m in range(MICRO):
-        dh, small, pairs, dk, dv = run_on(up, upper_bwd, chunk(cot, m), up_saved[m], pool_k, pool_v)
+        dh, small, pairs, dpool = run_on(
+            up, upper_bwd, chunk(cot, m), up_saved[m], chunk(slot, m), chunk(cut_all, m), pool
+        )
         up_grad.append(dh)
         up_small.append(small)
         up_pairs.append(pairs)
-        pool_dk = dk if pool_dk is None else pool_dk + dk
-        pool_dv = dv if pool_dv is None else pool_dv + dv
+        pool_grad = dpool if pool_grad is None else pool_grad + dpool
         returned.append(lax.ppermute(bf(dh), "section", [(1, 0)]))
 
     def cat(name_path, pairs_list):
@@ -297,11 +422,7 @@
 
     up_w, cross_w = run_on(up, upper_wgrads, up_pairs)
 
-    parts = bf(
-        jnp.concatenate(
-            [pool_dk.reshape(3, img_tok, H * HD), pool_dv.reshape(3, img_tok, H * HD)], -1
-        )
-    )
+    parts = bf(pool_grad)
     from_next = lax.ppermute(parts[0], "dp", ring_down)
     from_prev = lax.ppermute(parts[2], "dp", ring_up)
     kv_grad = bf(parts[1].astype(F32) + from_next.astype(F32) + from_prev.astype(F32))

time: 1860 us -> 1590 us (0.85)
  waiting for transfers between devices: 1080 us -> 890 us
  local copies, waits for them, and re-layouts: 278 us -> 213 us
    ppermute x2, waiting for transfers between devices: 756 us -> 548 us  [per_device(): returned.append(lax.ppermute(bf(dh), 'section', [(1, 0)]))]
    another operation x95 -> x89, local copies, waits for them, and re-layouts: 152 us -> 108 us
    ppermute x1, waiting for transfers between devices: 0.01 us -> 20 us  [per_device(): from_next = lax.ppermute(parts[0], 'dp', ring_down)]
    convert_element_type x15 -> x16, other arithmetic: 34.9 us -> 37.6 us  [bf(): return x.astype(BF16)]
  transfers between devices with their start and end apart: 18 -> 18, of which waited for: 7 -> 8; matrix products, arithmetic and copies ran while one was open for 27% -> 29% of each run, Pallas kernels for 0% -> 0%
where the time goes in v2:
time: 1590 us; the launch traced here: 1580 us
  waiting for transfers between devices  890 us (56%)
  local copies, waits for them, and re-layouts  213 us (13%)
  matrix products  202 us (13%)
  other arithmetic  110 us (7%)
  blocking collectives  96.5 us (6%)
  loops' own time  31.1 us (2%)
  starting transfers between devices  19.8 us (1%)
  between operations  16.8 us (1%)
    ppermute x2, waiting for transfers between devices, per_device(): returned.append(lax.ppermute(bf(dh), 'section', [(1, 0)]))  548 us
    reduce_scatter x7, waiting for transfers between devices, rs(): return lax.psum_scatter(a, 'dp', scatter_dimension=dim, tiled=True)  300 us
    another operation x89, local copies, waits for them, and re-layouts  108 us
    unnamed x1, blocking collectives  74.9 us
    dot_general x8, matrix products, mm_t(): return jnp.einsum('...e,de->...d', g, w, preferred_element_type=F32)  66.6 us
    dot_general x8, matrix products, mm(): return jnp.einsum('...d,de->...e', a, w, preferred_element_type=F32)  65 us
    convert_element_type x16, other arithmetic, bf(): return x.astype(BF16)  37.6 us
  transfers between devices with their start and end apart: 18, of which 8 were waited for; matrix products, arithmetic and copies ran while one was open for 29% of the time, Pallas kernels for 0%

profile of v2, /device:TPU:0, one launch (start us, length us, event | category | flops | bytes accessed | tf_op | source)
XLA Modules:
  0.0 1578.8 jit_solution(14542367877598359825)
XLA Ops:
  12.1 9.7 collective-permute-done.1
  32.1 72.2 %conditional.12 = (f32[8,64,768]{2,1,0:T(8,128)}, bf16[8,64,12,64]{3,1,2,0:T(8,128)(2,1)}, bf16[8,64,768]{2,1,0:T(8,128)(2,1)}, f32[8,64,768]{2,1,0:T(8,128)}, f...) conditional(s32[]{:T(128)} %convert_element_type.284, ...), branch_computations={%region_0.0_spmd, %region_1.8_spmd} | conditional | flops 7464489984 | bytes 121335072 | solution.py:31
  78.4 19.7 %fusion.69 = (bf16[8,64,3072]{2,1,0:T(8,128)(2,1)}, f32[8,64,3072]{2,1,0:T(8,128)}) fusion(f32[3072]{0:T(1024)S(1)} %bitcast.554, bf16[8,64,768]{2,1,0:T(8,128)(2,1)} %get-tuple-element.1768, bf16[768,3072]{1,0:T(8,128)(2,1)S(1)} %bitcast.515), kind=kOutput, calls=%fused_computation.87 | convolution fusion | flops 2519728128 | bytes 14954496 | tf_op jit(solution)/shard_map/cond/branch_1_fun/...d,de->...e/dot_general | solution.py:58
  109.0 71.6 %conditional.15 = (f32[8,64,768]{2,1,0:T(8,128)}, bf16[8,64,12,64]{3,1,2,0:T(8,128)(2,1)}, bf16[8,64,768]{2,1,0:T(8,128)(2,1)}, f32[8,64,768]{2,1,0:T(8,128)}, f...) conditional(s32[]{:T(128)} %convert_element_type.284, ...), branch_computations={%region_21.22_spmd, %region_22.29_spmd} | conditional | flops 7464489984 | bytes 121335072 | solution.py:31
  154.9 19.8 %fusion.137 = (bf16[8,64,3072]{2,1,0:T(8,128)(2,1)}, f32[8,64,3072]{2,1,0:T(8,128)}) fusion(f32[3072]{0:T(1024)S(1)} %bitcast.555, bf16[8,64,768]{2,1,0:T(8,128)(2,1)} %get-tuple-element.1698, bf16[768,3072]{1,0:T(8,128)(2,1)S(1)} %bitcast.517), kind=kOutput, calls=%fused_computation.215 | convolution fusion | flops 2519728128 | bytes 14954496 | tf_op jit(solution)/shard_map/cond/branch_1_fun/...d,de->...e/dot_general | solution.py:58
  199.3 29.4 %conditional.16 = (bf16[8,64,12,64]{3,1,2,0:T(8,128)(2,1)}, bf16[8,64,768]{2,1,0:T(8,128)(2,1)}, f32[8,64,768]{2,1,0:T(8,128)}, f32[8,64,1]{1,0,2:T(8,128)S(1)},...) conditional(s32[]{:T(128)} %convert_element_type.283, ...), branch_computations={%region_29.30_spmd, %region_30.39_spmd} | conditional | flops 10490288128 | bytes 182703808 | solution.py:31
  228.8 22.6 %conditional.18 = (f32[8,64,768]{2,1,0:T(8,128)S(1)}, f32[768]{0:T(1024)S(1)}, f32[768]{0:T(1024)S(1)}, f32[768]{0:T(1024)S(1)}, f32[768]{0:T(1024)S(1)}, /*inde...) conditional(s32[]{:T(128)} %convert_element_type.283, ...), branch_computations={%region_54.55_spmd, %region_55.69_spmd} | conditional | flops 13324111872 | bytes 171006560 | solution.py:31
  252.6 29.3 %conditional.14 = (bf16[8,64,12,64]{3,1,2,0:T(8,128)(2,1)}, bf16[8,64,768]{2,1,0:T(8,128)(2,1)}, f32[8,64,768]{2,1,0:T(8,128)}, f32[8,64,1]{1,0,2:T(8,128)S(1)},...) conditional(s32[]{:T(128)} %convert_element_type.283, ...), branch_computations={%region_11.12_spmd, %region_12.21_spmd} | conditional | flops 10490288128 | bytes 176412288 | solution.py:31
  281.9 25.0 %conditional.17 = (f32[8,64,768]{2,1,0:T(8,128)S(1)}, f32[768]{0:T(1024)S(1)}, f32[768]{0:T(1024)S(1)}, f32[768]{0:T(1024)S(1)}, f32[768]{0:T(1024)S(1)}, /*inde...) conditional(s32[]{:T(128)} %convert_element_type.283, ...), branch_computations={%region_39.40_spmd, %region_40.54_spmd} | conditional | flops 13324111872 | bytes 171006560 | solution.py:31
  308.1 22.9 %conditional.22 = (f32[768,2304]{1,0:T(8,128)}, f32[768,768]{1,0:T(8,128)}, f32[768,3072]{1,0:T(8,128)}, f32[3072]{0:T(1024)}, f32[3072,768]{1,0:T(8,128)}, /*in...) conditional(s32[]{:T(128)} %convert_element_type.283, () %tuple.134, ...), branch_computations={%region_95.96_spmd, %region_96.99_spmd} | conditional | flops 16931090432 | bytes 132136328 | solution.py:31
  343.8 20.0 %collective-permute-done.7 = bf16[576,1536]{1,0:T(8,128)(2,1)S(1)} collective-permute-done((bf16[576,1536]{1,0:T(8,128)(2,1)S(1)}, bf16[576,1536]{1,0:T(8,128)(2,1)S(1)}, u32[]{:S(2)}, u32[]{:S(2)}) %collective-permute-start.7) | collective-permute-done | bytes 1769504 | tf_op jit(solution)/shard_map/ppermute | solution.py:426
  379.8 548.2 %collective-permute-done.6 = bf16[8,64,768]{2,1,0:T(8,128)(2,1)S(1)} collective-permute-done((bf16[8,64,768]{2,1,0:T(8,128)(2,1)S(1)}, bf16[8,64,768]{2,1,0:T(8,128)(2,1)S(1)}, u32[]{:S(2)}, u32[]{:S(2)}) %collective-permute-start.6) | collective-permute-done | bytes 786464 | tf_op jit(solution)/shard_map/ppermute | solution.py:401
  929.3 75.9 %conditional.20 = (f32[768]{0:T(1024)S(1)}, f32[768]{0:T(1024)S(1)}, f32[768]{0:T(1024)S(1)}, f32[768]{0:T(1024)S(1)}, bf16[8,64,2304]{2,1,0:T(8,128)(2,1)}, /*i...) conditional(s32[]{:T(128)} %convert_element_type.284, ...), branch_computations={%region_80.81_spmd, %region_81.91_spmd} | conditional | flops 7580802048 | bytes 115728592 | solution.py:31
  935.0 19.2 %fusion.287 = bf16[8,64,3072]{2,1,0:T(8,128)(2,1)} fusion(f32[8,64,3072]{2,1,0:T(8,128)} %get-tuple-element.587, bf16[8,64,768]{2,1,0:T(8,128)(2,1)} %get-tuple-element.1873, bf16[3072,768]{1,0:T(8,128)(2,1)} %get-tuple-element.588), kind=kOutput, calls=%fused_computation.517 | convolution fusion | flops 2529165312 | bytes 14942208 | tf_op jit(solution)/shard_map/cond/branch_1_fun/...e,de->...d/dot_general | solution.py:62
  1006.7 74.2 %conditional.19 = (f32[768]{0:T(1024)S(1)}, f32[768]{0:T(1024)S(1)}, f32[768]{0:T(1024)S(1)}, f32[768]{0:T(1024)S(1)}, bf16[8,64,2304]{2,1,0:T(8,128)(2,1)}, /*i...) conditional(s32[]{:T(128)} %convert_element_type.284, ...), branch_computations={%region_69.70_spmd, %region_70.80_spmd} | conditional | flops 7580802048 | bytes 109437112 | solution.py:31
  1010.3 19.9 %fusion.262 = bf16[8,64,3072]{2,1,0:T(8,128)(2,1)} fusion(f32[8,64,3072]{2,1,0:T(8,128)} %get-tuple-element.566, bf16[8,64,768]{2,1,0:T(8,128)(2,1)} %get-tuple-element.1939, bf16[3072,768]{1,0:T(8,128)(2,1)} %get-tuple-element.567), kind=kOutput, calls=%fused_computation.466 | convolution fusion | flops 2529165312 | bytes 14942208 | tf_op jit(solution)/shard_map/cond/branch_1_fun/...e,de->...d/dot_general | solution.py:62
  1080.9 39.6 %conditional.23 = (f32[768,2304]{1,0:T(8,128)}, f32[768,768]{1,0:T(8,128)S(1)}, f32[768,3072]{1,0:T(8,128)}, f32[3072]{0:T(1024)S(1)}, f32[3072,768]{1,0:T(8,128)}, /*index=5*/f32[768]{0:T(1024)S(1)}) conditional(s32[]{:T(128)} %convert_element_type.284, () %tuple.136, (bf16[8,64,768]{2,1,0:T(8,128)(2,1)}, bf16[8,64,768]{2,1,0:T(8,128)(2,1)}, ...), branch_computations={%region_99.100_spmd, %region_100.103_spmd} | conditional | flops 14512025600 | bytes 77085744 | solution.py:31
  1093.1 9.7 fusion.44
  1131.3 10.2 broadcast_select_fusion.1
  1152.9 74.9 %all-reduce.8 = (f32[768]{0:T(1024)S(1)}, f32[768]{0:T(1024)S(1)}, f32[768]{0:T(1024)S(1)}, f32[768]{0:T(1024)S(1)}, f32[3072]{0:T(1024)S(1)}, /*index=5*/f32[768]{0:T(1024)S(1)}, f32[768]{0:T(1024)S(1)}, f32[768]{0:T(1024)S(1)}) all-reduce(f32[768]{0:T(1024)S(1)} %get-tuple-element.1673, ...), channel_id=2, replica_groups=mesh['section'=2,'dp'=16] {'dp'}, use_global_device_ids=true, to_apply=%region_93.94.clone | all-reduce | flops 8448 | bytes 67584
  1232.0 21.6 %all-reduce.9 = (f32[48]{0:T(128)}, f32[48]{0:T(128)}) all-reduce(f32[48]{0:T(128)S(1)} %broadcast_select_fusion.10, f32[48]{0:T(128)S(1)} %broadcast_select_fusion.9), channel_id=1, replica_groups=mesh['section'=2,'dp'=16] {'section'}, use_global_device_ids=true, to_apply=%region_112.113 | all-reduce | flops 96 | bytes 768 | tf_op jit(solution)/shard_map/psum | solution.py:481
  1266.6 68.3 %reduce-scatter.8.cloned.1.call-done = f32[48,2304]{1,0:T(8,128)} async-done(((f32[768,2304]{1,0:T(8,128)}), f32[48,2304]{1,0:T(8,128)}) %reduce-scatter.8.cloned.1.call-update) | async-done | bytes 442384 | tf_op jit(solution)/shard_map/reduce_scatter | solution.py:478
  1334.9 115.6 %reduce-scatter.12.cloned.1.call-done = f32[48,3072]{1,0:T(8,128)} async-done(((f32[768,3072]{1,0:T(8,128)}), f32[48,3072]{1,0:T(8,128)}) %reduce-scatter.12.cloned.1.call-update) | async-done | bytes 589840 | tf_op jit(solution)/shard_map/reduce_scatter | solution.py:478
  1450.5 116.4 %reduce-scatter.14.cloned.1.call-done = f32[192,768]{1,0:T(8,128)} async-done(((f32[3072,768]{1,0:T(8,128)}), f32[192,768]{1,0:T(8,128)}) %reduce-scatter.14.cloned.1.call-update) | async-done | bytes 589840 | tf_op jit(solution)/shard_map/reduce_scatter | solution.py:478
  (460 shorter events, 464.5 us)
Async XLA Ops:
  7.2 1115.0 %reduce-scatter.16.cloned.1.call-start = ((), (), s32[]{:S(2)}) async-start(), calls=%async_computation.11 | async-start | bytes 2506752 | tf_op jit(solution)/shard_map/reduce_scatter | solution.py:478
  7.2 14.6 collective-permute-start.1
  26.6 160.7 %collective-permute-start.3 = (bf16[576,1536]{1,0:T(8,128)(2,1)}, bf16[576,1536]{1,0:T(8,128)(2,1)}, u32[]{:S(2)}, u32[]{:S(2)}) collective-permute-start(bf16[576,1536]{1,0:T(8,128)(2,1)} %get-tuple-element.816), channel_id=1, source_target_pairs={{1,0},{2,1},{3,2},{4,3},{5,4},{6,5},{7,6},{8,7},{9,8},{10,9},{11,1... | collective-permute-start | bytes 5308424 | tf_op jit(solution)/shard_map/ppermute | solution.py:342
  29.7 157.6 %collective-permute-start.2 = (bf16[576,1536]{1,0:T(8,128)(2,1)}, bf16[576,1536]{1,0:T(8,128)(2,1)}, u32[]{:S(2)}, u32[]{:S(2)}) collective-permute-start(bf16[576,1536]{1,0:T(8,128)(2,1)} %get-tuple-element.816), channel_id=1, source_target_pairs={{0,1},{1,2},{2,3},{3,4},{4,5},{5,6},{6,7},{7,8},{8,9},{9,10},{10,1... | collective-permute-start | bytes 5308424 | tf_op jit(solution)/shard_map/ppermute | solution.py:341
  106.7 144.7 %collective-permute-start = (bf16[8,64,768]{2,1,0:T(8,128)(2,1)}, bf16[8,64,768]{2,1,0:T(8,128)(2,1)}, u32[]{:S(2)}, u32[]{:S(2)}) collective-permute-start(bf16[8,64,768]{2,1,0:T(8,128)(2,1)} %convert_element_type.286), channel_id=1, source_target_pairs={{0,16},{1,17},{2,18},{3,19},{4,20},{5,21},{6,22},{7,23},{8,24},{9,... | collective-permute-start | bytes 2359304 | tf_op jit(solution)/shard_map/ppermute | solution.py:372
  182.2 17.1 %collective-permute-start.4 = (bf16[8,64,768]{2,1,0:T(8,128)(2,1)S(1)}, bf16[8,64,768]{2,1,0:T(8,128)(2,1)S(1)}, u32[]{:S(2)}, u32[]{:S(2)}) collective-permute-start(bf16[8,64,768]{2,1,0:T(8,128)(2,1)S(1)} %convert_element_type.288), channel_id=1, source_target_pairs={{0,16},{1,17},{2,18},{3,19},{4,20},{5,21},{6,22},{7,23},{8,24},{9,... | collective-permute-start | bytes 2359304 | tf_op jit(solution)/shard_map/ppermute | solution.py:372
  331.0 791.9 %reduce-scatter.20.cloned.1.call-start = ((), (), s32[]{:S(2)}) async-start(), calls=%async_computation.13 | async-start | bytes 2506752 | tf_op jit(solution)/shard_map/reduce_scatter | solution.py:478
  331.8 791.8 %reduce-scatter.18.cloned.1.call-start = ((), (), s32[]{:S(2)}) async-start(), calls=%async_computation.12 | async-start | bytes 5013504 | tf_op jit(solution)/shard_map/reduce_scatter | solution.py:478
  339.9 23.9 %collective-permute-start.7 = (bf16[576,1536]{1,0:T(8,128)(2,1)S(1)}, bf16[576,1536]{1,0:T(8,128)(2,1)S(1)}, u32[]{:S(2)}, u32[]{:S(2)}) collective-permute-start(bf16[576,1536]{1,0:T(8,128)(2,1)S(1)} %get-tuple-element.1658), channel_id=1, source_target_pairs={{1,0},{2,1},{3,2},{4,3},{5,4},{6,5},{7,6},{8,7},{9,8},{10,9},{11,1... | collective-permute-start | bytes 5308424 | tf_op jit(solution)/shard_map/ppermute | solution.py:426
  343.8 24.8 %collective-permute-start.8 = (bf16[576,1536]{1,0:T(8,128)(2,1)S(1)}, bf16[576,1536]{1,0:T(8,128)(2,1)S(1)}, u32[]{:S(2)}, u32[]{:S(2)}) collective-permute-start(bf16[576,1536]{1,0:T(8,128)(2,1)S(1)} %get-tuple-element.1659), channel_id=1, source_target_pairs={{0,1},{1,2},{2,3},{3,4},{4,5},{5,6},{6,7},{7,8},{8,9},{9,10},{10,1... | collective-permute-start | bytes 5308424 | tf_op jit(solution)/shard_map/ppermute | solution.py:427
  373.3 893.3 %reduce-scatter.10.cloned.1.call-start = ((), (), s32[]{:S(2)}) async-start(), calls=%async_computation.8 | async-start | bytes 2506752 | tf_op jit(solution)/shard_map/reduce_scatter | solution.py:478
  374.6 554.7 %copy-start.6 = (f32[8,64,768]{2,1,0:T(8,128)S(1)}, f32[8,64,768]{2,1,0:T(8,128)}, u32[]{:S(2)}) copy-start(f32[8,64,768]{2,1,0:T(8,128)} %get-tuple-element.1661) | copy-start | bytes 4718596
  374.6 554.7 %copy-start.68 = (f32[8,64,1]{1,0,2:T(8,128)S(1)}, f32[8,64,1]{1,0,2:T(8,128)}, u32[]{:S(2)}) copy-start(f32[8,64,1]{1,0,2:T(8,128)} %copy-done.67) | copy-start | bytes 6148
  374.7 554.7 %copy-start.72 = (f32[8,64,1]{1,0,2:T(8,128)S(1)}, f32[8,64,1]{1,0,2:T(8,128)}, u32[]{:S(2)}) copy-start(f32[8,64,1]{1,0,2:T(8,128)} %copy-done.71) | copy-start | bytes 6148
  374.7 553.3 %collective-permute-start.6 = (bf16[8,64,768]{2,1,0:T(8,128)(2,1)S(1)}, bf16[8,64,768]{2,1,0:T(8,128)(2,1)S(1)}, u32[]{:S(2)}, u32[]{:S(2)}) collective-permute-start(bf16[8,64,768]{2,1,0:T(8,128)(2,1)S(1)} %convert_element_type.292), channel_id=1, source_target_pairs={{16,0},{17,1},{18,2},{19,3},{20,4},{21,5},{22,6},{23,7},{24,8},{25... | collective-permute-start | bytes 2359304 | tf_op jit(solution)/shard_map/ppermute | solution.py:401
  378.6 626.8 %collective-permute-start.5 = (bf16[8,64,768]{2,1,0:T(8,128)(2,1)}, bf16[8,64,768]{2,1,0:T(8,128)(2,1)}, u32[]{:S(2)}, u32[]{:S(2)}) collective-permute-start(bf16[8,64,768]{2,1,0:T(8,128)(2,1)} %convert_element_type.290), channel_id=1, source_target_pairs={{16,0},{17,1},{18,2},{19,3},{20,4},{21,5},{22,6},{23,7},{24,8},{25... | collective-permute-start | bytes 2359304 | tf_op jit(solution)/shard_map/ppermute | solution.py:401
  929.3 77.3 %copy-start.66 = (f32[8,64,1]{1,0,2:T(8,128)S(1)}, f32[8,64,1]{1,0,2:T(8,128)}, u32[]{:S(2)}) copy-start(f32[8,64,1]{1,0,2:T(8,128)} %copy-done.65) | copy-start | bytes 6148
  1122.2 144.4 %all-reduce.13.cloned.1.call-start = ((), (), s32[]{:S(2)}) async-start(), calls=%async_computation.14 | async-start | bytes 1179648 | tf_op jit(solution)/shard_map/psum | solution.py:481
  1124.4 210.5 %reduce-scatter.8.cloned.1.call-start = ((), (), s32[]{:S(2)}) async-start(), calls=%async_computation.7 | async-start | bytes 7520256 | tf_op jit(solution)/shard_map/reduce_scatter | solution.py:478
  1131.2 319.2 %reduce-scatter.12.cloned.1.call-start = ((), (), s32[]{:S(2)}) async-start(), calls=%async_computation.9 | async-start | bytes 10027008 | tf_op jit(solution)/shard_map/reduce_scatter | solution.py:478
  1141.5 425.4 %reduce-scatter.14.cloned.1.call-start = ((), (), s32[]{:S(2)}) async-start(), calls=%async_computation.10 | async-start | bytes 10027008 | tf_op jit(solution)/shard_map/reduce_scatter | solution.py:478
  1150.2 106.3 %copy-start.22 = (f32[8,64,768]{2,1,0:T(8,128)S(1)}, f32[8,64,768]{2,1,0:T(8,128)}, u32[]{:S(2)}) copy-start(f32[8,64,768]{2,1,0:T(8,128)} %copy-done.21) | copy-start | bytes 4718596
  1150.3 106.2 %copy-start.20 = (f32[8,64,768]{2,1,0:T(8,128)S(1)}, f32[8,64,768]{2,1,0:T(8,128)}, u32[]{:S(2)}) copy-start(f32[8,64,768]{2,1,0:T(8,128)} %copy-done.18) | copy-start | bytes 4718596
  1230.0 34.0 %collective-permute-start.9 = (f32[288,768]{1,0:T(8,128)}, f32[288,768]{1,0:T(8,128)}, u32[]{:S(2)}, u32[]{:S(2)}) collective-permute-start(f32[288,768]{1,0:T(8,128)} %slice.111), channel_id=1, source_target_pairs={{16,0},{17,1},{18,2},{19,3},{20,4},{21,5},{22,6},{23,7},{24,8},{25... | collective-permute-start | bytes 2654216 | tf_op jit(solution)/shard_map/ppermute | solution.py:437
  (81 other events, 694.2 us)
Sparse Core Ops, SparseCore 0:
  331.1 605.0 reduce-scatter.15
  940.5 61.9 reduce-scatter.19
  1006.3 74.4 reduce-scatter.17
  1122.3 79.0 reduce-scatter.9
  1204.8 31.4 all-reduce.12
  1241.3 93.5 reduce-scatter.7
  1339.6 110.8 reduce-scatter.11
  1455.7 111.1 reduce-scatter.13

commit v3 on v2

--- a/solution.py
+++ b/solution.py
@@ -366,14 +366,20 @@
 
     low_out, low_saved, sent = [], [], []
     for m in range(MICRO):
-        out, saved = run_on(low, lower_fwd, chunk(x, m), chunk(seg_ids, m))
+        x_m = chunk(x, m)
+        if m > 0:
+            x_m, low_out[-1] = lax.optimization_barrier((x_m, low_out[-1]))
+        out, saved = run_on(low, lower_fwd, x_m, chunk(seg_ids, m))
         low_out.append(out)
         low_saved.append(saved)
         sent.append(lax.ppermute(bf(out), "section", [(0, 1)]))
     up_out, up_saved = [], []
     for m in range(MICRO):
+        arriving = sent[m]
+        if m > 0:
+            arriving, up_out[-1] = lax.optimization_barrier((arriving, up_out[-1]))
         out, saved = run_on(
-            up, upper_fwd, sent[m], chunk(seg_ids, m), chunk(slot, m), chunk(cut_all, m), pool
+            up, upper_fwd, arriving, chunk(seg_ids, m), chunk(slot, m), chunk(cut_all, m), pool
         )
         up_out.append(out)
         up_saved.append(saved)
@@ -391,8 +397,11 @@
     returned = []
     pool_grad = None
     for m in range(MICRO):
+        cot_m = chunk(cot, m)
+        if m > 0:
+            cot_m, up_grad[-1] = lax.optimization_barrier((cot_m, up_grad[-1]))
         dh, small, pairs, dpool = run_on(
-            up, upper_bwd, chunk(cot, m), up_saved[m], chunk(slot, m), chunk(cut_all, m), pool
+            up, upper_bwd, cot_m, up_saved[m], chunk(slot, m), chunk(cut_all, m), pool
         )
         up_grad.append(dh)
         up_small.append(small)
@@ -437,6 +446,41 @@
     ig_first = lax.ppermute(image_grad_full[:half], "section", [(1, 0)])
     image_grad = jnp.where(up, image_grad_full[half:], ig_first)[None]
 
+    def tree_sum(xs):
+        total = xs[0]
+        for v in xs[1:]:
+            total = jax.tree.map(jnp.add, total, v)
+        return total
+
+    def rs(a, dim=0):
+        return lax.psum_scatter(a, "dp", scatter_dimension=dim, tiled=True)
+
+    def rs_bf(a, dim=0):
+        return rs(bf(a), dim).astype(F32)
+
+    def pack(vs):
+        return jnp.concatenate([v.reshape(n_dp, -1) for v in vs], 1)
+
+    def unpack(row, vs):
+        out, at = [], 0
+        for v in vs:
+            width = v.size // n_dp
+            out.append(row[:, at : at + width])
+            at += width
+        return out
+
+    def reduce_layer(lw, sm):
+        d_wqkv, d_wout, d_wup, d_bup, d_wdown, d_bdown = lw
+        big = [rs_bf(d_wqkv), rs_bf(d_wout), rs_bf(d_wup), rs_bf(d_wdown)]
+        vecs = [sm[0][0], sm[0][1], sm[1][0], sm[1][1], d_bup, d_bdown]
+        return big, vecs
+
+    up_sm = tree_sum(up_small)
+    a_big, a_vecs = reduce_layer(up_w, up_sm)
+    a_cross = [rs_bf(cross_w[0]), rs_bf(cross_w[1]), rs_bf(d_wkv)]
+    a_vecs = a_vecs + [up_sm[2][0], up_sm[2][1]]
+    a_small = unpack(rs(pack(a_vecs)), a_vecs)
+
     def lower_bwd(gout, saved):
         s_self, s_ffn = saved
         dh3, ln2g, pf = ffn_bwd(gout, s_ffn, g2, wup, wdown)
@@ -446,12 +490,29 @@
     low_grad, low_small, low_pairs = [], [], []
     for m in range(MICRO):
         gout = chunk(cot, m) + returned[m].astype(F32)
+        if m == 0:
+            gout, (a_big, a_small, a_cross) = lax.optimization_barrier(
+                (gout, (a_big, a_small, a_cross))
+            )
+        else:
+            gout, low_grad[-1] = lax.optimization_barrier((gout, low_grad[-1]))
         dh, small, pairs = run_on(low, lower_bwd, gout, low_saved[m])
         low_grad.append(dh)
         low_small.append(small)
         low_pairs.append(pairs)
 
     low_w = run_on(low, layer_weight_grads, low_pairs)
+    low_sm = tree_sum(low_small)
+    low_w, low_sm, (a_big, a_small, a_cross) = lax.optimization_barrier(
+        (low_w, low_sm, (a_big, a_small, a_cross))
+    )
+    b_big, b_vecs = reduce_layer(low_w, low_sm)
+    b_small = unpack(rs(pack(b_vecs)), b_vecs)
+
+    cross_out = a_cross + a_small[6:]
+    cross_out, (b_big, b_small) = lax.optimization_barrier((cross_out, (b_big, b_small)))
+    cross_copy = lax.ppermute(cross_out, "section", [(1, 0)])
+    cross_out = [jnp.where(up, a, c) for a, c in zip(cross_out, cross_copy)]
 
     activations = jnp.where(
         up, jnp.concatenate(up_out, 0), jnp.concatenate(low_out, 0)
@@ -459,46 +520,29 @@
     back_grads = jnp.where(
         up, jnp.concatenate(up_grad, 0), jnp.concatenate(low_grad, 0)
     )[None]
-
-    def tree_sum(xs):
-        total = xs[0]
-        for v in xs[1:]:
-            total = jax.tree.map(jnp.add, total, v)
-        return total
-
-    up_sm = tree_sum(up_small)
-    low_sm = tree_sum(low_small)
-    ln1g = jax.tree.map(lambda a, b: jnp.where(up, a, b), up_sm[0], low_sm[0])
-    ln2g = jax.tree.map(lambda a, b: jnp.where(up, a, b), up_sm[1], low_sm[1])
-    lncg = up_sm[2]
-    lw = jax.tree.map(lambda a, b: jnp.where(up, a, b), up_w, low_w)
-    d_wqkv, d_wout, d_wup, d_bup, d_wdown, d_bdown = lw
-
-    def rs(a, dim=0):
-        return lax.psum_scatter(a, "dp", scatter_dimension=dim, tiled=True)
-
-    def rs_cross(a):
-        return lax.psum(jnp.where(up, rs(a), 0.0), "section")
+    big = [jnp.where(up, a, b)[None] for a, b in zip(a_big, b_big)]
+    small = [jnp.where(up, a, b) for a, b in zip(a_small[:6], b_small)]
+    d_wq, d_wo, d_wkv_sh, lnc_g, lnc_b = cross_out
 
     return (
         activations,
         back_grads,
         image_grad,
-        rs(ln1g[0])[None],
-        rs(ln1g[1])[None],
-        rs(d_wqkv)[None],
-        rs(d_wout)[None],
-        rs(ln2g[0])[None],
-        rs(ln2g[1])[None],
-        rs(d_wup)[None],
-        rs(d_bup)[None],
-        rs(d_wdown)[None],
-        rs(d_bdown)[None],
-        rs_cross(lncg[0]),
-        rs_cross(lncg[1]),
-        rs_cross(cross_w[0]),
-        rs_cross(d_wkv),
-        rs_cross(cross_w[1]),
+        small[0],
+        small[1],
+        big[0],
+        big[1],
+        small[2],
+        small[3],
+        big[2],
+        small[4],
+        big[3],
+        small[5],
+        lnc_g[0],
+        lnc_b[0],
+        d_wq,
+        d_wkv_sh,
+        d_wo,
     )
 
 

time: 1590 us -> 1800 us (1.13)
  waiting for transfers between devices: 890 us -> 1100 us
  blocking collectives: 96.5 us -> 129 us
    reduce_scatter x7 -> x11, waiting for transfers between devices: 300 us -> 576 us  [rs(): return lax.psum_scatter(a, 'dp', scatter_dimension=dim, tiled=True)]
    ppermute x2, waiting for transfers between devices: 548 us -> 457 us  [per_device(): returned.append(lax.ppermute(bf(dh), 'section', [(1, 0)]))]
    unnamed x1 -> x2, blocking collectives: 74.9 us -> 129 us
    select_n x13 -> x7, other arithmetic: 29.5 us -> 4.23 us  [the longest x4 2.12 us: per_device(): small = [jnp.where(up, a, b) for a, b in zip(a_small[:6], b_small)]]
    psum x1 -> x0, blocking collectives: 21.6 us -> none  [rs_cross(): return lax.psum(jnp.where(up, rs(a), 0.0), 'section')]
    ppermute x1, waiting for transfers between devices: 0.01 us -> 21 us  [per_device(): ig_first = lax.ppermute(image_grad_full[:half], 'section', [(1, 0)])]
    another operation x89 -> x88, local copies, waits for them, and re-layouts: 108 us -> 101 us
  transfers between devices with their start and end apart: 18 -> 26, of which waited for: 8 -> 16; matrix products, arithmetic and copies ran while one was open for 29% -> 14% of each run, Pallas kernels for 0% -> 0%
where the time goes in v3:
time: 1800 us; the launch traced here: 1790 us
  waiting for transfers between devices  1100 us (61%)
  local copies, waits for them, and re-layouts  201 us (11%)
  matrix products  189 us (10%)
  blocking collectives  129 us (7%)
  other arithmetic  106 us (6%)
  loops' own time  32 us (2%)
  starting transfers between devices  25.1 us (1%)
    reduce_scatter x11, waiting for transfers between devices, rs(): return lax.psum_scatter(a, 'dp', scatter_dimension=dim, tiled=True)  576 us
    ppermute x2, waiting for transfers between devices, per_device(): returned.append(lax.ppermute(bf(dh), 'section', [(1, 0)]))  457 us
    unnamed x2, blocking collectives  129 us
    another operation x88, local copies, waits for them, and re-layouts  101 us
    dot_general x8, matrix products, mm_t(): return jnp.einsum('...e,de->...d', g, w, preferred_element_type=F32)  68.1 us
    dot_general x8, matrix products, mm(): return jnp.einsum('...d,de->...e', a, w, preferred_element_type=F32)  62.5 us
    convert_element_type x16, other arithmetic, bf(): return x.astype(BF16)  39.2 us
  transfers between devices with their start and end apart: 26, of which 16 were waited for; matrix products, arithmetic and copies ran while one was open for 14% of the time, Pallas kernels for 0%

profile of v3, /device:TPU:0, one launch (start us, length us, event | category | flops | bytes accessed | tf_op | source)
XLA Modules:
  0.0 1794.5 jit_solution(488093397925257755)
XLA Ops:
  32.8 67.4 %conditional.12 = (f32[8,64,768]{2,1,0:T(8,128)}, bf16[8,64,12,64]{3,1,2,0:T(8,128)(2,1)}, bf16[8,64,768]{2,1,0:T(8,128)(2,1)}, f32[8,64,768]{2,1,0:T(8,128)}, f...) conditional(s32[]{:T(128)} %convert_element_type.349, ...), branch_computations={%region_0.0_spmd, %region_1.8_spmd} | conditional | flops 7464489984 | bytes 124480776 | solution.py:31
  105.1 66.7 %conditional.13 = (f32[8,64,768]{2,1,0:T(8,128)}, bf16[8,64,12,64]{3,1,2,0:T(8,128)(2,1)S(1)}, bf16[8,64,768]{2,1,0:T(8,128)(2,1)}, f32[8,64,768]{2,1,0:T(8,128)...) conditional(s32[]{:T(128)} %convert_element_type.349, ...), branch_computations={%region_8.9_spmd, %region_9.16_spmd} | conditional | flops 7464489984 | bytes 118189384 | solution.py:31
  187.1 29.1 %conditional.15 = (f32[8,64,768]{2,1,0:T(8,128)}, bf16[8,64,12,64]{3,1,2,0:T(8,128)(2,1)}, bf16[8,64,768]{2,1,0:T(8,128)(2,1)}, f32[8,64,768]{2,1,0:T(8,128)}, f...) conditional(s32[]{:T(128)} %convert_element_type.352, ...), branch_computations={%region_19.20_spmd, %region_20.29_spmd} | conditional | flops 10490288128 | bytes 124310992 | solution.py:31
  216.3 23.6 %conditional.17 = (f32[8,64,768]{2,1,0:T(8,128)}, f32[768]{0:T(1024)S(1)}, f32[768]{0:T(1024)S(1)}, f32[768]{0:T(1024)S(1)}, f32[768]{0:T(1024)S(1)}, /*index=5*...) conditional(s32[]{:T(128)} %convert_element_type.352, ...), branch_computations={%region_39.40_spmd, %region_40.54_spmd} | conditional | flops 13324111872 | bytes 152132064 | solution.py:31
  240.5 29.3 %conditional.16 = (bf16[8,64,12,64]{3,1,2,0:T(8,128)(2,1)}, bf16[8,64,768]{2,1,0:T(8,128)(2,1)}, f32[8,64,768]{2,1,0:T(8,128)}, f32[8,64,1]{1,0,2:T(8,128)S(1)},...) conditional(s32[]{:T(128)} %convert_element_type.352, ...), branch_computations={%region_29.30_spmd, %region_30.39_spmd} | conditional | flops 10490288128 | bytes 124311000 | solution.py:31
  269.9 26.9 %conditional.18 = (f32[8,64,768]{2,1,0:T(8,128)}, f32[768]{0:T(1024)S(1)}, f32[768]{0:T(1024)S(1)}, f32[768]{0:T(1024)S(1)}, f32[768]{0:T(1024)S(1)}, /*index=5*...) conditional(s32[]{:T(128)} %convert_element_type.352, ...), branch_computations={%region_54.55_spmd, %region_55.69_spmd} | conditional | flops 13324111872 | bytes 152132064 | solution.py:31
  323.9 19.8 %collective-permute-done.7 = bf16[576,1536]{1,0:T(8,128)(2,1)S(1)} collective-permute-done((bf16[576,1536]{1,0:T(8,128)(2,1)S(1)}, bf16[576,1536]{1,0:T(8,128)(2,1)S(1)}, u32[]{:S(2)}, u32[]{:S(2)}) %collective-permute-start.7) | collective-permute-done | bytes 1769504 | tf_op jit(solution)/shard_map/ppermute | solution.py:435
  363.0 71.1 %all-reduce = f32[16,528]{1,0:T(8,128)S(1)} all-reduce(f32[16,528]{1,0:T(8,128)S(1)} %concatenate.142), channel_id=6, replica_groups=mesh['section'=2,'dp'=16] {'dp'}, use_global_device_ids=true, to_apply=%region_77.78.clone | all-reduce | flops 8448 | bytes 67584
  436.8 447.5 %collective-permute-done.5 = bf16[8,64,768]{2,1,0:T(8,128)(2,1)} collective-permute-done((bf16[8,64,768]{2,1,0:T(8,128)(2,1)}, bf16[8,64,768]{2,1,0:T(8,128)(2,1)}, u32[]{:S(2)}, u32[]{:S(2)}) %collective-permute-start.5) | collective-permute-done | bytes 786464 | tf_op jit(solution)/shard_map/ppermute | solution.py:410
  898.8 45.6 %reduce-scatter.20.cloned.1.call-done = bf16[48,768]{1,0:T(8,128)(2,1)} async-done(((bf16[768,768]{1,0:T(8,128)(2,1)}), bf16[48,768]{1,0:T(8,128)(2,1)}) %reduce-scatter.20.cloned.1.call-update) | async-done | bytes 73744 | tf_op jit(solution)/shard_map/reduce_scatter | solution.py:456
  945.9 59.2 %reduce-scatter.22.cloned.1.call-done = bf16[48,768]{1,0:T(8,128)(2,1)} async-done(((bf16[768,768]{1,0:T(8,128)(2,1)}), bf16[48,768]{1,0:T(8,128)(2,1)}) %reduce-scatter.22.cloned.1.call-update) | async-done | bytes 73744 | tf_op jit(solution)/shard_map/reduce_scatter | solution.py:456
  1006.6 69.3 %reduce-scatter.12.cloned.1.call-done = bf16[48,2304]{1,0:T(8,128)(2,1)} async-done(((bf16[768,2304]{1,0:T(8,128)(2,1)}), bf16[48,2304]{1,0:T(8,128)(2,1)}) %reduce-scatter.12.cloned.1.call-update) | async-done | bytes 221200 | tf_op jit(solution)/shard_map/reduce_scatter | solution.py:456
  1077.6 63.7 %reduce-scatter.24.cloned.1.call-done = bf16[48,1536]{1,0:T(8,128)(2,1)} async-done(((bf16[768,1536]{1,0:T(8,128)(2,1)}), bf16[48,1536]{1,0:T(8,128)(2,1)}) %reduce-scatter.24.cloned.1.call-update) | async-done | bytes 147472 | tf_op jit(solution)/shard_map/reduce_scatter | solution.py:456
  1143.0 77.2 %reduce-scatter.16.cloned.1.call-done = bf16[48,3072]{1,0:T(8,128)(2,1)} async-done(((bf16[768,3072]{1,0:T(8,128)(2,1)}), bf16[48,3072]{1,0:T(8,128)(2,1)}) %reduce-scatter.16.cloned.1.call-update) | async-done | bytes 294928 | tf_op jit(solution)/shard_map/reduce_scatter | solution.py:456
  1222.0 76.7 %reduce-scatter.18.cloned.1.call-done = bf16[192,768]{1,0:T(8,128)(2,1)} async-done(((bf16[3072,768]{1,0:T(8,128)(2,1)}), bf16[192,768]{1,0:T(8,128)(2,1)}) %reduce-scatter.18.cloned.1.call-update) | async-done | bytes 294928 | tf_op jit(solution)/shard_map/reduce_scatter | solution.py:456
  1300.5 73.3 %conditional.21 = (f32[8,64,768]{2,1,0:T(8,128)}, f32[768]{0:T(1024)S(1)}, f32[768]{0:T(1024)S(1)}, f32[768]{0:T(1024)S(1)}, f32[768]{0:T(1024)S(1)}, /*index=5*...) conditional(s32[]{:T(128)} %convert_element_type.349, ...), branch_computations={%region_83.84_spmd, %region_84.94_spmd} | conditional | flops 7580408832 | bytes 107864288 | solution.py:31
  1302.9 19.3 %fusion.262 = bf16[8,64,3072]{2,1,0:T(8,128)(2,1)} fusion(f32[8,64,3072]{2,1,0:T(8,128)} %get-tuple-element.584, bf16[8,64,768]{2,1,0:T(8,128)(2,1)} %convert_element_type.294, bf16[3072,768]{1,0:T(8,128)(2,1)} %get-tuple-element.585), kind=kOutput, calls=%fused_computation.465 | convolution fusion | flops 2529165312 | bytes 14942208 | tf_op jit(solution)/shard_map/cond/branch_1_fun/...e,de->...d/dot_general | solution.py:62
  1373.9 71.5 %conditional.22 = (f32[768]{0:T(1024)S(1)}, f32[768]{0:T(1024)S(1)}, f32[768]{0:T(1024)S(1)}, f32[768]{0:T(1024)S(1)}, bf16[8,64,2304]{2,1,0:T(8,128)(2,1)}, /*i...) conditional(s32[]{:T(128)} %convert_element_type.349, ...), branch_computations={%region_94.95_spmd, %region_95.105_spmd} | conditional | flops 7580408832 | bytes 142467424 | solution.py:31
  1447.2 35.0 %conditional.23 = (bf16[768,2304]{1,0:T(8,128)(2,1)S(1)}, bf16[768,768]{1,0:T(8,128)(2,1)}, bf16[768,3072]{1,0:T(8,128)(2,1)}, f32[3072]{0:T(1024)S(1)}, bf16[3072,768]{1,0:T(8,128)(2,1)}, /*index=5*/f32[768]{0:T(1024)}) conditional(s32[]{:T(128)} %convert_element_type.349, () %tuple.148, (bf16[8,64,768]{2,1,0:T(8,128)(2,1)}, ...), branch_computations={%region_105.106_spmd, %region_106.109_spmd} | conditional | flops 14512025600 | bytes 62929968 | solution.py:31
  1488.0 21.0 %collective-permute-done.9 = f32[288,768]{1,0:T(8,128)S(1)} collective-permute-done((f32[288,768]{1,0:T(8,128)S(1)}, f32[288,768]{1,0:T(8,128)S(1)}, u32[]{:S(2)}, u32[]{:S(2)}) %collective-permute-start.9) | collective-permute-done | bytes 884768 | tf_op jit(solution)/shard_map/ppermute | solution.py:446
  1512.4 57.6 %all-reduce.1 = f32[16,432]{1,0:T(8,128)S(1)} all-reduce(f32[16,432]{1,0:T(8,128)S(1)} %concatenate.145), channel_id=14, replica_groups=mesh['section'=2,'dp'=16] {'dp'}, use_global_device_ids=true, to_apply=%region_113.114.clone | all-reduce | flops 6912 | bytes 55296
  1580.8 29.4 %reduce-scatter.26.cloned.1.call-done = bf16[48,2304]{1,0:T(8,128)(2,1)} async-done(((bf16[768,2304]{1,0:T(8,128)(2,1)}), bf16[48,2304]{1,0:T(8,128)(2,1)}) %reduce-scatter.26.cloned.1.call-update) | async-done | bytes 221200 | tf_op jit(solution)/shard_map/reduce_scatter | solution.py:456
  1611.2 77.7 %reduce-scatter.30.cloned.1.call-done = bf16[48,3072]{1,0:T(8,128)(2,1)} async-done(((bf16[768,3072]{1,0:T(8,128)(2,1)}), bf16[48,3072]{1,0:T(8,128)(2,1)}) %reduce-scatter.30.cloned.1.call-update) | async-done | bytes 294928 | tf_op jit(solution)/shard_map/reduce_scatter | solution.py:456
  1689.9 77.5 %reduce-scatter.32.cloned.1.call-done = bf16[192,768]{1,0:T(8,128)(2,1)} async-done(((bf16[3072,768]{1,0:T(8,128)(2,1)}), bf16[192,768]{1,0:T(8,128)(2,1)}) %reduce-scatter.32.cloned.1.call-update) | async-done | bytes 294928 | tf_op jit(solution)/shard_map/reduce_scatter | solution.py:456
  (543 shorter events, 554.4 us)
Async XLA Ops:
  7.2 889.9 %reduce-scatter.14.cloned.1.call-start = ((), (), s32[]{:S(2)}) async-start(), calls=%async_computation.12 | async-start | bytes 1253376 | tf_op jit(solution)/shard_map/reduce_scatter | solution.py:456
  7.2 14.6 collective-permute-start.2
  26.5 154.7 %collective-permute-start.3 = (bf16[576,1536]{1,0:T(8,128)(2,1)}, bf16[576,1536]{1,0:T(8,128)(2,1)}, u32[]{:S(2)}, u32[]{:S(2)}) collective-permute-start(bf16[576,1536]{1,0:T(8,128)(2,1)} %get-tuple-element.873), channel_id=1, source_target_pairs={{0,1},{1,2},{2,3},{3,4},{4,5},{5,6},{6,7},{7,8},{8,9},{9,10},{10,1... | collective-permute-start | bytes 5308424 | tf_op jit(solution)/shard_map/ppermute | solution.py:341
  26.5 154.6 %collective-permute-start.4 = (bf16[576,1536]{1,0:T(8,128)(2,1)}, bf16[576,1536]{1,0:T(8,128)(2,1)}, u32[]{:S(2)}, u32[]{:S(2)}) collective-permute-start(bf16[576,1536]{1,0:T(8,128)(2,1)} %get-tuple-element.873), channel_id=1, source_target_pairs={{1,0},{2,1},{3,2},{4,3},{5,4},{6,5},{7,6},{8,7},{9,8},{10,9},{11,1... | collective-permute-start | bytes 5308424 | tf_op jit(solution)/shard_map/ppermute | solution.py:342
  102.7 84.4 %collective-permute-start.1 = (bf16[8,64,768]{2,1,0:T(8,128)(2,1)}, bf16[8,64,768]{2,1,0:T(8,128)(2,1)}, u32[]{:S(2)}, u32[]{:S(2)}) collective-permute-start(bf16[8,64,768]{2,1,0:T(8,128)(2,1)} %convert_element_type.353), channel_id=1, source_target_pairs={{0,16},{1,17},{2,18},{3,19},{4,20},{5,21},{6,22},{7,23},{8,24},{9,... | collective-permute-start | bytes 2359304 | tf_op jit(solution)/shard_map/ppermute | solution.py:375
  174.8 65.1 %collective-permute-start = (bf16[8,64,768]{2,1,0:T(8,128)(2,1)}, bf16[8,64,768]{2,1,0:T(8,128)(2,1)}, u32[]{:S(2)}, u32[]{:S(2)}) collective-permute-start(bf16[8,64,768]{2,1,0:T(8,128)(2,1)} %convert_element_type.351), channel_id=1, source_target_pairs={{0,16},{1,17},{2,18},{3,19},{4,20},{5,21},{6,22},{7,23},{8,24},{9,... | collective-permute-start | bytes 2359304 | tf_op jit(solution)/shard_map/ppermute | solution.py:375
  313.1 631.2 %reduce-scatter.20.cloned.1.call-start = ((), (), s32[]{:S(2)}) async-start(), calls=%async_computation.15 | async-start | bytes 1253376 | tf_op jit(solution)/shard_map/reduce_scatter | solution.py:456
  313.9 691.2 %reduce-scatter.22.cloned.1.call-start = ((), (), s32[]{:S(2)}) async-start(), calls=%async_computation.16 | async-start | bytes 1253376 | tf_op jit(solution)/shard_map/reduce_scatter | solution.py:456
  314.6 761.3 %reduce-scatter.12.cloned.1.call-start = ((), (), s32[]{:S(2)}) async-start(), calls=%async_computation.11 | async-start | bytes 3760128 | tf_op jit(solution)/shard_map/reduce_scatter | solution.py:456
  315.2 826.2 %reduce-scatter.24.cloned.1.call-start = ((), (), s32[]{:S(2)}) async-start(), calls=%async_computation.17 | async-start | bytes 2506752 | tf_op jit(solution)/shard_map/reduce_scatter | solution.py:456
  323.3 20.3 %collective-permute-start.7 = (bf16[576,1536]{1,0:T(8,128)(2,1)S(1)}, bf16[576,1536]{1,0:T(8,128)(2,1)S(1)}, u32[]{:S(2)}, u32[]{:S(2)}) collective-permute-start(bf16[576,1536]{1,0:T(8,128)(2,1)S(1)} %get-tuple-element.1754), channel_id=1, source_target_pairs={{1,0},{2,1},{3,2},{4,3},{5,4},{6,5},{7,6},{8,7},{9,8},{10,9},{11,1... | collective-permute-start | bytes 5308424 | tf_op jit(solution)/shard_map/ppermute | solution.py:435
  323.6 24.8 %collective-permute-start.8 = (bf16[576,1536]{1,0:T(8,128)(2,1)S(1)}, bf16[576,1536]{1,0:T(8,128)(2,1)S(1)}, u32[]{:S(2)}, u32[]{:S(2)}) collective-permute-start(bf16[576,1536]{1,0:T(8,128)(2,1)S(1)} %get-tuple-element.1755), channel_id=1, source_target_pairs={{0,1},{1,2},{2,3},{3,4},{4,5},{5,6},{6,7},{7,8},{8,9},{9,10},{10,1... | collective-permute-start | bytes 5308424 | tf_op jit(solution)/shard_map/ppermute | solution.py:436
  352.1 868.1 %reduce-scatter.16.cloned.1.call-start = ((), (), s32[]{:S(2)}) async-start(), calls=%async_computation.13 | async-start | bytes 5013504 | tf_op jit(solution)/shard_map/reduce_scatter | solution.py:456
  352.6 946.0 %reduce-scatter.18.cloned.1.call-start = ((), (), s32[]{:S(2)}) async-start(), calls=%async_computation.14 | async-start | bytes 5013504 | tf_op jit(solution)/shard_map/reduce_scatter | solution.py:456
  353.5 1226.3 %reduce-scatter.28.cloned.1.call-start = ((), (), s32[]{:S(2)}) async-start(), calls=%async_computation.19 | async-start | bytes 1253376 | tf_op jit(solution)/shard_map/reduce_scatter | solution.py:456
  358.5 525.7 %collective-permute-start.5 = (bf16[8,64,768]{2,1,0:T(8,128)(2,1)}, bf16[8,64,768]{2,1,0:T(8,128)(2,1)}, u32[]{:S(2)}, u32[]{:S(2)}) collective-permute-start(bf16[8,64,768]{2,1,0:T(8,128)(2,1)} %convert_element_type.356), channel_id=1, source_target_pairs={{16,0},{17,1},{18,2},{19,3},{20,4},{21,5},{22,6},{23,7},{24,8},{25... | collective-permute-start | bytes 2359304 | tf_op jit(solution)/shard_map/ppermute | solution.py:410
  359.8 533.7 %collective-permute-start.6 = (bf16[8,64,768]{2,1,0:T(8,128)(2,1)}, bf16[8,64,768]{2,1,0:T(8,128)(2,1)}, u32[]{:S(2)}, u32[]{:S(2)}) collective-permute-start(bf16[8,64,768]{2,1,0:T(8,128)(2,1)} %convert_element_type.358), channel_id=1, source_target_pairs={{16,0},{17,1},{18,2},{19,3},{20,4},{21,5},{22,6},{23,7},{24,8},{25... | collective-permute-start | bytes 2359304 | tf_op jit(solution)/shard_map/ppermute | solution.py:410
  1482.3 127.9 %reduce-scatter.26.cloned.1.call-start = ((), (), s32[]{:S(2)}) async-start(), calls=%async_computation.18 | async-start | bytes 3760128 | tf_op jit(solution)/shard_map/reduce_scatter | solution.py:456
  1484.1 204.8 %reduce-scatter.30.cloned.1.call-start = ((), (), s32[]{:S(2)}) async-start(), calls=%async_computation.20 | async-start | bytes 5013504 | tf_op jit(solution)/shard_map/reduce_scatter | solution.py:456
  1484.7 282.7 %reduce-scatter.32.cloned.1.call-start = ((), (), s32[]{:S(2)}) async-start(), calls=%async_computation.21 | async-start | bytes 5013504 | tf_op jit(solution)/shard_map/reduce_scatter | solution.py:456
  1486.7 22.3 %collective-permute-start.9 = (f32[288,768]{1,0:T(8,128)S(1)}, f32[288,768]{1,0:T(8,128)S(1)}, u32[]{:S(2)}, u32[]{:S(2)}) collective-permute-start(f32[288,768]{1,0:T(8,128)S(1)} %slice.161), channel_id=1, source_target_pairs={{16,0},{17,1},{18,2},{19,3},{20,4},{21,5},{22,6},{23,7},{24,8},{25... | collective-permute-start | bytes 2654216 | tf_op jit(solution)/shard_map/ppermute | solution.py:446
  1768.5 17.1 collective-permute-start.14
  1769.8 17.2 collective-permute-start.13
  1771.1 15.2 collective-permute-start.12
  (110 other events, 5275.9 us)
Sparse Core Ops, SparseCore 0:
  313.2 570.2 reduce-scatter.13
  887.1 57.1 reduce-scatter.19
  948.0 57.0 reduce-scatter.21
  1008.8 67.0 reduce-scatter.11
  1079.5 61.7 reduce-scatter.23
  1145.6 74.5 reduce-scatter.15
  1224.0 74.5 reduce-scatter.17
  1482.4 56.2 reduce-scatter.27
  1543.1 67.0 reduce-scatter.25
  1614.4 74.3 reduce-scatter.29
  1692.7 74.5 reduce-scatter.31

commit v4 on v3

--- a/solution.py
+++ b/solution.py
@@ -296,7 +296,93 @@
     return gout + dx, (d_gain, d_bias), pairs
 
 
+def chip_cycle(mesh):
+    n_dp = mesh.shape["dp"]
+    plane = mesh.devices.reshape(-1, n_dp)[0]
+    try:
+        chips = {}
+        for i, dev in enumerate(plane):
+            chips.setdefault(tuple(dev.coords), []).append(i)
+    except AttributeError:
+        return list(range(n_dp))
+    keys = sorted(chips)
+    if len(keys) < 3:
+        return [i for k in keys for i in sorted(chips[k])]
+    near = {
+        k: [j for j in keys if sum(abs(a - b) for a, b in zip(k, j)) == 1] for k in keys
+    }
+    path, seen, budget = [keys[0]], {keys[0]}, [200000]
+
+    def walk():
+        budget[0] -= 1
+        if budget[0] < 0:
+            return False
+        if len(path) == len(keys):
+            return keys[0] in near[path[-1]]
+        options = sorted(
+            (j for j in near[path[-1]] if j not in seen),
+            key=lambda j: sum(1 for n in near[j] if n not in seen),
+        )
+        for j in options:
+            path.append(j)
+            seen.add(j)
+            if walk():
+                return True
+            path.pop()
+            seen.discard(j)
+        return False
+
+    if not walk():
+        return list(range(n_dp))
+    return [i for k in path for i in sorted(chips[k])]
+
+
+def ring_reduce_scatter(packed, plane, cycle, dp_index):
+    n = len(cycle)
+    n_dp = packed.shape[0]
+    axes = ("section", "dp")
+    fwd = [(plane * n_dp + cycle[i], plane * n_dp + cycle[(i + 1) % n]) for i in range(n)]
+    bwd = [(b, a) for a, b in fwd]
+    where_in = [0] * n
+    for i, d in enumerate(cycle):
+        where_in[d] = i
+    rows = packed[jnp.array(cycle, jnp.int32)]
+    half = rows.shape[1] // 2
+    cw, ccw = rows[:, :half], rows[:, half:]
+    p = jnp.array(where_in, jnp.int32)[dp_index]
+
+    def take(a, idx):
+        return lax.dynamic_index_in_dim(a, idx % n, 0, keepdims=False)
+
+    send_c, send_w = take(cw, p - 1), take(ccw, p + 1)
+    for step in range(n - 1):
+        got_c = lax.ppermute(send_c, axes, fwd)
+        got_w = lax.ppermute(send_w, axes, bwd)
+        acc_c = got_c.astype(F32) + take(cw, p - step - 2).astype(F32)
+        acc_w = got_w.astype(F32) + take(ccw, p + step + 2).astype(F32)
+        send_c, send_w = bf(acc_c), bf(acc_w)
+    return jnp.concatenate([acc_c, acc_w], 0)
+
+
+def pack_rows(arrays, n):
+    flat = [bf(a).reshape(n, -1) for a in arrays]
+    width = sum(f.shape[1] for f in flat)
+    if width % 2:
+        flat.append(jnp.zeros((n, 1), BF16))
+    return jnp.concatenate(flat, 1)
+
+
+def unpack_row(row, arrays, n):
+    out, at = [], 0
+    for a in arrays:
+        size = a.size // n
+        out.append(row[at : at + size].reshape((a.shape[0] // n,) + a.shape[1:]))
+        at += size
+    return out
+
+
 def per_device(
+    cycle,
     inputs,
     cotangent,
     images,
@@ -452,34 +538,13 @@
             total = jax.tree.map(jnp.add, total, v)
         return total
 
-    def rs(a, dim=0):
-        return lax.psum_scatter(a, "dp", scatter_dimension=dim, tiled=True)
-
-    def rs_bf(a, dim=0):
-        return rs(bf(a), dim).astype(F32)
-
-    def pack(vs):
-        return jnp.concatenate([v.reshape(n_dp, -1) for v in vs], 1)
-
-    def unpack(row, vs):
-        out, at = [], 0
-        for v in vs:
-            width = v.size // n_dp
-            out.append(row[:, at : at + width])
-            at += width
-        return out
-
-    def reduce_layer(lw, sm):
+    def layer_list(lw, sm):
         d_wqkv, d_wout, d_wup, d_bup, d_wdown, d_bdown = lw
-        big = [rs_bf(d_wqkv), rs_bf(d_wout), rs_bf(d_wup), rs_bf(d_wdown)]
-        vecs = [sm[0][0], sm[0][1], sm[1][0], sm[1][1], d_bup, d_bdown]
-        return big, vecs
+        return [d_wqkv, d_wout, d_wup, d_wdown, sm[0][0], sm[0][1], sm[1][0], sm[1][1], d_bup, d_bdown]
 
     up_sm = tree_sum(up_small)
-    a_big, a_vecs = reduce_layer(up_w, up_sm)
-    a_cross = [rs_bf(cross_w[0]), rs_bf(cross_w[1]), rs_bf(d_wkv)]
-    a_vecs = a_vecs + [up_sm[2][0], up_sm[2][1]]
-    a_small = unpack(rs(pack(a_vecs)), a_vecs)
+    a_list = layer_list(up_w, up_sm) + [cross_w[0], cross_w[1], d_wkv, up_sm[2][0], up_sm[2][1]]
+    a_row = ring_reduce_scatter(pack_rows(a_list, n_dp), 1, cycle, dp_index)
 
     def lower_bwd(gout, saved):
         s_self, s_ffn = saved
@@ -491,9 +556,7 @@
     for m in range(MICRO):
         gout = chunk(cot, m) + returned[m].astype(F32)
         if m == 0:
-            gout, (a_big, a_small, a_cross) = lax.optimization_barrier(
-                (gout, (a_big, a_small, a_cross))
-            )
+            gout, a_row = lax.optimization_barrier((gout, a_row))
         else:
             gout, low_grad[-1] = lax.optimization_barrier((gout, low_grad[-1]))
         dh, small, pairs = run_on(low, lower_bwd, gout, low_saved[m])
@@ -503,14 +566,12 @@
 
     low_w = run_on(low, layer_weight_grads, low_pairs)
     low_sm = tree_sum(low_small)
-    low_w, low_sm, (a_big, a_small, a_cross) = lax.optimization_barrier(
-        (low_w, low_sm, (a_big, a_small, a_cross))
-    )
-    b_big, b_vecs = reduce_layer(low_w, low_sm)
-    b_small = unpack(rs(pack(b_vecs)), b_vecs)
-
-    cross_out = a_cross + a_small[6:]
-    cross_out, (b_big, b_small) = lax.optimization_barrier((cross_out, (b_big, b_small)))
+    b_list = layer_list(low_w, low_sm)
+    b_row = ring_reduce_scatter(pack_rows(b_list, n_dp), 0, cycle, dp_index)
+    a_got = unpack_row(a_row, a_list, n_dp)
+    b_got = unpack_row(b_row, b_list, n_dp)
+
+    cross_out = a_got[10:]
     cross_copy = lax.ppermute(cross_out, "section", [(1, 0)])
     cross_out = [jnp.where(up, a, c) for a, c in zip(cross_out, cross_copy)]
 
@@ -520,8 +581,8 @@
     back_grads = jnp.where(
         up, jnp.concatenate(up_grad, 0), jnp.concatenate(low_grad, 0)
     )[None]
-    big = [jnp.where(up, a, b)[None] for a, b in zip(a_big, b_big)]
-    small = [jnp.where(up, a, b) for a, b in zip(a_small[:6], b_small)]
+    layer = [jnp.where(up, a, b)[None] for a, b in zip(a_got[:10], b_got)]
+    big, small = layer[:4], [v.reshape(1, -1) for v in layer[4:]]
     d_wq, d_wo, d_wkv_sh, lnc_g, lnc_b = cross_out
 
     return (
@@ -538,8 +599,8 @@
         small[4],
         big[3],
         small[5],
-        lnc_g[0],
-        lnc_b[0],
+        lnc_g,
+        lnc_b,
         d_wq,
         d_wkv_sh,
         d_wo,
@@ -571,7 +632,7 @@
         P(),
     )
     return jax.shard_map(
-        per_device,
+        partial(per_device, chip_cycle(mesh)),
         mesh=mesh,
         in_specs=placed,
         out_specs=(

time: 1800 us -> 1860 us (1.033)
  waiting for transfers between devices: 1100 us -> 577 us
  other arithmetic: 106 us -> 486 us
  local copies, waits for them, and re-layouts: 201 us -> 393 us
  blocking collectives: 129 us -> 0 us
  starting transfers between devices: 25.1 us -> 143 us
    reduce_scatter x11 -> x0, waiting for transfers between devices: 576 us -> none  [rs(): return lax.psum_scatter(a, 'dp', scatter_dimension=dim, tiled=True)]
    convert_element_type x11 -> x6, other arithmetic: 15.8 us -> 314 us  [the longest x4 176 us: ring_reduce_scatter(): acc_c = got_c.astype(F32) + take(cw, p - step - 2).astype(F32)]
    unnamed x2 -> x0, blocking collectives: 129 us -> none
    ppermute x0 -> x60, starting transfers between devices: none -> 118 us  [the longest x30 74.6 us: ring_reduce_scatter(): got_w = lax.ppermute(send_w, axes, bwd)]
    gather x0 -> x12, local copies, waits for them, and re-layouts: none -> 94.6 us  [ring_reduce_scatter(): rows = packed[jnp.array(cycle, jnp.int32)]]
    ppermute x0 -> x60, waiting for transfers between devices: none -> 52.7 us  [the longest x30 26.8 us: ring_reduce_scatter(): got_c = lax.ppermute(send_c, axes, fwd)]
    unnamed x0 -> x2, other arithmetic: none -> 37 us
    ppermute x5, waiting for transfers between devices: 4.12 us -> 40 us  [per_device(): cross_copy = lax.ppermute(cross_out, 'section', [(1, 0)])]
  transfers between devices with their start and end apart: 26 -> 75, of which waited for: 16 -> 31; matrix products, arithmetic and copies ran while one was open for 14% -> 26% of each run, Pallas kernels for 0% -> 0%
where the time goes in v4:
time: 1860 us; the launch traced here: 1850 us
  waiting for transfers between devices  577 us (31%)
  other arithmetic  486 us (26%)
  local copies, waits for them, and re-layouts  393 us (21%)
  matrix products  192 us (10%)
  starting transfers between devices  143 us (8%)
  loops' own time  29 us (2%)
  between operations  24.8 us (1%)
    ppermute x2, waiting for transfers between devices, per_device(): returned.append(lax.ppermute(bf(dh), 'section', [(1, 0)]))  475 us
    convert_element_type x4, other arithmetic, ring_reduce_scatter(): acc_c = got_c.astype(F32) + take(cw, p - step - 2).astype(F32)  176 us
    convert_element_type x2, other arithmetic, ring_reduce_scatter(): acc_w = got_w.astype(F32) + take(ccw, p + step + 2).astype(F32)  138 us
    gather x12, local copies, waits for them, and re-layouts, ring_reduce_scatter(): rows = packed[jnp.array(cycle, jnp.int32)]  94.6 us
    another operation x81, local copies, waits for them, and re-layouts  91.8 us
    ppermute x30, starting transfers between devices, ring_reduce_scatter(): got_w = lax.ppermute(send_w, axes, bwd)  74.6 us
    dot_general x8, matrix products, mm_t(): return jnp.einsum('...e,de->...d', g, w, preferred_element_type=F32)  68.2 us
    dot_general x8, matrix products, mm(): return jnp.einsum('...d,de->...e', a, w, preferred_element_type=F32)  62.4 us
  transfers between devices with their start and end apart: 75, of which 31 were waited for; matrix products, arithmetic and copies ran while one was open for 26% of the time, Pallas kernels for 0%

profile of v4, /device:TPU:0, one launch (start us, length us, event | category | flops | bytes accessed | tf_op | source)
XLA Modules:
  0.0 1845.2 jit_solution(12086114281599319910)
XLA Ops:
  26.3 67.8 %conditional.12 = (f32[8,64,768]{2,1,0:T(8,128)}, bf16[8,64,12,64]{3,1,2,0:T(8,128)(2,1)}, bf16[8,64,768]{2,1,0:T(8,128)(2,1)}, f32[8,64,768]{2,1,0:T(8,128)}, f...) conditional(s32[]{:T(128)} %convert_element_type.1093, ...), branch_computations={%region_0.0_spmd, %region_1.8_spmd} | conditional | flops 7464489984 | bytes 124480776 | solution.py:31
  68.3 18.6 %fusion.85 = (bf16[8,64,3072]{2,1,0:T(8,128)(2,1)}, f32[8,64,3072]{2,1,0:T(8,128)}) fusion(f32[3072]{0:T(1024)S(1)} %bitcast.549, bf16[8,64,768]{2,1,0:T(8,128)(2,1)} %get-tuple-element.1618, bf16[768,3072]{1,0:T(8,128)(2,1)} %get-tuple-element.446), kind=kOutput, calls=%fused_computation.99 | convolution fusion | flops 2519728128 | bytes 14954496 | tf_op jit(solution)/shard_map/cond/branch_1_fun/...d,de->...e/dot_general | solution.py:58
  99.0 66.4 %conditional.13 = (f32[8,64,768]{2,1,0:T(8,128)}, bf16[8,64,12,64]{3,1,2,0:T(8,128)(2,1)S(1)}, bf16[8,64,768]{2,1,0:T(8,128)(2,1)}, f32[8,64,768]{2,1,0:T(8,128)...) conditional(s32[]{:T(128)} %convert_element_type.1093, ...), branch_computations={%region_8.9_spmd, %region_9.16_spmd} | conditional | flops 7464489984 | bytes 118189384 | solution.py:31
  139.4 18.5 %fusion.116 = (bf16[8,64,3072]{2,1,0:T(8,128)(2,1)}, f32[8,64,3072]{2,1,0:T(8,128)}) fusion(f32[3072]{0:T(1024)S(1)} %bitcast.550, bf16[8,64,768]{2,1,0:T(8,128)(2,1)} %get-tuple-element.1646, bf16[768,3072]{1,0:T(8,128)(2,1)} %get-tuple-element.458), kind=kOutput, calls=%fused_computation.157 | convolution fusion | flops 2519728128 | bytes 14954496 | tf_op jit(solution)/shard_map/cond/branch_1_fun/...d,de->...e/dot_general | solution.py:58
  204.7 29.4 %conditional.15 = (f32[8,64,768]{2,1,0:T(8,128)}, bf16[8,64,12,64]{3,1,2,0:T(8,128)(2,1)}, bf16[8,64,768]{2,1,0:T(8,128)(2,1)}, f32[8,64,768]{2,1,0:T(8,128)}, f...) conditional(s32[]{:T(128)} %convert_element_type.1096, ...), branch_computations={%region_19.20_spmd, %region_20.29_spmd} | conditional | flops 10490288128 | bytes 124310992 | solution.py:31
  234.1 23.9 %conditional.17 = (f32[8,64,768]{2,1,0:T(8,128)}, f32[768]{0:T(1024)S(1)}, f32[768]{0:T(1024)S(1)}, f32[768]{0:T(1024)S(1)}, f32[768]{0:T(1024)S(1)}, /*index=5*...) conditional(s32[]{:T(128)} %convert_element_type.1096, ...), branch_computations={%region_39.40_spmd, %region_40.54_spmd} | conditional | flops 13324111872 | bytes 152132064 | solution.py:31
  260.5 29.1 %conditional.16 = (bf16[8,64,12,64]{3,1,2,0:T(8,128)(2,1)}, bf16[8,64,768]{2,1,0:T(8,128)(2,1)}, f32[8,64,768]{2,1,0:T(8,128)}, f32[8,64,1]{1,0,2:T(8,128)S(1)},...) conditional(s32[]{:T(128)} %convert_element_type.1096, ...), branch_computations={%region_29.30_spmd, %region_30.39_spmd} | conditional | flops 10490288128 | bytes 124311000 | solution.py:31
  289.6 27.7 %conditional.18 = (f32[8,64,768]{2,1,0:T(8,128)}, f32[768]{0:T(1024)S(1)}, f32[768]{0:T(1024)S(1)}, f32[768]{0:T(1024)S(1)}, f32[768]{0:T(1024)S(1)}, /*index=5*...) conditional(s32[]{:T(128)} %convert_element_type.1096, ...), branch_computations={%region_54.55_spmd, %region_55.69_spmd} | conditional | flops 13324111872 | bytes 152132064 | solution.py:31
  425.6 458.8 %collective-permute-done.5 = bf16[8,64,768]{2,1,0:T(8,128)(2,1)} collective-permute-done((bf16[8,64,768]{2,1,0:T(8,128)(2,1)}, bf16[8,64,768]{2,1,0:T(8,128)(2,1)}, u32[]{:S(2)}, u32[]{:S(2)}) %collective-permute-start.5) | collective-permute-done | bytes 786464 | tf_op jit(solution)/shard_map/ppermute | solution.py:496
  884.4 16.2 collective-permute-done.6
  928.7 25.1 %pad_maximum_fusion.6 = (bf16[16,295176]{1,0:T(8,128)(2,1)S(1)}, bf16[16,295176]{1,0:T(8,128)(2,1)S(1)}) fusion(bf16[16,118144]{1,0:T(8,128)(2,1)} %gather_fusion.2, bf16[16,118144]{1,0:T(8,128)(2,1)} %gather_fusion.1, bf16[16,118144]{1,0:T(8,128)(2,1)} %gather_fusion, bf16[16,117776]{1,0:T(8,128)(2,1)} %gather_fusion.4, bf16[16,118144]{1,0:T(8,128)(2,1)} %gather_fusion.3), kind=kLoop, calls=%fused_computation.609 | loop fusion | flops 56673792 | bytes 37782528
  953.9 12.1 dynamic-slice_reduce_fusion.1
  984.2 77.7 %convert_reduce_fusion.31 = (f32[295176]{0:T(1024)}, f32[295176]{0:T(1024)S(1)}, f32[295176]{0:T(1024)}, f32[295176]{0:T(1024)}, f32[295176]{0:T(1024)}, /*index...) fusion(bf16[16,295176]{1,0:T(8,128)(2,1)} %copy-done.1, ...), kind=kLoop, calls=%fused_computation.692 | loop fusion | flops 4427640 | bytes 26565900 | tf_op jit(solution)/shard_map/convert_element_type | solution.py:361
  1061.9 78.3 %convert_reduce_fusion.16 = (f32[295176]{0:T(1024)}, f32[295176]{0:T(1024)S(1)}, f32[295176]{0:T(1024)}, f32[295176]{0:T(1024)}, f32[295176]{0:T(1024)}, /*index...) fusion(bf16[16,295176]{1,0:T(8,128)(2,1)} %copy-done, ...), kind=kLoop, calls=%fused_computation.677 | loop fusion | flops 4427640 | bytes 26565900 | tf_op jit(solution)/shard_map/convert_element_type | solution.py:362
  1176.4 72.1 %conditional.21 = (f32[8,64,768]{2,1,0:T(8,128)}, f32[768]{0:T(1024)S(1)}, f32[768]{0:T(1024)S(1)}, f32[768]{0:T(1024)S(1)}, f32[768]{0:T(1024)S(1)}, /*index=5*...) conditional(s32[]{:T(128)} %convert_element_type.1093, ...), branch_computations={%region_77.78_spmd, %region_78.88_spmd} | conditional | flops 7580408832 | bytes 114155768 | solution.py:31
  1177.6 19.4 %fusion.278 = bf16[8,64,3072]{2,1,0:T(8,128)(2,1)} fusion(f32[8,64,3072]{2,1,0:T(8,128)} %get-tuple-element.597, bf16[8,64,768]{2,1,0:T(8,128)(2,1)} %convert_element_type.812, bf16[3072,768]{1,0:T(8,128)(2,1)} %get-tuple-element.598), kind=kOutput, calls=%fused_computation.477 | convolution fusion | flops 2529165312 | bytes 14942208 | tf_op jit(solution)/shard_map/cond/branch_1_fun/...e,de->...d/dot_general | solution.py:62
  1249.1 71.7 %conditional.22 = (f32[768]{0:T(1024)S(1)}, f32[768]{0:T(1024)S(1)}, f32[768]{0:T(1024)S(1)}, f32[768]{0:T(1024)S(1)}, bf16[8,64,2304]{2,1,0:T(8,128)(2,1)}, /*i...) conditional(s32[]{:T(128)} %convert_element_type.1093, ...), branch_computations={%region_88.89_spmd, %region_89.99_spmd} | conditional | flops 7580408832 | bytes 142467424 | solution.py:31
  1251.5 18.3 fusion.303
  1321.5 53.5 %conditional.23 = (bf16[16,110592]{1,0:T(8,128)(2,1)S(1)}, bf16[16,36864]{1,0:T(8,128)(2,1)}, bf16[16,147456]{1,0:T(8,128)(2,1)}, bf16[16,192]{1,0:T(8,128)(2,1)...) conditional(s32[]{:T(128)} %convert_element_type.1093, () %tuple.172, ...), branch_computations={%region_99.100_spmd, %region_100.105_spmd} | conditional | flops 14519103488 | bytes 75551280 | solution.py:31
  1415.5 39.5 %convert_reduce_fusion.46 = (f32[221400]{0:T(1024)}, f32[221400]{0:T(1024)}, f32[221400]{0:T(1024)}, f32[221400]{0:T(1024)}, f32[221400]{0:T(1024)}, /*index=5*/f32[221400]{0:T(1024)}) fusion(s32[]{:T(128)S(6)} %select_n.657, bf16[16,110720]{1,0:T(8,128)(2,1)} %gather_fusion.6, bf16[16,110720]{1,0:T(8,128)(2,1)} %gather_fusion.5, s32[]{:T(128)S(6)} %select_n.659, ...), kind=kLoop, calls=%fused_computation.755 | loop fusion | flops 5313600 | bytes 12399704 | tf_op jit(solution)/shard_map/convert_element_type | solution.py:361
  1455.0 39.5 %convert_reduce_fusion.40 = (f32[221400]{0:T(1024)}, f32[221400]{0:T(1024)}, f32[221400]{0:T(1024)}, f32[221400]{0:T(1024)}, f32[221400]{0:T(1024)}, /*index=5*/f32[221400]{0:T(1024)}) fusion(s32[]{:T(128)S(6)} %select_n.669, bf16[16,110720]{1,0:T(8,128)(2,1)} %gather_fusion.6, bf16[16,110720]{1,0:T(8,128)(2,1)} %gather_fusion.5, s32[]{:T(128)S(6)} %select_n.671, ...), kind=kLoop, calls=%fused_computation.749 | loop fusion | flops 5313600 | bytes 12399704 | tf_op jit(solution)/shard_map/convert_element_type | solution.py:361
  1494.5 19.3 %convert_reduce_fusion.34 = (f32[221400]{0:T(1024)}, f32[221400]{0:T(1024)}, f32[221400]{0:T(1024)}) fusion(s32[]{:T(128)S(6)} %select_n.681, bf16[16,110720]{1,0:T(8,128)(2,1)} %gather_fusion.6, bf16[16,110720]{1,0:T(8,128)(2,1)} %gather_fusion.5, s32[]{:T(128)S(6)} %select_n.683, s32[]{:T(128)S(6)} %select_n.685), kind=kLoop, calls=%fused_computation.743 | loop fusion | flops 2656800 | bytes 9742892 | tf_op jit(solution)/shard_map/convert_element_type | solution.py:361
  1551.7 59.3 %convert_reduce_fusion.61 = (f32[221400]{0:T(1024)}, f32[221400]{0:T(1024)S(1)}, f32[221400]{0:T(1024)}, f32[221400]{0:T(1024)}, f32[221400]{0:T(1024)}, /*index...) fusion(bf16[16,221400]{1,0:T(8,128)(2,1)} %pad_maximum_fusion.8, ...), kind=kLoop, calls=%fused_computation.770 | loop fusion | flops 3321000 | bytes 19926060 | tf_op jit(solution)/shard_map/convert_element_type | solution.py:362
  1639.5 40.0 %collective-permute-done.73 = f32[48,1536]{1,0:T(8,128)S(1)} collective-permute-done((f32[48,1536]{1,0:T(8,128)S(1)}, f32[48,1536]{1,0:T(8,128)S(1)}, u32[]{:S(2)}, u32[]{:S(2)}) %collective-permute-start.73) | collective-permute-done | bytes 294944 | tf_op jit(solution)/shard_map/ppermute | solution.py:575
  (820 shorter events, 866.2 us)
Async XLA Ops:
  0.7 14.6 collective-permute-start.2
  20.0 178.8 %collective-permute-start.3 = (bf16[576,1536]{1,0:T(8,128)(2,1)}, bf16[576,1536]{1,0:T(8,128)(2,1)}, u32[]{:S(2)}, u32[]{:S(2)}) collective-permute-start(bf16[576,1536]{1,0:T(8,128)(2,1)} %get-tuple-element.832), channel_id=1, source_target_pairs={{0,1},{1,2},{2,3},{3,4},{4,5},{5,6},{6,7},{7,8},{8,9},{9,10},{10,1... | collective-permute-start | bytes 5308424 | tf_op jit(solution)/shard_map/ppermute | solution.py:427
  20.0 178.7 %collective-permute-start.4 = (bf16[576,1536]{1,0:T(8,128)(2,1)}, bf16[576,1536]{1,0:T(8,128)(2,1)}, u32[]{:S(2)}, u32[]{:S(2)}) collective-permute-start(bf16[576,1536]{1,0:T(8,128)(2,1)} %get-tuple-element.832), channel_id=1, source_target_pairs={{1,0},{2,1},{3,2},{4,3},{5,4},{6,5},{7,6},{8,7},{9,8},{10,9},{11,1... | collective-permute-start | bytes 5308424 | tf_op jit(solution)/shard_map/ppermute | solution.py:428
  96.6 108.0 %collective-permute-start.1 = (bf16[8,64,768]{2,1,0:T(8,128)(2,1)}, bf16[8,64,768]{2,1,0:T(8,128)(2,1)}, u32[]{:S(2)}, u32[]{:S(2)}) collective-permute-start(bf16[8,64,768]{2,1,0:T(8,128)(2,1)} %convert_element_type.1097), channel_id=1, source_target_pairs={{0,16},{1,17},{2,18},{3,19},{4,20},{5,21},{6,22},{7,23},{8,24},{9,... | collective-permute-start | bytes 2359304 | tf_op jit(solution)/shard_map/ppermute | solution.py:461
  168.4 92.1 %collective-permute-start = (bf16[8,64,768]{2,1,0:T(8,128)(2,1)}, bf16[8,64,768]{2,1,0:T(8,128)(2,1)}, u32[]{:S(2)}, u32[]{:S(2)}) collective-permute-start(bf16[8,64,768]{2,1,0:T(8,128)(2,1)} %convert_element_type.1095), channel_id=1, source_target_pairs={{0,16},{1,17},{2,18},{3,19},{4,20},{5,21},{6,22},{7,23},{8,24},{9,... | collective-permute-start | bytes 2359304 | tf_op jit(solution)/shard_map/ppermute | solution.py:461
  344.5 559.6 %collective-permute-start.7 = (bf16[576,1536]{1,0:T(8,128)(2,1)}, bf16[576,1536]{1,0:T(8,128)(2,1)}, u32[]{:S(2)}, u32[]{:S(2)}) collective-permute-start(bf16[576,1536]{1,0:T(8,128)(2,1)} %get-tuple-element.1551), channel_id=1, source_target_pairs={{1,0},{2,1},{3,2},{4,3},{5,4},{6,5},{7,6},{8,7},{9,8},{10,9},{11,1... | collective-permute-start | bytes 5308424 | tf_op jit(solution)/shard_map/ppermute | solution.py:521
  344.8 559.3 %collective-permute-start.8 = (bf16[576,1536]{1,0:T(8,128)(2,1)}, bf16[576,1536]{1,0:T(8,128)(2,1)}, u32[]{:S(2)}, u32[]{:S(2)}) collective-permute-start(bf16[576,1536]{1,0:T(8,128)(2,1)} %get-tuple-element.1552), channel_id=1, source_target_pairs={{0,1},{1,2},{2,3},{3,4},{4,5},{5,6},{6,7},{7,8},{8,9},{9,10},{10,1... | collective-permute-start | bytes 5308424 | tf_op jit(solution)/shard_map/ppermute | solution.py:522
  349.8 534.6 %collective-permute-start.5 = (bf16[8,64,768]{2,1,0:T(8,128)(2,1)}, bf16[8,64,768]{2,1,0:T(8,128)(2,1)}, u32[]{:S(2)}, u32[]{:S(2)}) collective-permute-start(bf16[8,64,768]{2,1,0:T(8,128)(2,1)} %convert_element_type.1100), channel_id=1, source_target_pairs={{16,0},{17,1},{18,2},{19,3},{20,4},{21,5},{22,6},{23,7},{24,8},{25... | collective-permute-start | bytes 2359304 | tf_op jit(solution)/shard_map/ppermute | solution.py:496
  351.1 549.5 %collective-permute-start.6 = (bf16[8,64,768]{2,1,0:T(8,128)(2,1)}, bf16[8,64,768]{2,1,0:T(8,128)(2,1)}, u32[]{:S(2)}, u32[]{:S(2)}) collective-permute-start(bf16[8,64,768]{2,1,0:T(8,128)(2,1)} %convert_element_type.1102), channel_id=1, source_target_pairs={{16,0},{17,1},{18,2},{19,3},{20,4},{21,5},{22,6},{23,7},{24,8},{25... | collective-permute-start | bytes 2359304 | tf_op jit(solution)/shard_map/ppermute | solution.py:496
  966.0 174.3 %collective-permute-start.9 = (bf16[295176]{0:T(1024)(128)(2,1)}, bf16[295176]{0:T(1024)(128)(2,1)}, u32[]{:S(2)}, u32[]{:S(2)}) collective-permute-start(bf16[295176]{0:T(1024)(128)(2,1)} %dynamic-slice_reduce_fusion.1), channel_id=1, source_target_pairs={{16,17},{17,18},{18,19},{19,22},{22,23},{23,26},{26,27},{27,30},{3... | collective-permute-start | bytes 1771064 | tf_op jit(solution)/shard_map/ppermute | solution.py:359
  979.3 163.3 %collective-permute-start.24 = (bf16[295176]{0:T(1024)(128)(2,1)}, bf16[295176]{0:T(1024)(128)(2,1)}, u32[]{:S(2)}, u32[]{:S(2)}) collective-permute-start(bf16[295176]{0:T(1024)(128)(2,1)} %dynamic-slice_reduce_fusion), channel_id=1, source_target_pairs={{17,16},{18,17},{19,18},{22,19},{23,22},{26,23},{27,26},{30,27},{3... | collective-permute-start | bytes 1771064 | tf_op jit(solution)/shard_map/ppermute | solution.py:360
  982.9 161.9 %collective-permute-start.39 = (f32[288,768]{1,0:T(8,128)}, f32[288,768]{1,0:T(8,128)}, u32[]{:S(2)}, u32[]{:S(2)}) collective-permute-start(f32[288,768]{1,0:T(8,128)} %slice.200), channel_id=1, source_target_pairs={{16,0},{17,1},{18,2},{19,3},{20,4},{21,5},{22,6},{23,7},{24,8},{25... | collective-permute-start | bytes 2654216 | tf_op jit(solution)/shard_map/ppermute | solution.py:532
  1622.6 57.6 %collective-permute-start.55 = (bf16[221400]{0:T(1024)(128)(2,1)}, bf16[221400]{0:T(1024)(128)(2,1)}, u32[]{:S(2)}, u32[]{:S(2)}) collective-permute-start(bf16[221400]{0:T(1024)(128)(2,1)} %fusion.342), channel_id=1, source_target_pairs={{0,1},{1,2},{2,3},{3,6},{6,7},{7,10},{10,11},{11,14},{14,15},{15,1... | collective-permute-start | bytes 1328408 | tf_op jit(solution)/shard_map/ppermute | solution.py:359
  1625.5 54.0 %collective-permute-start.73 = (f32[48,1536]{1,0:T(8,128)S(1)}, f32[48,1536]{1,0:T(8,128)S(1)}, u32[]{:S(2)}, u32[]{:S(2)}) collective-permute-start(f32[48,1536]{1,0:T(8,128)S(1)} %reshape.1137), channel_id=1, source_target_pairs={{16,0},{17,1},{18,2},{19,3},{20,4},{21,5},{22,6},{23,7},{24,8},{25... | collective-permute-start | bytes 884744 | tf_op jit(solution)/shard_map/ppermute | solution.py:575
  1626.8 56.6 %collective-permute-start.40 = (bf16[221400]{0:T(1024)(128)(2,1)}, bf16[221400]{0:T(1024)(128)(2,1)S(1)}, u32[]{:S(2)}, u32[]{:S(2)}) collective-permute-start(bf16[221400]{0:T(1024)(128)(2,1)} %dynamic-slice_reduce_fusion.2), channel_id=1, source_target_pairs={{1,0},{2,1},{3,2},{6,3},{7,6},{10,7},{11,10},{14,11},{15,14},{12,1... | collective-permute-start | bytes 1328408 | tf_op jit(solution)/shard_map/ppermute | solution.py:360
  1630.5 202.2 %collective-permute-start.71 = (f32[48]{0:T(128)S(1)}, f32[48]{0:T(128)S(1)}, u32[]{:S(2)}, u32[]{:S(2)}) collective-permute-start(f32[48]{0:T(128)S(1)} %slice.224), channel_id=1, source_target_pairs={{16,0},{17,1},{18,2},{19,3},{20,4},{21,5},{22,6},{23,7},{24,8},{25... | collective-permute-start | bytes 584 | tf_op jit(solution)/shard_map/ppermute | solution.py:575
  1703.4 10.1 collective-permute-start.43
  1713.6 10.1 collective-permute-start.44
  1723.8 10.1 collective-permute-start.45
  1734.0 10.1 collective-permute-start.46
  1744.1 10.1 collective-permute-start.47
  1784.9 10.1 collective-permute-start.51
  1829.3 12.5 collective-permute-start.74
  1831.3 12.2 collective-permute-start.72
  (206 other events, 2582.5 us)

commit v5 on v4

--- a/solution.py
+++ b/solution.py
@@ -337,47 +337,52 @@
     return [i for k in path for i in sorted(chips[k])]
 
 
-def ring_reduce_scatter(packed, plane, cycle, dp_index):
+def ring_reduce_scatter(blocks, plane, cycle, dp_index):
     n = len(cycle)
-    n_dp = packed.shape[0]
+    n_dp = blocks[0].shape[0]
     axes = ("section", "dp")
     fwd = [(plane * n_dp + cycle[i], plane * n_dp + cycle[(i + 1) % n]) for i in range(n)]
     bwd = [(b, a) for a, b in fwd]
     where_in = [0] * n
     for i, d in enumerate(cycle):
         where_in[d] = i
-    rows = packed[jnp.array(cycle, jnp.int32)]
-    half = rows.shape[1] // 2
-    cw, ccw = rows[:, :half], rows[:, half:]
+    order = jnp.array(cycle * 2, jnp.int32)
+    cw = [bf(x[..., : x.shape[-1] // 2]) for x in blocks]
+    ccw = [bf(x[..., x.shape[-1] // 2 :]) for x in blocks]
     p = jnp.array(where_in, jnp.int32)[dp_index]
 
-    def take(a, idx):
-        return lax.dynamic_index_in_dim(a, idx % n, 0, keepdims=False)
-
-    send_c, send_w = take(cw, p - 1), take(ccw, p + 1)
+    def take(arrays, idx):
+        at = order[idx % n]
+        return [lax.dynamic_index_in_dim(x, at, 0, keepdims=False) for x in arrays]
+
+    send_c, send_w = take(cw, p + n - 1), take(ccw, p + 1)
     for step in range(n - 1):
         got_c = lax.ppermute(send_c, axes, fwd)
         got_w = lax.ppermute(send_w, axes, bwd)
-        acc_c = got_c.astype(F32) + take(cw, p - step - 2).astype(F32)
-        acc_w = got_w.astype(F32) + take(ccw, p + step + 2).astype(F32)
-        send_c, send_w = bf(acc_c), bf(acc_w)
-    return jnp.concatenate([acc_c, acc_w], 0)
-
-
-def pack_rows(arrays, n):
-    flat = [bf(a).reshape(n, -1) for a in arrays]
-    width = sum(f.shape[1] for f in flat)
-    if width % 2:
-        flat.append(jnp.zeros((n, 1), BF16))
-    return jnp.concatenate(flat, 1)
-
-
-def unpack_row(row, arrays, n):
-    out, at = [], 0
+        own_c = take(cw, p + 2 * n - step - 2)
+        own_w = take(ccw, p + step + 2)
+        acc_c = [g.astype(F32) + o.astype(F32) for g, o in zip(got_c, own_c)]
+        acc_w = [g.astype(F32) + o.astype(F32) for g, o in zip(got_w, own_w)]
+        send_c, send_w = [bf(x) for x in acc_c], [bf(x) for x in acc_w]
+    return [jnp.concatenate([c, w], -1) for c, w in zip(acc_c, acc_w)]
+
+
+def as_blocks(arrays, n):
+    big = [a.reshape((n, a.shape[0] // n) + a.shape[1:]) for a in arrays if a.ndim == 2]
+    small = [a.reshape(n, -1) for a in arrays if a.ndim == 1]
+    return big + [jnp.concatenate(small, 1)]
+
+
+def from_blocks(got, arrays, n):
+    big = iter(got[:-1])
+    small, at, out = got[-1], 0, []
     for a in arrays:
-        size = a.size // n
-        out.append(row[at : at + size].reshape((a.shape[0] // n,) + a.shape[1:]))
-        at += size
+        if a.ndim == 2:
+            out.append(next(big))
+        else:
+            width = a.size // n
+            out.append(small[at : at + width])
+            at += width
     return out
 
 
@@ -544,7 +549,7 @@
 
     up_sm = tree_sum(up_small)
     a_list = layer_list(up_w, up_sm) + [cross_w[0], cross_w[1], d_wkv, up_sm[2][0], up_sm[2][1]]
-    a_row = ring_reduce_scatter(pack_rows(a_list, n_dp), 1, cycle, dp_index)
+    a_blocks = as_blocks(a_list, n_dp)
 
     def lower_bwd(gout, saved):
         s_self, s_ffn = saved
@@ -556,7 +561,7 @@
     for m in range(MICRO):
         gout = chunk(cot, m) + returned[m].astype(F32)
         if m == 0:
-            gout, a_row = lax.optimization_barrier((gout, a_row))
+            pass
         else:
             gout, low_grad[-1] = lax.optimization_barrier((gout, low_grad[-1]))
         dh, small, pairs = run_on(low, lower_bwd, gout, low_saved[m])
@@ -567,9 +572,10 @@
     low_w = run_on(low, layer_weight_grads, low_pairs)
     low_sm = tree_sum(low_small)
     b_list = layer_list(low_w, low_sm)
-    b_row = ring_reduce_scatter(pack_rows(b_list, n_dp), 0, cycle, dp_index)
-    a_got = unpack_row(a_row, a_list, n_dp)
-    b_got = unpack_row(b_row, b_list, n_dp)
+    b_blocks = as_blocks(b_list, n_dp)
+    a_blocks, b_blocks = lax.optimization_barrier((a_blocks, b_blocks))
+    a_got = from_blocks(ring_reduce_scatter(a_blocks, 1, cycle, dp_index), a_list, n_dp)
+    b_got = from_blocks(ring_reduce_scatter(b_blocks, 0, cycle, dp_index), b_list, n_dp)
 
     cross_out = a_got[10:]
     cross_copy = lax.ppermute(cross_out, "section", [(1, 0)])

time: 1860 us -> 2140 us (1.15)
  starting transfers between devices: 143 us -> 551 us
  other arithmetic: 486 us -> 145 us
  waiting for transfers between devices: 577 us -> 858 us
  local copies, waits for them, and re-layouts: 393 us -> 240 us
  between operations: 24.8 us -> 86.4 us
    convert_element_type x6 -> x3, other arithmetic: 314 us -> 2.7 us  [the longest x1 1.26 us: per_device(): gout = chunk(cot, m) + returned[m].astype(F32)]
    ppermute x30 -> x195, starting transfers between devices: 43.3 us -> 274 us  [ring_reduce_scatter(): got_c = lax.ppermute(send_c, axes, fwd)]
    ppermute x5, waiting for transfers between devices: 40 us -> 252 us  [per_device(): cross_copy = lax.ppermute(cross_out, 'section', [(1, 0)])]
    ppermute x30 -> x195, starting transfers between devices: 74.6 us -> 252 us  [ring_reduce_scatter(): got_w = lax.ppermute(send_w, axes, bwd)]
    ppermute x30 -> x195, waiting for transfers between devices: 26.8 us -> 138 us  [ring_reduce_scatter(): got_c = lax.ppermute(send_c, axes, fwd)]
    ppermute x2, waiting for transfers between devices: 475 us -> 378 us  [per_device(): returned.append(lax.ppermute(bf(dh), 'section', [(1, 0)]))]
    gather x12 -> x0, local copies, waits for them, and re-layouts: 94.6 us -> none  [ring_reduce_scatter(): rows = packed[jnp.array(cycle, jnp.int32)]]
    ppermute x30 -> x195, waiting for transfers between devices: 25.9 us -> 80.9 us  [ring_reduce_scatter(): got_w = lax.ppermute(send_w, axes, bwd)]
  transfers between devices with their start and end apart: 75 -> 405, of which waited for: 31 -> 102; matrix products, arithmetic and copies ran while one was open for 26% -> 24% of each run, Pallas kernels for 0% -> 0%
where the time goes in v5:
time: 2140 us; the launch traced here: 2110 us
  waiting for transfers between devices  858 us (40%)
  starting transfers between devices  551 us (26%)
  local copies, waits for them, and re-layouts  240 us (11%)
  matrix products  190 us (9%)
  other arithmetic  145 us (7%)
  between operations  86.4 us (4%)
  loops' own time  36.3 us (2%)
    ppermute x2, waiting for transfers between devices, per_device(): returned.append(lax.ppermute(bf(dh), 'section', [(1, 0)]))  378 us
    ppermute x195, starting transfers between devices, ring_reduce_scatter(): got_c = lax.ppermute(send_c, axes, fwd)  274 us
    ppermute x5, waiting for transfers between devices, per_device(): cross_copy = lax.ppermute(cross_out, 'section', [(1, 0)])  252 us
    ppermute x195, starting transfers between devices, ring_reduce_scatter(): got_w = lax.ppermute(send_w, axes, bwd)  252 us
    ppermute x195, waiting for transfers between devices, ring_reduce_scatter(): got_c = lax.ppermute(send_c, axes, fwd)  138 us
    convert_element_type x380, other arithmetic, bf(): return x.astype(BF16)  92.1 us
    another operation x81, local copies, waits for them, and re-layouts  90.6 us
    ppermute x195, waiting for transfers between devices, ring_reduce_scatter(): got_w = lax.ppermute(send_w, axes, bwd)  80.9 us
  transfers between devices with their start and end apart: 405, of which 102 were waited for; matrix products, arithmetic and copies ran while one was open for 24% of the time, Pallas kernels for 0%

profile of v5, /device:TPU:0, one launch (start us, length us, event | category | flops | bytes accessed | tf_op | source)
XLA Modules:
  0.0 2106.7 jit_solution(14234733257707881951)
XLA Ops:
  5.6 9.7 collective-permute-done.2
  26.3 67.7 %conditional.12 = (f32[8,64,768]{2,1,0:T(8,128)}, bf16[8,64,12,64]{3,1,2,0:T(8,128)(2,1)}, bf16[8,64,768]{2,1,0:T(8,128)(2,1)}, f32[8,64,768]{2,1,0:T(8,128)}, f...) conditional(s32[]{:T(128)} %convert_element_type.4911, ...), branch_computations={%region_0.0_spmd, %region_1.8_spmd} | conditional | flops 7464489984 | bytes 124480776 | solution.py:31
  67.9 18.6 fusion.71
  98.9 66.4 %conditional.13 = (f32[8,64,768]{2,1,0:T(8,128)}, bf16[8,64,12,64]{3,1,2,0:T(8,128)(2,1)S(1)}, bf16[8,64,768]{2,1,0:T(8,128)(2,1)}, f32[8,64,768]{2,1,0:T(8,128)...) conditional(s32[]{:T(128)} %convert_element_type.4911, ...), branch_computations={%region_8.9_spmd, %region_9.16_spmd} | conditional | flops 7464489984 | bytes 118189384 | solution.py:31
  139.4 18.5 fusion.102
  158.0 7.1 add_add_fusion.1
  180.8 29.3 %conditional.15 = (f32[8,64,768]{2,1,0:T(8,128)}, bf16[8,64,12,64]{3,1,2,0:T(8,128)(2,1)}, bf16[8,64,768]{2,1,0:T(8,128)(2,1)}, f32[8,64,768]{2,1,0:T(8,128)}, f...) conditional(s32[]{:T(128)} %convert_element_type.4914, ...), branch_computations={%region_19.20_spmd, %region_20.29_spmd} | conditional | flops 10490288128 | bytes 124310992 | solution.py:31
  210.2 23.6 %conditional.17 = (f32[8,64,768]{2,1,0:T(8,128)}, f32[768]{0:T(1024)S(1)}, f32[768]{0:T(1024)S(1)}, f32[768]{0:T(1024)S(1)}, f32[768]{0:T(1024)S(1)}, /*index=5*...) conditional(s32[]{:T(128)} %convert_element_type.4914, ...), branch_computations={%region_39.40_spmd, %region_40.54_spmd} | conditional | flops 13324111872 | bytes 152132064 | solution.py:31
  234.5 29.3 %conditional.16 = (bf16[8,64,12,64]{3,1,2,0:T(8,128)(2,1)}, bf16[8,64,768]{2,1,0:T(8,128)(2,1)}, f32[8,64,768]{2,1,0:T(8,128)}, f32[8,64,1]{1,0,2:T(8,128)S(1)},...) conditional(s32[]{:T(128)} %convert_element_type.4914, ...), branch_computations={%region_29.30_spmd, %region_30.39_spmd} | conditional | flops 10490288128 | bytes 124311000 | solution.py:31
  263.7 29.1 %conditional.18 = (f32[8,64,768]{2,1,0:T(8,128)}, f32[768]{0:T(1024)S(1)}, f32[768]{0:T(1024)S(1)}, f32[768]{0:T(1024)S(1)}, f32[768]{0:T(1024)S(1)}, /*index=5*...) conditional(s32[]{:T(128)} %convert_element_type.4914, ...), branch_computations={%region_54.55_spmd, %region_55.69_spmd} | conditional | flops 13324111872 | bytes 152132064 | solution.py:31
  292.9 7.9 add_convert_fusion.10
  391.4 19.3 conditional.22
  411.5 377.7 %collective-permute-done.6 = bf16[8,64,768]{2,1,0:T(8,128)(2,1)} collective-permute-done((bf16[8,64,768]{2,1,0:T(8,128)(2,1)}, bf16[8,64,768]{2,1,0:T(8,128)(2,1)}, u32[]{:S(2)}, u32[]{:S(2)}) %collective-permute-start.6) | collective-permute-done | bytes 786464 | tf_op jit(solution)/shard_map/ppermute | solution.py:501
  790.5 74.2 %conditional.19 = (f32[8,64,768]{2,1,0:T(8,128)}, f32[768]{0:T(1024)S(1)}, f32[768]{0:T(1024)S(1)}, f32[768]{0:T(1024)S(1)}, f32[768]{0:T(1024)S(1)}, /*index=5*...) conditional(s32[]{:T(128)} %convert_element_type.4911, ...), branch_computations={%region_69.70_spmd, %region_70.80_spmd} | conditional | flops 7580802048 | bytes 129884416 | solution.py:31
  793.8 19.7 fusion.264
  845.1 8.4 convert_element_type.3348
  867.3 71.0 %conditional.20 = (f32[768]{0:T(1024)S(1)}, f32[768]{0:T(1024)S(1)}, f32[768]{0:T(1024)S(1)}, f32[768]{0:T(1024)S(1)}, bf16[8,64,2304]{2,1,0:T(8,128)(2,1)}, /*i...) conditional(s32[]{:T(128)} %convert_element_type.4911, ...), branch_computations={%region_80.81_spmd, %region_81.91_spmd} | conditional | flops 7580408832 | bytes 117301536 | solution.py:31
  868.4 19.1 fusion.289
  918.8 8.4 convert_element_type.3355
  941.1 36.6 %conditional.23 = (bf16[16,48,2304]{2,1,0:T(8,128)(2,1)S(1)}, bf16[16,48,768]{2,1,0:T(8,128)(2,1)}, bf16[16,48,3072]{2,1,0:T(8,128)(2,1)}, bf16[16,192]{1,0:T(8,...) conditional(s32[]{:T(128)} %convert_element_type.4911, () %tuple.171, ...), branch_computations={%region_97.98_spmd, %region_98.101_spmd} | conditional | flops 14512025600 | bytes 62937648 | solution.py:31
  945.3 8.3 fusion.60
  957.0 8.8 fusion.42
  979.2 7.5 maximum_select_fusion
  1561.0 243.8 %collective-permute-done.404 = f32[48,768]{1,0:T(8,128)S(1)} collective-permute-done((f32[48,768]{1,0:T(8,128)S(1)}, f32[48,768]{1,0:T(8,128)S(1)}, u32[]{:S(2)}, u32[]{:S(2)}) %collective-permute-start.404) | collective-permute-done | bytes 147488 | tf_op jit(solution)/shard_map/ppermute | solution.py:581
  (1716 shorter events, 1223.5 us)
Async XLA Ops:
  19.9 155.0 %collective-permute-start.3 = (bf16[576,1536]{1,0:T(8,128)(2,1)}, bf16[576,1536]{1,0:T(8,128)(2,1)}, u32[]{:S(2)}, u32[]{:S(2)}) collective-permute-start(bf16[576,1536]{1,0:T(8,128)(2,1)} %get-tuple-element.847), channel_id=1, source_target_pairs={{0,1},{1,2},{2,3},{3,4},{4,5},{5,6},{6,7},{7,8},{8,9},{9,10},{10,1... | collective-permute-start | bytes 5308424 | tf_op jit(solution)/shard_map/ppermute | solution.py:432
  19.9 155.0 %collective-permute-start.4 = (bf16[576,1536]{1,0:T(8,128)(2,1)}, bf16[576,1536]{1,0:T(8,128)(2,1)}, u32[]{:S(2)}, u32[]{:S(2)}) collective-permute-start(bf16[576,1536]{1,0:T(8,128)(2,1)} %get-tuple-element.847), channel_id=1, source_target_pairs={{1,0},{2,1},{3,2},{4,3},{5,4},{6,5},{7,6},{8,7},{9,8},{10,9},{11,1... | collective-permute-start | bytes 5308424 | tf_op jit(solution)/shard_map/ppermute | solution.py:433
  96.6 84.2 %collective-permute-start.1 = (bf16[8,64,768]{2,1,0:T(8,128)(2,1)}, bf16[8,64,768]{2,1,0:T(8,128)(2,1)}, u32[]{:S(2)}, u32[]{:S(2)}) collective-permute-start(bf16[8,64,768]{2,1,0:T(8,128)(2,1)} %convert_element_type.4915), channel_id=1, source_target_pairs={{0,16},{1,17},{2,18},{3,19},{4,20},{5,21},{6,22},{7,23},{8,24},{9,... | collective-permute-start | bytes 2359304 | tf_op jit(solution)/shard_map/ppermute | solution.py:466
  168.3 65.5 %collective-permute-start = (bf16[8,64,768]{2,1,0:T(8,128)(2,1)}, bf16[8,64,768]{2,1,0:T(8,128)(2,1)}, u32[]{:S(2)}, u32[]{:S(2)}) collective-permute-start(bf16[8,64,768]{2,1,0:T(8,128)(2,1)} %convert_element_type.4913), channel_id=1, source_target_pairs={{0,16},{1,17},{2,18},{3,19},{4,20},{5,21},{6,22},{7,23},{8,24},{9,... | collective-permute-start | bytes 2359304 | tf_op jit(solution)/shard_map/ppermute | solution.py:466
  304.3 682.4 %collective-permute-start.7 = (bf16[576,1536]{1,0:T(8,128)(2,1)}, bf16[576,1536]{1,0:T(8,128)(2,1)}, u32[]{:S(2)}, u32[]{:S(2)}) collective-permute-start(bf16[576,1536]{1,0:T(8,128)(2,1)} %get-tuple-element.1551), channel_id=1, source_target_pairs={{1,0},{2,1},{3,2},{4,3},{5,4},{6,5},{7,6},{8,7},{9,8},{10,9},{11,1... | collective-permute-start | bytes 5308424 | tf_op jit(solution)/shard_map/ppermute | solution.py:526
  304.5 682.2 %collective-permute-start.8 = (bf16[576,1536]{1,0:T(8,128)(2,1)}, bf16[576,1536]{1,0:T(8,128)(2,1)}, u32[]{:S(2)}, u32[]{:S(2)}) collective-permute-start(bf16[576,1536]{1,0:T(8,128)(2,1)} %get-tuple-element.1552), channel_id=1, source_target_pairs={{0,1},{1,2},{2,3},{3,4},{4,5},{5,6},{6,7},{7,8},{8,9},{9,10},{10,1... | collective-permute-start | bytes 5308424 | tf_op jit(solution)/shard_map/ppermute | solution.py:527
  307.2 482.0 %collective-permute-start.6 = (bf16[8,64,768]{2,1,0:T(8,128)(2,1)}, bf16[8,64,768]{2,1,0:T(8,128)(2,1)}, u32[]{:S(2)}, u32[]{:S(2)}) collective-permute-start(bf16[8,64,768]{2,1,0:T(8,128)(2,1)} %convert_element_type.4920), channel_id=1, source_target_pairs={{16,0},{17,1},{18,2},{19,3},{20,4},{21,5},{22,6},{23,7},{24,8},{25... | collective-permute-start | bytes 2359304 | tf_op jit(solution)/shard_map/ppermute | solution.py:501
  310.9 553.9 %collective-permute-start.5 = (bf16[8,64,768]{2,1,0:T(8,128)(2,1)}, bf16[8,64,768]{2,1,0:T(8,128)(2,1)}, u32[]{:S(2)}, u32[]{:S(2)}) collective-permute-start(bf16[8,64,768]{2,1,0:T(8,128)(2,1)} %convert_element_type.4918), channel_id=1, source_target_pairs={{16,0},{17,1},{18,2},{19,3},{20,4},{21,5},{22,6},{23,7},{24,8},{25... | collective-permute-start | bytes 2359304 | tf_op jit(solution)/shard_map/ppermute | solution.py:501
  994.6 206.2 %collective-permute-start.374 = (bf16[48,384]{1,0:T(8,128)(2,1)}, bf16[48,384]{1,0:T(8,128)(2,1)}, u32[]{:S(2)}, u32[]{:S(2)}) collective-permute-start(bf16[48,384]{1,0:T(8,128)(2,1)} %fusion.699), channel_id=1, source_target_pairs={{16,17},{17,18},{18,19},{19,22},{22,23},{23,26},{26,27},{27,30},{3... | collective-permute-start | bytes 110600 | tf_op jit(solution)/shard_map/ppermute | solution.py:360
  996.4 205.8 %collective-permute-start.389 = (bf16[48,384]{1,0:T(8,128)(2,1)}, bf16[48,384]{1,0:T(8,128)(2,1)}, u32[]{:S(2)}, u32[]{:S(2)}) collective-permute-start(bf16[48,384]{1,0:T(8,128)(2,1)} %fusion.683), channel_id=1, source_target_pairs={{17,16},{18,17},{19,18},{22,19},{23,22},{26,23},{27,26},{30,27},{3... | collective-permute-start | bytes 110600 | tf_op jit(solution)/shard_map/ppermute | solution.py:361
  1000.4 222.9 %collective-permute-start.343 = (bf16[48,768]{1,0:T(8,128)(2,1)}, bf16[48,768]{1,0:T(8,128)(2,1)}, u32[]{:S(2)}, u32[]{:S(2)}) collective-permute-start(bf16[48,768]{1,0:T(8,128)(2,1)} %fusion.551), channel_id=1, source_target_pairs={{16,17},{17,18},{18,19},{19,22},{22,23},{23,26},{26,27},{27,30},{3... | collective-permute-start | bytes 221192 | tf_op jit(solution)/shard_map/ppermute | solution.py:360
  1002.3 222.7 %collective-permute-start.358 = (bf16[48,768]{1,0:T(8,128)(2,1)}, bf16[48,768]{1,0:T(8,128)(2,1)S(1)}, u32[]{:S(2)}, u32[]{:S(2)}) collective-permute-start(bf16[48,768]{1,0:T(8,128)(2,1)} %fusion.535), channel_id=1, source_target_pairs={{17,16},{18,17},{19,18},{22,19},{23,22},{26,23},{27,26},{30,27},{3... | collective-permute-start | bytes 221192 | tf_op jit(solution)/shard_map/ppermute | solution.py:361
  1202.2 82.4 %collective-permute-start.280 = (bf16[192,384]{1,0:T(8,128)(2,1)}, bf16[192,384]{1,0:T(8,128)(2,1)S(1)}, u32[]{:S(2)}, u32[]{:S(2)}) collective-permute-start(bf16[192,384]{1,0:T(8,128)(2,1)} %dynamic-slice_bitcast_fusion.1), channel_id=1, source_target_pairs={{0,1},{1,2},{2,3},{3,6},{6,7},{7,10},{10,11},{11,14},{14,15},{15,1... | collective-permute-start | bytes 442376 | tf_op jit(solution)/shard_map/ppermute | solution.py:360
  1205.1 80.2 %collective-permute-start.295 = (bf16[192,384]{1,0:T(8,128)(2,1)S(1)}, bf16[192,384]{1,0:T(8,128)(2,1)S(1)}, u32[]{:S(2)}, u32[]{:S(2)}) collective-permute-start(bf16[192,384]{1,0:T(8,128)(2,1)S(1)} %dynamic-slice_bitcast_fusion), channel_id=1, source_target_pairs={{1,0},{2,1},{3,2},{6,3},{7,6},{10,7},{11,10},{14,11},{15,14},{12,1... | collective-permute-start | bytes 442376 | tf_op jit(solution)/shard_map/ppermute | solution.py:361
  1221.8 64.2 %collective-permute-start.250 = (bf16[192,384]{1,0:T(8,128)(2,1)S(1)}, bf16[192,384]{1,0:T(8,128)(2,1)S(1)}, u32[]{:S(2)}, u32[]{:S(2)}) collective-permute-start(bf16[192,384]{1,0:T(8,128)(2,1)S(1)} %dynamic-slice_bitcast_fusion.3), channel_id=1, source_target_pairs={{16,17},{17,18},{18,19},{19,22},{22,23},{23,26},{26,27},{27,30},{3... | collective-permute-start | bytes 442376 | tf_op jit(solution)/shard_map/ppermute | solution.py:360
  1223.3 65.5 %collective-permute-start.265 = (bf16[192,384]{1,0:T(8,128)(2,1)S(1)}, bf16[192,384]{1,0:T(8,128)(2,1)S(1)}, u32[]{:S(2)}, u32[]{:S(2)}) collective-permute-start(bf16[192,384]{1,0:T(8,128)(2,1)S(1)} %dynamic-slice_bitcast_fusion.2), channel_id=1, source_target_pairs={{17,16},{18,17},{19,18},{22,19},{23,22},{26,23},{27,26},{30,27},{3... | collective-permute-start | bytes 442376 | tf_op jit(solution)/shard_map/ppermute | solution.py:361
  1283.1 576.4 %collective-permute-start.9 = (f32[288,768]{1,0:T(8,128)S(1)}, f32[288,768]{1,0:T(8,128)S(1)}, u32[]{:S(2)}, u32[]{:S(2)}) collective-permute-start(f32[288,768]{1,0:T(8,128)S(1)} %slice.257), channel_id=1, source_target_pairs={{16,0},{17,1},{18,2},{19,3},{20,4},{21,5},{22,6},{23,7},{24,8},{25... | collective-permute-start | bytes 2654216 | tf_op jit(solution)/shard_map/ppermute | solution.py:537
  1390.4 60.0 %collective-permute-start.282 = (bf16[192,384]{1,0:T(8,128)(2,1)S(1)}, bf16[192,384]{1,0:T(8,128)(2,1)S(1)}, u32[]{:S(2)}, u32[]{:S(2)}) collective-permute-start(bf16[192,384]{1,0:T(8,128)(2,1)S(1)} %fusion.340), channel_id=1, source_target_pairs={{0,1},{1,2},{2,3},{3,6},{6,7},{7,10},{10,11},{11,14},{14,15},{15,1... | collective-permute-start | bytes 442376 | tf_op jit(solution)/shard_map/ppermute | solution.py:360
  1470.5 71.9 %collective-permute-start.283 = (bf16[192,384]{1,0:T(8,128)(2,1)S(1)}, bf16[192,384]{1,0:T(8,128)(2,1)S(1)}, u32[]{:S(2)}, u32[]{:S(2)}) collective-permute-start(bf16[192,384]{1,0:T(8,128)(2,1)S(1)} %fusion.339), channel_id=1, source_target_pairs={{0,1},{1,2},{2,3},{3,6},{6,7},{7,10},{10,11},{11,14},{14,15},{15,1... | collective-permute-start | bytes 442376 | tf_op jit(solution)/shard_map/ppermute | solution.py:360
  1486.7 56.4 %collective-permute-start.298 = (bf16[192,384]{1,0:T(8,128)(2,1)S(1)}, bf16[192,384]{1,0:T(8,128)(2,1)S(1)}, u32[]{:S(2)}, u32[]{:S(2)}) collective-permute-start(bf16[192,384]{1,0:T(8,128)(2,1)S(1)} %fusion.324), channel_id=1, source_target_pairs={{1,0},{2,1},{3,2},{6,3},{7,6},{10,7},{11,10},{14,11},{15,14},{12,1... | collective-permute-start | bytes 442376 | tf_op jit(solution)/shard_map/ppermute | solution.py:361
  1552.6 252.2 %collective-permute-start.404 = (f32[48,768]{1,0:T(8,128)S(1)}, f32[48,768]{1,0:T(8,128)S(1)}, u32[]{:S(2)}, u32[]{:S(2)}) collective-permute-start(f32[48,768]{1,0:T(8,128)S(1)} %pad_maximum_fusion.8), channel_id=1, source_target_pairs={{16,0},{17,1},{18,2},{19,3},{20,4},{21,5},{22,6},{23,7},{24,8},{25... | collective-permute-start | bytes 442376 | tf_op jit(solution)/shard_map/ppermute | solution.py:581
  1554.0 253.3 %collective-permute-start.342 = (f32[48,768]{1,0:T(8,128)S(1)}, f32[48,768]{1,0:T(8,128)S(1)}, u32[]{:S(2)}, u32[]{:S(2)}) collective-permute-start(f32[48,768]{1,0:T(8,128)S(1)} %pad_maximum_fusion.7), channel_id=1, source_target_pairs={{16,0},{17,1},{18,2},{19,3},{20,4},{21,5},{22,6},{23,7},{24,8},{25... | collective-permute-start | bytes 442376 | tf_op jit(solution)/shard_map/ppermute | solution.py:581
  1555.3 265.2 %collective-permute-start.284 = (bf16[192,384]{1,0:T(8,128)(2,1)S(1)}, bf16[192,384]{1,0:T(8,128)(2,1)S(1)}, u32[]{:S(2)}, u32[]{:S(2)}) collective-permute-start(bf16[192,384]{1,0:T(8,128)(2,1)S(1)} %fusion.338), channel_id=1, source_target_pairs={{0,1},{1,2},{2,3},{3,6},{6,7},{7,10},{10,11},{11,14},{14,15},{15,1... | collective-permute-start | bytes 442376 | tf_op jit(solution)/shard_map/ppermute | solution.py:360
  1557.7 263.5 %collective-permute-start.299 = (bf16[192,384]{1,0:T(8,128)(2,1)S(1)}, bf16[192,384]{1,0:T(8,128)(2,1)S(1)}, u32[]{:S(2)}, u32[]{:S(2)}) collective-permute-start(bf16[192,384]{1,0:T(8,128)(2,1)S(1)} %fusion.323), channel_id=1, source_target_pairs={{1,0},{2,1},{3,2},{6,3},{7,6},{10,7},{11,10},{14,11},{15,14},{12,1... | collective-permute-start | bytes 442376 | tf_op jit(solution)/shard_map/ppermute | solution.py:361
  (494 other events, 8178.9 us)

commit v6 on v4

--- a/solution.py
+++ b/solution.py
@@ -346,38 +346,55 @@
     where_in = [0] * n
     for i, d in enumerate(cycle):
         where_in[d] = i
-    rows = packed[jnp.array(cycle, jnp.int32)]
-    half = rows.shape[1] // 2
-    cw, ccw = rows[:, :half], rows[:, half:]
+    order = jnp.array(cycle * 2, jnp.int32)
+    half = packed.shape[-1] // 2
+    cw, ccw = packed[..., :half], packed[..., half:]
     p = jnp.array(where_in, jnp.int32)[dp_index]
 
     def take(a, idx):
-        return lax.dynamic_index_in_dim(a, idx % n, 0, keepdims=False)
-
-    send_c, send_w = take(cw, p - 1), take(ccw, p + 1)
+        return lax.dynamic_index_in_dim(a, order[idx % n], 0, keepdims=False)
+
+    send_c, send_w = take(cw, p + n - 1), take(ccw, p + 1)
     for step in range(n - 1):
         got_c = lax.ppermute(send_c, axes, fwd)
         got_w = lax.ppermute(send_w, axes, bwd)
-        acc_c = got_c.astype(F32) + take(cw, p - step - 2).astype(F32)
+        acc_c = got_c.astype(F32) + take(cw, p + 2 * n - step - 2).astype(F32)
         acc_w = got_w.astype(F32) + take(ccw, p + step + 2).astype(F32)
         send_c, send_w = bf(acc_c), bf(acc_w)
-    return jnp.concatenate([acc_c, acc_w], 0)
-
-
-def pack_rows(arrays, n):
-    flat = [bf(a).reshape(n, -1) for a in arrays]
-    width = sum(f.shape[1] for f in flat)
-    if width % 2:
-        flat.append(jnp.zeros((n, 1), BF16))
-    return jnp.concatenate(flat, 1)
-
-
-def unpack_row(row, arrays, n):
+    return jnp.concatenate([acc_c, acc_w], -1)
+
+
+def pack_rows(arrays, n, rows):
+    pieces = [bf(a).reshape(n, rows, -1) for a in arrays if a.ndim == 2]
+    vecs = jnp.concatenate([bf(a).reshape(n, -1) for a in arrays if a.ndim == 1], 1)
+    width = -(-vecs.shape[1] // rows)
+    vecs = jnp.pad(vecs, ((0, 0), (0, width * rows - vecs.shape[1]))).reshape(n, rows, width)
+    pieces.append(vecs)
+    cols = sum(x.shape[-1] for x in pieces)
+    target = -(-cols // 256) * 256
+    pieces.append(jnp.zeros((n, rows, target - cols), BF16))
+    return jnp.concatenate(pieces, -1)
+
+
+def unpack_row(block, arrays, n, rows):
     out, at = [], 0
-    for a in arrays:
-        size = a.size // n
-        out.append(row[at : at + size].reshape((a.shape[0] // n,) + a.shape[1:]))
-        at += size
+    mats = {}
+    for i, a in enumerate(arrays):
+        if a.ndim == 2:
+            width = a.size // n // rows
+            mats[i] = block[:, at : at + width].reshape((a.shape[0] // n,) + a.shape[1:])
+            at += width
+    vec_total = sum(a.size // n for a in arrays if a.ndim == 1)
+    width = -(-vec_total // rows)
+    flat = block[:, at : at + width].reshape(-1)
+    vat = 0
+    for i, a in enumerate(arrays):
+        if a.ndim == 2:
+            out.append(mats[i])
+        else:
+            size = a.size // n
+            out.append(flat[vat : vat + size])
+            vat += size
     return out
 
 
@@ -544,7 +561,8 @@
 
     up_sm = tree_sum(up_small)
     a_list = layer_list(up_w, up_sm) + [cross_w[0], cross_w[1], d_wkv, up_sm[2][0], up_sm[2][1]]
-    a_row = ring_reduce_scatter(pack_rows(a_list, n_dp), 1, cycle, dp_index)
+    block_rows = wqkv.shape[0] // n_dp
+    a_packed = pack_rows(a_list, n_dp, block_rows)
 
     def lower_bwd(gout, saved):
         s_self, s_ffn = saved
@@ -556,7 +574,7 @@
     for m in range(MICRO):
         gout = chunk(cot, m) + returned[m].astype(F32)
         if m == 0:
-            gout, a_row = lax.optimization_barrier((gout, a_row))
+            pass
         else:
             gout, low_grad[-1] = lax.optimization_barrier((gout, low_grad[-1]))
         dh, small, pairs = run_on(low, lower_bwd, gout, low_saved[m])
@@ -567,9 +585,12 @@
     low_w = run_on(low, layer_weight_grads, low_pairs)
     low_sm = tree_sum(low_small)
     b_list = layer_list(low_w, low_sm)
-    b_row = ring_reduce_scatter(pack_rows(b_list, n_dp), 0, cycle, dp_index)
-    a_got = unpack_row(a_row, a_list, n_dp)
-    b_got = unpack_row(b_row, b_list, n_dp)
+    b_packed = pack_rows(b_list, n_dp, block_rows)
+    a_packed, b_packed = lax.optimization_barrier((a_packed, b_packed))
+    a_row = ring_reduce_scatter(a_packed, 1, cycle, dp_index)
+    b_row = ring_reduce_scatter(b_packed, 0, cycle, dp_index)
+    a_got = unpack_row(a_row, a_list, n_dp, block_rows)
+    b_got = unpack_row(b_row, b_list, n_dp, block_rows)
 
     cross_out = a_got[10:]
     cross_copy = lax.ppermute(cross_out, "section", [(1, 0)])

time: 1860 us -> 1280 us (0.69)
  other arithmetic: 486 us -> 114 us
  waiting for transfers between devices: 577 us -> 428 us
  local copies, waits for them, and re-layouts: 393 us -> 281 us
  between operations: 24.8 us -> 79.8 us
    convert_element_type x6 -> x1, other arithmetic: 314 us -> 1.26 us  [per_device(): gout = chunk(cot, m) + returned[m].astype(F32)]
    ppermute x2, waiting for transfers between devices: 475 us -> 300 us  [per_device(): returned.append(lax.ppermute(bf(dh), 'section', [(1, 0)]))]
    gather x12 -> x0, local copies, waits for them, and re-layouts: 94.6 us -> none  [ring_reduce_scatter(): rows = packed[jnp.array(cycle, jnp.int32)]]
    ppermute x1, waiting for transfers between devices: 0.01 us -> 58.3 us  [per_device(): ig_first = lax.ppermute(image_grad_full[:half], 'section', [(1, 0)])]
    concatenate x3 -> x4, local copies, waits for them, and re-layouts: 10.7 us -> 54.6 us  [the longest x2 53.6 us: pack_rows(): return jnp.concatenate(pieces, -1)]
    unnamed x2 -> x0, other arithmetic: 37 us -> none
    unnamed x278 -> x105, local copies, waits for them, and re-layouts: 37.9 us -> 2.01 us
    dynamic_slice x3 -> x2, local copies, waits for them, and re-layouts: 34.7 us -> 1.51 us  [take(): return lax.dynamic_index_in_dim(a, order[idx % n], 0, keepdims=False)]
  transfers between devices with their start and end apart: 75 -> 75, of which waited for: 31 -> 24; matrix products, arithmetic and copies ran while one was open for 26% -> 42% of each run, Pallas kernels for 0% -> 0%
where the time goes in v6:
time: 1280 us; the launch traced here: 1260 us
  waiting for transfers between devices  428 us (33%)
  local copies, waits for them, and re-layouts  281 us (22%)
  matrix products  191 us (15%)
  starting transfers between devices  134 us (10%)
  other arithmetic  114 us (9%)
  between operations  79.8 us (6%)
  loops' own time  35.1 us (3%)
    ppermute x2, waiting for transfers between devices, per_device(): returned.append(lax.ppermute(bf(dh), 'section', [(1, 0)]))  300 us
    another operation x81, local copies, waits for them, and re-layouts  91.4 us
    dot_general x8, matrix products, mm_t(): return jnp.einsum('...e,de->...d', g, w, preferred_element_type=F32)  68.9 us
    ppermute x30, starting transfers between devices, ring_reduce_scatter(): got_w = lax.ppermute(send_w, axes, bwd)  67.8 us
    dot_general x8, matrix products, mm(): return jnp.einsum('...d,de->...e', a, w, preferred_element_type=F32)  62.4 us
    ppermute x1, waiting for transfers between devices, per_device(): ig_first = lax.ppermute(image_grad_full[:half], 'section', [(1, 0)])  58.3 us
    convert_element_type x77, other arithmetic, bf(): return x.astype(BF16)  56.4 us
    concatenate x2, local copies, waits for them, and re-layouts, pack_rows(): return jnp.concatenate(pieces, -1)  53.6 us
  transfers between devices with their start and end apart: 75, of which 24 were waited for; matrix products, arithmetic and copies ran while one was open for 42% of the time, Pallas kernels for 0%

profile of v6, /device:TPU:0, one launch (start us, length us, event | category | flops | bytes accessed | tf_op | source)
XLA Modules:
  0.0 1263.2 jit_solution(15339402245045066025)
XLA Ops:
  5.6 9.7 collective-permute-done.2
  26.3 67.6 %conditional.12 = (f32[8,64,768]{2,1,0:T(8,128)}, bf16[8,64,12,64]{3,1,2,0:T(8,128)(2,1)}, bf16[8,64,768]{2,1,0:T(8,128)(2,1)}, f32[8,64,768]{2,1,0:T(8,128)}, f...) conditional(s32[]{:T(128)} %convert_element_type.1093, ...), branch_computations={%region_0.0_spmd, %region_1.8_spmd} | conditional | flops 7464489984 | bytes 124480776 | solution.py:31
  67.9 18.6 %fusion.85 = (bf16[8,64,3072]{2,1,0:T(8,128)(2,1)}, f32[8,64,3072]{2,1,0:T(8,128)}) fusion(f32[3072]{0:T(1024)S(1)} %bitcast.780, bf16[8,64,768]{2,1,0:T(8,128)(2,1)} %get-tuple-element.1595, bf16[768,3072]{1,0:T(8,128)(2,1)} %get-tuple-element.449), kind=kOutput, calls=%fused_computation.90 | convolution fusion | flops 2519728128 | bytes 14954496 | tf_op jit(solution)/shard_map/cond/branch_1_fun/...d,de->...e/dot_general | solution.py:58
  98.8 66.3 %conditional.13 = (f32[8,64,768]{2,1,0:T(8,128)}, bf16[8,64,12,64]{3,1,2,0:T(8,128)(2,1)S(1)}, bf16[8,64,768]{2,1,0:T(8,128)(2,1)}, f32[8,64,768]{2,1,0:T(8,128)...) conditional(s32[]{:T(128)} %convert_element_type.1093, ...), branch_computations={%region_8.9_spmd, %region_9.16_spmd} | conditional | flops 7464489984 | bytes 118189384 | solution.py:31
  139.2 18.5 %fusion.116 = (bf16[8,64,3072]{2,1,0:T(8,128)(2,1)}, f32[8,64,3072]{2,1,0:T(8,128)}) fusion(f32[3072]{0:T(1024)S(1)} %bitcast.781, bf16[8,64,768]{2,1,0:T(8,128)(2,1)} %get-tuple-element.1623, bf16[768,3072]{1,0:T(8,128)(2,1)} %get-tuple-element.461), kind=kOutput, calls=%fused_computation.148 | convolution fusion | flops 2519728128 | bytes 14954496 | tf_op jit(solution)/shard_map/cond/branch_1_fun/...d,de->...e/dot_general | solution.py:58
  211.8 29.2 %conditional.15 = (f32[8,64,768]{2,1,0:T(8,128)}, bf16[8,64,12,64]{3,1,2,0:T(8,128)(2,1)}, bf16[8,64,768]{2,1,0:T(8,128)(2,1)}, f32[8,64,768]{2,1,0:T(8,128)}, f...) conditional(s32[]{:T(128)} %convert_element_type.1096, ...), branch_computations={%region_19.20_spmd, %region_20.29_spmd} | conditional | flops 10490288128 | bytes 124310992 | solution.py:31
  241.0 23.9 %conditional.17 = (f32[8,64,768]{2,1,0:T(8,128)}, f32[768]{0:T(1024)S(1)}, f32[768]{0:T(1024)S(1)}, f32[768]{0:T(1024)S(1)}, f32[768]{0:T(1024)S(1)}, /*index=5*...) conditional(s32[]{:T(128)} %convert_element_type.1096, ...), branch_computations={%region_39.40_spmd, %region_40.54_spmd} | conditional | flops 13324111872 | bytes 152132064 | solution.py:31
  268.8 29.0 %conditional.16 = (bf16[8,64,12,64]{3,1,2,0:T(8,128)(2,1)}, bf16[8,64,768]{2,1,0:T(8,128)(2,1)}, f32[8,64,768]{2,1,0:T(8,128)}, f32[8,64,1]{1,0,2:T(8,128)S(1)},...) conditional(s32[]{:T(128)} %convert_element_type.1096, ...), branch_computations={%region_29.30_spmd, %region_30.39_spmd} | conditional | flops 10490288128 | bytes 124311000 | solution.py:31
  297.8 28.0 %conditional.18 = (f32[8,64,768]{2,1,0:T(8,128)}, f32[768]{0:T(1024)S(1)}, f32[768]{0:T(1024)S(1)}, f32[768]{0:T(1024)S(1)}, f32[768]{0:T(1024)S(1)}, /*index=5*...) conditional(s32[]{:T(128)} %convert_element_type.1096, ...), branch_computations={%region_54.55_spmd, %region_55.69_spmd} | conditional | flops 13324111872 | bytes 152132064 | solution.py:31
  390.6 19.2 %conditional.22 = (bf16[16,48,2304]{2,1,0:T(8,128)(2,1)}, bf16[16,48,768]{2,1,0:T(8,128)(2,1)}, bf16[16,48,3072]{2,1,0:T(8,128)(2,1)}, bf16[16,192]{1,0:T(8,128)...) conditional(s32[]{:T(128)} %convert_element_type.1096, ...), branch_computations={%region_93.94_spmd, %region_94.0_spmd} | conditional | flops 16939347968 | bytes 65327688 | solution.py:31
  410.9 53.3 %collective-permute-done.6 = bf16[8,64,768]{2,1,0:T(8,128)(2,1)} collective-permute-done((bf16[8,64,768]{2,1,0:T(8,128)(2,1)}, bf16[8,64,768]{2,1,0:T(8,128)(2,1)}, u32[]{:S(2)}, u32[]{:S(2)}) %collective-permute-start.6) | collective-permute-done | bytes 786464 | tf_op jit(solution)/shard_map/ppermute | solution.py:513
  465.4 74.3 %conditional.19 = (f32[8,64,768]{2,1,0:T(8,128)}, f32[768]{0:T(1024)S(1)}, f32[768]{0:T(1024)S(1)}, f32[768]{0:T(1024)S(1)}, f32[768]{0:T(1024)S(1)}, /*index=5*...) conditional(s32[]{:T(128)} %convert_element_type.1093, ...), branch_computations={%region_69.70_spmd, %region_70.80_spmd} | conditional | flops 7580802048 | bytes 129884416 | solution.py:31
  468.8 19.6 %fusion.278 = bf16[8,64,3072]{2,1,0:T(8,128)(2,1)} fusion(f32[8,64,3072]{2,1,0:T(8,128)} %get-tuple-element.574, bf16[8,64,768]{2,1,0:T(8,128)(2,1)} %get-tuple-element.1811, bf16[3072,768]{1,0:T(8,128)(2,1)S(1)} %copy-done.91), kind=kOutput, calls=%fused_computation.468 | convolution fusion | flops 2529165312 | bytes 14942208 | tf_op jit(solution)/shard_map/cond/branch_1_fun/...e,de->...d/dot_general | solution.py:62
  539.8 247.0 %collective-permute-done.5 = bf16[8,64,768]{2,1,0:T(8,128)(2,1)} collective-permute-done((bf16[8,64,768]{2,1,0:T(8,128)(2,1)}, bf16[8,64,768]{2,1,0:T(8,128)(2,1)}, u32[]{:S(2)}, u32[]{:S(2)}) %collective-permute-start.5) | collective-permute-done | bytes 786464 | tf_op jit(solution)/shard_map/ppermute | solution.py:513
  788.6 70.5 %conditional.20 = (f32[768]{0:T(1024)S(1)}, f32[768]{0:T(1024)S(1)}, f32[768]{0:T(1024)S(1)}, f32[768]{0:T(1024)S(1)}, bf16[8,64,2304]{2,1,0:T(8,128)(2,1)}, /*i...) conditional(s32[]{:T(128)} %convert_element_type.1093, ...), branch_computations={%region_80.81_spmd, %region_81.91_spmd} | conditional | flops 7580408832 | bytes 117301536 | solution.py:31
  789.7 19.1 %fusion.303 = bf16[8,64,3072]{2,1,0:T(8,128)(2,1)} fusion(f32[8,64,3072]{2,1,0:T(8,128)} %get-tuple-element.595, bf16[8,64,768]{2,1,0:T(8,128)(2,1)} %convert_element_type.812, bf16[3072,768]{1,0:T(8,128)(2,1)} %get-tuple-element.596), kind=kOutput, calls=%fused_computation.519 | convolution fusion | flops 2529165312 | bytes 14942208 | tf_op jit(solution)/shard_map/cond/branch_1_fun/...e,de->...d/dot_general | solution.py:62
  861.9 46.3 %conditional.23 = (bf16[16,48,2304]{2,1,0:T(8,128)(2,1)S(1)}, bf16[16,48,768]{2,1,0:T(8,128)(2,1)}, bf16[16,48,3072]{2,1,0:T(8,128)(2,1)}, bf16[16,192]{1,0:T(8,...) conditional(s32[]{:T(128)} %convert_element_type.1093, () %tuple.171, ...), branch_computations={%region_99.100_spmd, %region_100.0_spmd} | conditional | flops 14519103488 | bytes 56676920 | solution.py:31
  861.9 9.1 bitcast_convert_fusion.6
  879.5 9.6 bitcast_convert_fusion.7
  911.3 22.1 %concatenate.159 = bf16[16,48,9472]{2,1,0:T(8,128)(2,1)} concatenate(bf16[16,48,2304]{2,1,0:T(8,128)(2,1)S(1)} %get-tuple-element.977, bf16[16,48,768]{2,1,0:T(8,128)(2,1)} %get-tuple-element.978, bf16[16,48,3072]{2,1,0:T(8,128)(2,1)} %get-tuple-element.979, bf16[16,48,3072]{2,1,0:T(8,128)(2,1)} %get-tuple-element.980, bf16[16,48,9]{2,1,0:T(8,128)(2,1)} %reshape.1069, ...), dimensions={2} | concatenate | bytes 29097984 | tf_op jit(solution)/shard_map/concatenate | solution.py:376
  946.0 31.6 %concatenate.157 = bf16[16,48,12544]{2,1,0:T(8,128)(2,1)} concatenate(bf16[16,48,2304]{2,1,0:T(8,128)(2,1)} %get-tuple-element.940, bf16[16,48,768]{2,1,0:T(8,128)(2,1)} %get-tuple-element.941, bf16[16,48,3072]{2,1,0:T(8,128)(2,1)} %get-tuple-element.942, bf16[16,48,3072]{2,1,0:T(8,128)(2,1)} %get-tuple-element.943, bf16[16,48,768]{2,1,0:T(8,128)(2,1)} %get-tuple-element.944, ...), dimensions={2} | concatenate | bytes 38535168 | tf_op jit(solution)/shard_map/concatenate | solution.py:376
  986.0 11.5 fusion.419
  1013.9 58.3 %collective-permute-done.9 = f32[288,768]{1,0:T(8,128)S(1)} collective-permute-done((f32[288,768]{1,0:T(8,128)S(1)}, f32[288,768]{1,0:T(8,128)S(1)}, u32[]{:S(2)}, u32[]{:S(2)}) %collective-permute-start.9) | collective-permute-done | bytes 884768 | tf_op jit(solution)/shard_map/ppermute | solution.py:549
  1230.8 14.8 %collective-permute-done.71 = f32[48]{0:T(128)S(1)} collective-permute-done((f32[48]{0:T(128)S(1)}, f32[48]{0:T(128)S(1)}, u32[]{:S(2)}, u32[]{:S(2)}) %collective-permute-start.71) | collective-permute-done | bytes 224 | tf_op jit(solution)/shard_map/ppermute | solution.py:596
  (622 shorter events, 609.9 us)
Async XLA Ops:
  0.7 14.6 %collective-permute-start.2 = (bf16[288,768]{1,0:T(8,128)(2,1)}, bf16[288,768]{1,0:T(8,128)(2,1)S(1)}, u32[]{:S(2)}, u32[]{:S(2)}) collective-permute-start(bf16[288,768]{1,0:T(8,128)(2,1)} %bitcast.743), channel_id=1, source_target_pairs={{0,16},{1,17},{2,18},{3,19},{4,20},{5,21},{6,22},{7,23},{8,24},{9,... | collective-permute-start | bytes 1327112 | tf_op jit(solution)/shard_map/ppermute | solution.py:435
  19.9 186.0 %collective-permute-start.3 = (bf16[576,1536]{1,0:T(8,128)(2,1)}, bf16[576,1536]{1,0:T(8,128)(2,1)}, u32[]{:S(2)}, u32[]{:S(2)}) collective-permute-start(bf16[576,1536]{1,0:T(8,128)(2,1)} %get-tuple-element.836), channel_id=1, source_target_pairs={{0,1},{1,2},{2,3},{3,4},{4,5},{5,6},{6,7},{7,8},{8,9},{9,10},{10,1... | collective-permute-start | bytes 5308424 | tf_op jit(solution)/shard_map/ppermute | solution.py:444
  20.0 185.9 %collective-permute-start.4 = (bf16[576,1536]{1,0:T(8,128)(2,1)}, bf16[576,1536]{1,0:T(8,128)(2,1)}, u32[]{:S(2)}, u32[]{:S(2)}) collective-permute-start(bf16[576,1536]{1,0:T(8,128)(2,1)} %get-tuple-element.836), channel_id=1, source_target_pairs={{1,0},{2,1},{3,2},{4,3},{5,4},{6,5},{7,6},{8,7},{9,8},{10,9},{11,1... | collective-permute-start | bytes 5308424 | tf_op jit(solution)/shard_map/ppermute | solution.py:445
  96.4 115.4 %collective-permute-start.1 = (bf16[8,64,768]{2,1,0:T(8,128)(2,1)}, bf16[8,64,768]{2,1,0:T(8,128)(2,1)}, u32[]{:S(2)}, u32[]{:S(2)}) collective-permute-start(bf16[8,64,768]{2,1,0:T(8,128)(2,1)} %convert_element_type.1097), channel_id=1, source_target_pairs={{0,16},{1,17},{2,18},{3,19},{4,20},{5,21},{6,22},{7,23},{8,24},{9,... | collective-permute-start | bytes 2359304 | tf_op jit(solution)/shard_map/ppermute | solution.py:478
  168.2 100.5 %collective-permute-start = (bf16[8,64,768]{2,1,0:T(8,128)(2,1)}, bf16[8,64,768]{2,1,0:T(8,128)(2,1)}, u32[]{:S(2)}, u32[]{:S(2)}) collective-permute-start(bf16[8,64,768]{2,1,0:T(8,128)(2,1)} %convert_element_type.1095), channel_id=1, source_target_pairs={{0,16},{1,17},{2,18},{3,19},{4,20},{5,21},{6,22},{7,23},{8,24},{9,... | collective-permute-start | bytes 2359304 | tf_op jit(solution)/shard_map/ppermute | solution.py:478
  267.4 196.7 %collective-permute-start.6 = (bf16[8,64,768]{2,1,0:T(8,128)(2,1)}, bf16[8,64,768]{2,1,0:T(8,128)(2,1)}, u32[]{:S(2)}, u32[]{:S(2)}) collective-permute-start(bf16[8,64,768]{2,1,0:T(8,128)(2,1)} %convert_element_type.1102), channel_id=1, source_target_pairs={{16,0},{17,1},{18,2},{19,3},{20,4},{21,5},{22,6},{23,7},{24,8},{25... | collective-permute-start | bytes 2359304 | tf_op jit(solution)/shard_map/ppermute | solution.py:513
  328.2 458.5 %collective-permute-start.5 = (bf16[8,64,768]{2,1,0:T(8,128)(2,1)}, bf16[8,64,768]{2,1,0:T(8,128)(2,1)}, u32[]{:S(2)}, u32[]{:S(2)}) collective-permute-start(bf16[8,64,768]{2,1,0:T(8,128)(2,1)} %convert_element_type.1100), channel_id=1, source_target_pairs={{16,0},{17,1},{18,2},{19,3},{20,4},{21,5},{22,6},{23,7},{24,8},{25... | collective-permute-start | bytes 2359304 | tf_op jit(solution)/shard_map/ppermute | solution.py:513
  340.7 600.2 %collective-permute-start.7 = (bf16[576,1536]{1,0:T(8,128)(2,1)}, bf16[576,1536]{1,0:T(8,128)(2,1)}, u32[]{:S(2)}, u32[]{:S(2)}) collective-permute-start(bf16[576,1536]{1,0:T(8,128)(2,1)} %get-tuple-element.1503), channel_id=1, source_target_pairs={{1,0},{2,1},{3,2},{4,3},{5,4},{6,5},{7,6},{8,7},{9,8},{10,9},{11,1... | collective-permute-start | bytes 5308424 | tf_op jit(solution)/shard_map/ppermute | solution.py:538
  341.0 600.0 %collective-permute-start.8 = (bf16[576,1536]{1,0:T(8,128)(2,1)}, bf16[576,1536]{1,0:T(8,128)(2,1)}, u32[]{:S(2)}, u32[]{:S(2)}) collective-permute-start(bf16[576,1536]{1,0:T(8,128)(2,1)} %get-tuple-element.1504), channel_id=1, source_target_pairs={{0,1},{1,2},{2,3},{3,4},{4,5},{5,6},{6,7},{7,8},{8,9},{9,10},{10,1... | collective-permute-start | bytes 5308424 | tf_op jit(solution)/shard_map/ppermute | solution.py:539
  985.3 26.8 %collective-permute-start.10 = (bf16[48,6272]{1,0:T(8,128)(2,1)S(1)}, bf16[48,6272]{1,0:T(8,128)(2,1)S(1)}, u32[]{:S(2)}, u32[]{:S(2)}) collective-permute-start(bf16[48,6272]{1,0:T(8,128)(2,1)S(1)} %dynamic-slice_bitcast_fusion.1), channel_id=1, source_target_pairs={{17,16},{18,17},{19,18},{22,19},{23,22},{26,23},{27,26},{30,27},{3... | collective-permute-start | bytes 1806344 | tf_op jit(solution)/shard_map/ppermute | solution.py:360
  999.6 13.4 %collective-permute-start.40 = (bf16[48,6272]{1,0:T(8,128)(2,1)S(1)}, bf16[48,6272]{1,0:T(8,128)(2,1)S(1)}, u32[]{:S(2)}, u32[]{:S(2)}) collective-permute-start(bf16[48,6272]{1,0:T(8,128)(2,1)S(1)} %dynamic-slice_bitcast_fusion), channel_id=1, source_target_pairs={{16,17},{17,18},{18,19},{19,22},{22,23},{23,26},{26,27},{27,30},{3... | collective-permute-start | bytes 1806344 | tf_op jit(solution)/shard_map/ppermute | solution.py:359
  1004.0 68.2 %collective-permute-start.9 = (f32[288,768]{1,0:T(8,128)S(1)}, f32[288,768]{1,0:T(8,128)S(1)}, u32[]{:S(2)}, u32[]{:S(2)}) collective-permute-start(f32[288,768]{1,0:T(8,128)S(1)} %slice.204), channel_id=1, source_target_pairs={{16,0},{17,1},{18,2},{19,3},{20,4},{21,5},{22,6},{23,7},{24,8},{25... | collective-permute-start | bytes 2654216 | tf_op jit(solution)/shard_map/ppermute | solution.py:549
  1005.5 68.7 %collective-permute-start.26 = (bf16[48,4736]{1,0:T(8,128)(2,1)S(1)}, bf16[48,4736]{1,0:T(8,128)(2,1)S(1)}, u32[]{:S(2)}, u32[]{:S(2)}) collective-permute-start(bf16[48,4736]{1,0:T(8,128)(2,1)S(1)} %fusion.381), channel_id=1, source_target_pairs={{1,0},{2,1},{3,2},{6,3},{7,6},{10,7},{11,10},{14,11},{15,14},{12,1... | collective-permute-start | bytes 1363976 | tf_op jit(solution)/shard_map/ppermute | solution.py:360
  1010.2 66.2 %collective-permute-start.56 = (bf16[48,4736]{1,0:T(8,128)(2,1)S(1)}, bf16[48,4736]{1,0:T(8,128)(2,1)S(1)}, u32[]{:S(2)}, u32[]{:S(2)}) collective-permute-start(bf16[48,4736]{1,0:T(8,128)(2,1)S(1)} %fusion.367), channel_id=1, source_target_pairs={{0,1},{1,2},{2,3},{3,6},{6,7},{7,10},{10,11},{11,14},{14,15},{15,1... | collective-permute-start | bytes 1363976 | tf_op jit(solution)/shard_map/ppermute | solution.py:359
  1012.3 66.6 %collective-permute-start.11 = (bf16[48,6272]{1,0:T(8,128)(2,1)S(1)}, bf16[48,6272]{1,0:T(8,128)(2,1)S(1)}, u32[]{:S(2)}, u32[]{:S(2)}) collective-permute-start(bf16[48,6272]{1,0:T(8,128)(2,1)S(1)} %fusion.353), channel_id=1, source_target_pairs={{17,16},{18,17},{19,18},{22,19},{23,22},{26,23},{27,26},{30,27},{3... | collective-permute-start | bytes 1806344 | tf_op jit(solution)/shard_map/ppermute | solution.py:360
  1013.1 66.6 %collective-permute-start.41 = (bf16[48,6272]{1,0:T(8,128)(2,1)S(1)}, bf16[48,6272]{1,0:T(8,128)(2,1)S(1)}, u32[]{:S(2)}, u32[]{:S(2)}) collective-permute-start(bf16[48,6272]{1,0:T(8,128)(2,1)S(1)} %fusion.339), channel_id=1, source_target_pairs={{16,17},{17,18},{18,19},{19,22},{22,23},{23,26},{26,27},{27,30},{3... | collective-permute-start | bytes 1806344 | tf_op jit(solution)/shard_map/ppermute | solution.py:359
  1088.8 20.2 %collective-permute-start.13 = (bf16[48,6272]{1,0:T(8,128)(2,1)S(1)}, bf16[48,6272]{1,0:T(8,128)(2,1)S(1)}, u32[]{:S(2)}, u32[]{:S(2)}) collective-permute-start(bf16[48,6272]{1,0:T(8,128)(2,1)S(1)} %fusion.351), channel_id=1, source_target_pairs={{17,16},{18,17},{19,18},{22,19},{23,22},{26,23},{27,26},{30,27},{3... | collective-permute-start | bytes 1806344 | tf_op jit(solution)/shard_map/ppermute | solution.py:360
  1089.7 20.2 %collective-permute-start.43 = (bf16[48,6272]{1,0:T(8,128)(2,1)S(1)}, bf16[48,6272]{1,0:T(8,128)(2,1)S(1)}, u32[]{:S(2)}, u32[]{:S(2)}) collective-permute-start(bf16[48,6272]{1,0:T(8,128)(2,1)S(1)} %fusion.337), channel_id=1, source_target_pairs={{16,17},{17,18},{18,19},{19,22},{22,23},{23,26},{26,27},{27,30},{3... | collective-permute-start | bytes 1806344 | tf_op jit(solution)/shard_map/ppermute | solution.py:359
  1129.5 20.2 %collective-permute-start.16 = (bf16[48,6272]{1,0:T(8,128)(2,1)S(1)}, bf16[48,6272]{1,0:T(8,128)(2,1)S(1)}, u32[]{:S(2)}, u32[]{:S(2)}) collective-permute-start(bf16[48,6272]{1,0:T(8,128)(2,1)S(1)} %fusion.348), channel_id=1, source_target_pairs={{17,16},{18,17},{19,18},{22,19},{23,22},{26,23},{27,26},{30,27},{3... | collective-permute-start | bytes 1806344 | tf_op jit(solution)/shard_map/ppermute | solution.py:360
  1130.4 20.2 %collective-permute-start.46 = (bf16[48,6272]{1,0:T(8,128)(2,1)S(1)}, bf16[48,6272]{1,0:T(8,128)(2,1)S(1)}, u32[]{:S(2)}, u32[]{:S(2)}) collective-permute-start(bf16[48,6272]{1,0:T(8,128)(2,1)S(1)} %fusion.334), channel_id=1, source_target_pairs={{16,17},{17,18},{18,19},{19,22},{22,23},{23,26},{26,27},{27,30},{3... | collective-permute-start | bytes 1806344 | tf_op jit(solution)/shard_map/ppermute | solution.py:359
  1170.2 20.2 %collective-permute-start.19 = (bf16[48,6272]{1,0:T(8,128)(2,1)S(1)}, bf16[48,6272]{1,0:T(8,128)(2,1)S(1)}, u32[]{:S(2)}, u32[]{:S(2)}) collective-permute-start(bf16[48,6272]{1,0:T(8,128)(2,1)S(1)} %fusion.345), channel_id=1, source_target_pairs={{17,16},{18,17},{19,18},{22,19},{23,22},{26,23},{27,26},{30,27},{3... | collective-permute-start | bytes 1806344 | tf_op jit(solution)/shard_map/ppermute | solution.py:360
  1171.0 20.2 %collective-permute-start.49 = (bf16[48,6272]{1,0:T(8,128)(2,1)S(1)}, bf16[48,6272]{1,0:T(8,128)(2,1)S(1)}, u32[]{:S(2)}, u32[]{:S(2)}) collective-permute-start(bf16[48,6272]{1,0:T(8,128)(2,1)S(1)} %fusion.331), channel_id=1, source_target_pairs={{16,17},{17,18},{18,19},{19,22},{22,23},{23,26},{26,27},{27,30},{3... | collective-permute-start | bytes 1806344 | tf_op jit(solution)/shard_map/ppermute | solution.py:359
  1227.4 29.2 %collective-permute-start.73 = (f32[48,1536]{1,0:T(8,128)S(1)}, f32[48,1536]{1,0:T(8,128)S(1)}, u32[]{:S(2)}, u32[]{:S(2)}) collective-permute-start(f32[48,1536]{1,0:T(8,128)S(1)} %slice.265), channel_id=1, source_target_pairs={{16,0},{17,1},{18,2},{19,3},{20,4},{21,5},{22,6},{23,7},{24,8},{25... | collective-permute-start | bytes 884744 | tf_op jit(solution)/shard_map/ppermute | solution.py:596
  1228.9 16.8 %collective-permute-start.71 = (f32[48]{0:T(128)S(1)}, f32[48]{0:T(128)S(1)}, u32[]{:S(2)}, u32[]{:S(2)}) collective-permute-start(f32[48]{0:T(128)S(1)} %slice.232), channel_id=1, source_target_pairs={{16,0},{17,1},{18,2},{19,3},{20,4},{21,5},{22,6},{23,7},{24,8},{25... | collective-permute-start | bytes 584 | tf_op jit(solution)/shard_map/ppermute | solution.py:596
  (126 other events, 3188.5 us)

commit v7 on v6

--- a/solution.py
+++ b/solution.py
@@ -9,7 +9,7 @@
 
 H = 12
 HD = 64
-MICRO = 2
+MICRO = 4
 
 EPS = 1e-05
 MASKED = -1e30

time: 1280 us -> 1620 us (1.27)
  waiting for transfers between devices: 428 us -> 548 us
  local copies, waits for them, and re-layouts: 281 us -> 378 us
  matrix products: 191 us -> 243 us
  other arithmetic: 114 us -> 161 us
  loops' own time: 35.1 us -> 53.9 us
    ppermute x2 -> x4, waiting for transfers between devices: 300 us -> 464 us  [per_device(): returned.append(lax.ppermute(bf(dh), 'section', [(1, 0)]))]
    another operation x81 -> x161, local copies, waits for them, and re-layouts: 91.4 us -> 166 us
    ppermute x1, waiting for transfers between devices: 58.3 us -> 14.3 us  [per_device(): ig_first = lax.ppermute(image_grad_full[:half], 'section', [(1, 0)])]
    convert_element_type x77 -> x91, other arithmetic: 56.4 us -> 83.6 us  [bf(): return x.astype(BF16)]
    dot_general x8 -> x16, matrix products: 62.4 us -> 85.1 us  [mm(): return jnp.einsum('...d,de->...e', a, w, preferred_element_type=F32)]
    dot_general x8 -> x16, matrix products: 68.9 us -> 88.2 us  [mm_t(): return jnp.einsum('...e,de->...d', g, w, preferred_element_type=F32)]
    another operation x12 -> x20, loops' own time: 35.1 us -> 53.9 us  [run_on(): return lax.cond(flag, fn, idle, *args)]
  transfers between devices with their start and end apart: 75 -> 79, of which waited for: 24 -> 25; matrix products, arithmetic and copies ran while one was open for 42% -> 45% of each run, Pallas kernels for 0% -> 0%
where the time goes in v7:
time: 1620 us; the launch traced here: 1600 us
  waiting for transfers between devices  548 us (34%)
  local copies, waits for them, and re-layouts  378 us (23%)
  matrix products  243 us (15%)
  other arithmetic  161 us (10%)
  starting transfers between devices  141 us (9%)
  between operations  78.9 us (5%)
  loops' own time  53.9 us (3%)
    ppermute x4, waiting for transfers between devices, per_device(): returned.append(lax.ppermute(bf(dh), 'section', [(1, 0)]))  464 us
    another operation x161, local copies, waits for them, and re-layouts  166 us
    dot_general x16, matrix products, mm_t(): return jnp.einsum('...e,de->...d', g, w, preferred_element_type=F32)  88.2 us
    dot_general x16, matrix products, mm(): return jnp.einsum('...d,de->...e', a, w, preferred_element_type=F32)  85.1 us
    convert_element_type x91, other arithmetic, bf(): return x.astype(BF16)  83.6 us
    ppermute x30, starting transfers between devices, ring_reduce_scatter(): got_w = lax.ppermute(send_w, axes, bwd)  67.8 us
    concatenate x2, local copies, waits for them, and re-layouts, pack_rows(): return jnp.concatenate(pieces, -1)  54.1 us
    another operation x20, loops' own time, run_on(): return lax.cond(flag, fn, idle, *args)  53.9 us
  transfers between devices with their start and end apart: 79, of which 25 were waited for; matrix products, arithmetic and copies ran while one was open for 45% of the time, Pallas kernels for 0%

profile of v7, /device:TPU:0, one launch (start us, length us, event | category | flops | bytes accessed | tf_op | source)
XLA Modules:
  0.0 1603.6 jit_solution(6413538546471680074)
XLA Ops:
  27.1 44.8 %conditional.20 = (f32[4,64,768]{2,1,0:T(8,128)S(1)}, bf16[4,64,12,64]{3,1,2,0:T(8,128)(2,1)S(1)}, bf16[4,64,768]{2,1,0:T(8,128)(2,1)S(1)}, f32[4,64,768]{2,1,0:...) conditional(s32[]{:T(128)} %convert_element_type.1325, ...), branch_computations={%region_0.0_spmd, %region_1.8_spmd} | conditional | flops 3732247040 | bytes 59931036 | solution.py:31
  77.2 49.6 %conditional.21 = (f32[4,64,768]{2,1,0:T(8,128)}, bf16[4,64,12,64]{3,1,2,0:T(8,128)(2,1)S(1)}, bf16[4,64,768]{2,1,0:T(8,128)(2,1)}, f32[4,64,768]{2,1,0:T(8,128)...) conditional(s32[]{:T(128)} %convert_element_type.1325, ...), branch_computations={%region_8.9_spmd, %region_9.16_spmd} | conditional | flops 3732247040 | bytes 63076740 | solution.py:31
  131.0 51.2 %conditional.24 = (f32[4,64,768]{2,1,0:T(8,128)}, bf16[4,64,12,64]{3,1,2,0:T(8,128)(2,1)}, bf16[4,64,768]{2,1,0:T(8,128)(2,1)}, f32[4,64,768]{2,1,0:T(8,128)}, f...) conditional(s32[]{:T(128)} %convert_element_type.1325, ...), branch_computations={%region_29.30_spmd, %region_30.37_spmd} | conditional | flops 3732247040 | bytes 56785200 | solution.py:31
  249.8 46.8 %conditional.26 = (f32[4,64,768]{2,1,0:T(8,128)}, bf16[4,64,12,64]{3,1,2,0:T(8,128)(2,1)}, bf16[4,64,768]{2,1,0:T(8,128)(2,1)S(1)}, f32[4,64,768]{2,1,0:T(8,128)...) conditional(s32[]{:T(128)} %convert_element_type.1325, ...), branch_computations={%region_47.48_spmd, %region_48.55_spmd} | conditional | flops 3732247040 | bytes 58370436 | solution.py:31
  331.9 24.7 %conditional.23 = (f32[4,64,768]{2,1,0:T(8,128)}, bf16[4,64,12,64]{3,1,2,0:T(8,128)(2,1)}, bf16[4,64,768]{2,1,0:T(8,128)(2,1)}, f32[4,64,768]{2,1,0:T(8,128)}, f...) conditional(s32[]{:T(128)} %convert_element_type.1328, ...), branch_computations={%region_19.20_spmd, %region_20.29_spmd} | conditional | flops 5245146112 | bytes 66075112 | solution.py:31
  356.6 23.6 %conditional.29 = (f32[4,64,768]{2,1,0:T(8,128)}, f32[768]{0:T(1024)}, f32[768]{0:T(1024)}, f32[768]{0:T(1024)}, f32[768]{0:T(1024)}, /*index=5*/f32[768]{0:T(10...) conditional(s32[]{:T(128)} %convert_element_type.1328, ...), branch_computations={%region_75.76_spmd, %region_76.90_spmd} | conditional | flops 6662053888 | bytes 87629288 | solution.py:31
  383.4 24.5 %conditional.25 = (f32[4,64,768]{2,1,0:T(8,128)}, bf16[4,64,12,64]{3,1,2,0:T(8,128)(2,1)}, bf16[4,64,768]{2,1,0:T(8,128)(2,1)}, f32[4,64,768]{2,1,0:T(8,128)}, f...) conditional(s32[]{:T(128)} %convert_element_type.1328, ...), branch_computations={%region_37.38_spmd, %region_38.47_spmd} | conditional | flops 5245146112 | bytes 66075112 | solution.py:31
  408.0 23.7 %conditional.30 = (f32[4,64,768]{2,1,0:T(8,128)}, f32[768]{0:T(1024)}, f32[768]{0:T(1024)}, f32[768]{0:T(1024)}, f32[768]{0:T(1024)}, /*index=5*/f32[768]{0:T(10...) conditional(s32[]{:T(128)} %convert_element_type.1328, ...), branch_computations={%region_90.91_spmd, %region_91.105_spmd} | conditional | flops 6662053888 | bytes 87629288 | solution.py:31
  433.6 24.3 %conditional.27 = (f32[4,64,768]{2,1,0:T(8,128)}, bf16[4,64,12,64]{3,1,2,0:T(8,128)(2,1)}, bf16[4,64,768]{2,1,0:T(8,128)(2,1)}, f32[4,64,768]{2,1,0:T(8,128)}, f...) conditional(s32[]{:T(128)} %convert_element_type.1328, ...), branch_computations={%region_55.56_spmd, %region_56.65_spmd} | conditional | flops 5245146112 | bytes 66075112 | solution.py:31
  458.0 23.4 %conditional.31 = (f32[4,64,768]{2,1,0:T(8,128)}, f32[768]{0:T(1024)}, f32[768]{0:T(1024)}, f32[768]{0:T(1024)}, f32[768]{0:T(1024)}, /*index=5*/f32[768]{0:T(10...) conditional(s32[]{:T(128)} %convert_element_type.1328, ...), branch_computations={%region_105.106_spmd, %region_106.120_spmd} | conditional | flops 6662053888 | bytes 87629288 | solution.py:31
  483.4 24.4 %conditional.28 = (bf16[4,64,12,64]{3,1,2,0:T(8,128)(2,1)}, bf16[4,64,768]{2,1,0:T(8,128)(2,1)}, f32[4,64,768]{2,1,0:T(8,128)}, f32[4,64,1]{1,0,2:T(4,128)}, bf1...) conditional(s32[]{:T(128)} %convert_element_type.1328, ...), branch_computations={%region_65.66_spmd, %region_66.75_spmd} | conditional | flops 5245146112 | bytes 66075112 | solution.py:31
  507.8 28.0 %conditional.32 = (f32[4,64,768]{2,1,0:T(8,128)}, f32[768]{0:T(1024)}, f32[768]{0:T(1024)}, f32[768]{0:T(1024)}, f32[768]{0:T(1024)}, /*index=5*/f32[768]{0:T(10...) conditional(s32[]{:T(128)} %convert_element_type.1328, ...), branch_computations={%region_120.121_spmd, %region_121.135_spmd} | conditional | flops 6662053888 | bytes 82898472 | solution.py:31
  542.6 14.7 add_convert_fusion.20
  565.4 21.8 %conditional.38 = (bf16[16,48,2304]{2,1,0:T(8,128)(2,1)}, bf16[16,48,768]{2,1,0:T(8,128)(2,1)}, bf16[16,48,3072]{2,1,0:T(8,128)(2,1)}, bf16[16,192]{1,0:T(8,128)...) conditional(s32[]{:T(128)} %convert_element_type.1328, ...), branch_computations={%region_181.182_spmd, %region_182.191_spmd} | conditional | flops 16970804224 | bytes 65358408 | solution.py:31
  591.4 45.5 %conditional.33 = (f32[4,64,768]{2,1,0:T(8,128)}, f32[768]{0:T(1024)S(1)}, f32[768]{0:T(1024)}, f32[768]{0:T(1024)}, f32[768]{0:T(1024)}, /*index=5*/bf16[4,64,2...) conditional(s32[]{:T(128)} %convert_element_type.1325, ...), branch_computations={%region_135.136_spmd, %region_136.146_spmd} | conditional | flops 3790399488 | bytes 61823256 | solution.py:31
  636.9 450.7 %collective-permute-done.10 = bf16[4,64,768]{2,1,0:T(8,128)(2,1)} collective-permute-done((bf16[4,64,768]{2,1,0:T(8,128)(2,1)}, bf16[4,64,768]{2,1,0:T(8,128)(2,1)}, u32[]{:S(2)}, u32[]{:S(2)}) %collective-permute-start.10) | collective-permute-done | bytes 393248 | tf_op jit(solution)/shard_map/ppermute | solution.py:513
  1104.3 46.5 %conditional.34 = (f32[4,64,768]{2,1,0:T(8,128)}, f32[768]{0:T(1024)}, f32[768]{0:T(1024)}, f32[768]{0:T(1024)}, f32[768]{0:T(1024)}, /*index=5*/bf16[4,64,2304]...) conditional(s32[]{:T(128)} %convert_element_type.1325, ...), branch_computations={%region_146.147_spmd, %region_147.157_spmd} | conditional | flops 3790202880 | bytes 55531744 | solution.py:31
  1150.8 46.7 %conditional.35 = (f32[4,64,768]{2,1,0:T(8,128)}, f32[768]{0:T(1024)}, f32[768]{0:T(1024)}, f32[768]{0:T(1024)}, f32[768]{0:T(1024)}, /*index=5*/bf16[4,64,2304]...) conditional(s32[]{:T(128)} %convert_element_type.1325, ...), branch_computations={%region_157.158_spmd, %region_158.168_spmd} | conditional | flops 3790202880 | bytes 68106488 | solution.py:31
  1197.5 43.4 %conditional.36 = (f32[768]{0:T(1024)}, f32[768]{0:T(1024)}, f32[768]{0:T(1024)}, f32[768]{0:T(1024)}, bf16[4,64,2304]{2,1,0:T(8,128)(2,1)}, /*index=5*/bf16[4,6...) conditional(s32[]{:T(128)} %convert_element_type.1325, ...), branch_computations={%region_168.169_spmd, %region_169.179_spmd} | conditional | flops 3790202880 | bytes 68114744 | solution.py:31
  1244.6 49.3 %conditional.39 = (bf16[16,48,2304]{2,1,0:T(8,128)(2,1)}, bf16[16,48,768]{2,1,0:T(8,128)(2,1)S(1)}, bf16[16,48,3072]{2,1,0:T(8,128)(2,1)}, bf16[16,192]{1,0:T(8,...) conditional(s32[]{:T(128)} %convert_element_type.1325, () %tuple.267, ...), branch_computations={%region_191.192_spmd, %region_192.201_spmd} | conditional | flops 14544268288 | bytes 75582256 | solution.py:31
  1295.2 22.6 %concatenate.183 = bf16[16,48,9472]{2,1,0:T(8,128)(2,1)} concatenate(bf16[16,48,2304]{2,1,0:T(8,128)(2,1)} %get-tuple-element.1881, bf16[16,48,768]{2,1,0:T(8,128)(2,1)} %copy-done.53, bf16[16,48,3072]{2,1,0:T(8,128)(2,1)} %get-tuple-element.1883, bf16[16,48,3072]{2,1,0:T(8,128)(2,1)} %get-tuple-element.1884, bf16[16,48,9]{2,1,0:T(8,128)(2,1)S(1)} %reshape.1695, ...), dimensions={2} | concatenate | bytes 29097984 | tf_op jit(solution)/shard_map/concatenate | solution.py:376
  1329.5 31.6 %concatenate.181 = bf16[16,48,12544]{2,1,0:T(8,128)(2,1)} concatenate(bf16[16,48,2304]{2,1,0:T(8,128)(2,1)} %get-tuple-element.1816, bf16[16,48,768]{2,1,0:T(8,128)(2,1)} %get-tuple-element.1817, bf16[16,48,3072]{2,1,0:T(8,128)(2,1)} %get-tuple-element.1818, bf16[16,48,3072]{2,1,0:T(8,128)(2,1)} %get-tuple-element.1819, bf16[16,48,768]{2,1,0:T(8,128)(2,1)} %get-tuple-element.1820, ...), dimensions={2} | concatenate | bytes 38535168 | tf_op jit(solution)/shard_map/concatenate | solution.py:376
  1397.3 14.3 collective-permute-done.13
  1570.3 15.8 collective-permute-done.75
  (872 shorter events, 925.6 us)
Async XLA Ops:
  20.0 303.8 %collective-permute-start.3 = (bf16[576,1536]{1,0:T(8,128)(2,1)}, bf16[576,1536]{1,0:T(8,128)(2,1)}, u32[]{:S(2)}, u32[]{:S(2)}) collective-permute-start(bf16[576,1536]{1,0:T(8,128)(2,1)} %get-tuple-element.1600), channel_id=1, source_target_pairs={{0,1},{1,2},{2,3},{3,4},{4,5},{5,6},{6,7},{7,8},{8,9},{9,10},{10,1... | collective-permute-start | bytes 5308424 | tf_op jit(solution)/shard_map/ppermute | solution.py:444
  20.0 305.8 %collective-permute-start.4 = (bf16[576,1536]{1,0:T(8,128)(2,1)}, bf16[576,1536]{1,0:T(8,128)(2,1)}, u32[]{:S(2)}, u32[]{:S(2)}) collective-permute-start(bf16[576,1536]{1,0:T(8,128)(2,1)} %get-tuple-element.1600), channel_id=1, source_target_pairs={{1,0},{2,1},{3,2},{4,3},{5,4},{6,5},{7,6},{8,7},{9,8},{10,9},{11,1... | collective-permute-start | bytes 5308424 | tf_op jit(solution)/shard_map/ppermute | solution.py:445
  72.8 259.1 %collective-permute-start.1 = (bf16[4,64,768]{2,1,0:T(8,128)(2,1)}, bf16[4,64,768]{2,1,0:T(8,128)(2,1)}, u32[]{:S(2)}, u32[]{:S(2)}) collective-permute-start(bf16[4,64,768]{2,1,0:T(8,128)(2,1)} %convert_element_type.1329), channel_id=1, source_target_pairs={{0,16},{1,17},{2,18},{3,19},{4,20},{5,21},{6,22},{7,23},{8,24},{9,... | collective-permute-start | bytes 1179656 | tf_op jit(solution)/shard_map/ppermute | solution.py:478
  129.0 254.4 %collective-permute-start = (bf16[4,64,768]{2,1,0:T(8,128)(2,1)}, bf16[4,64,768]{2,1,0:T(8,128)(2,1)}, u32[]{:S(2)}, u32[]{:S(2)}) collective-permute-start(bf16[4,64,768]{2,1,0:T(8,128)(2,1)} %convert_element_type.1327), channel_id=1, source_target_pairs={{0,16},{1,17},{2,18},{3,19},{4,20},{5,21},{6,22},{7,23},{8,24},{9,... | collective-permute-start | bytes 1179656 | tf_op jit(solution)/shard_map/ppermute | solution.py:478
  184.3 249.3 %collective-permute-start.5 = (bf16[4,64,768]{2,1,0:T(8,128)(2,1)}, bf16[4,64,768]{2,1,0:T(8,128)(2,1)}, u32[]{:S(2)}, u32[]{:S(2)}) collective-permute-start(bf16[4,64,768]{2,1,0:T(8,128)(2,1)} %convert_element_type.1331), channel_id=1, source_target_pairs={{0,16},{1,17},{2,18},{3,19},{4,20},{5,21},{6,22},{7,23},{8,24},{9,... | collective-permute-start | bytes 1179656 | tf_op jit(solution)/shard_map/ppermute | solution.py:478
  323.8 159.5 %collective-permute-start.6 = (bf16[4,64,768]{2,1,0:T(8,128)(2,1)}, bf16[4,64,768]{2,1,0:T(8,128)(2,1)}, u32[]{:S(2)}, u32[]{:S(2)}) collective-permute-start(bf16[4,64,768]{2,1,0:T(8,128)(2,1)} %convert_element_type.1332), channel_id=1, source_target_pairs={{0,16},{1,17},{2,18},{3,19},{4,20},{5,21},{6,22},{7,23},{8,24},{9,... | collective-permute-start | bytes 1179656 | tf_op jit(solution)/shard_map/ppermute | solution.py:478
  382.1 178.9 %collective-permute-start.8 = (bf16[4,64,768]{2,1,0:T(8,128)(2,1)}, bf16[4,64,768]{2,1,0:T(8,128)(2,1)}, u32[]{:S(2)}, u32[]{:S(2)}) collective-permute-start(bf16[4,64,768]{2,1,0:T(8,128)(2,1)} %convert_element_type.1336), channel_id=1, source_target_pairs={{16,0},{17,1},{18,2},{19,3},{20,4},{21,5},{22,6},{23,7},{24,8},{25... | collective-permute-start | bytes 1179656 | tf_op jit(solution)/shard_map/ppermute | solution.py:513
  537.8 549.8 %collective-permute-start.10 = (bf16[4,64,768]{2,1,0:T(8,128)(2,1)}, bf16[4,64,768]{2,1,0:T(8,128)(2,1)}, u32[]{:S(2)}, u32[]{:S(2)}) collective-permute-start(bf16[4,64,768]{2,1,0:T(8,128)(2,1)} %convert_element_type.1340), channel_id=1, source_target_pairs={{16,0},{17,1},{18,2},{19,3},{20,4},{21,5},{22,6},{23,7},{24,8},{25... | collective-permute-start | bytes 1179656 | tf_op jit(solution)/shard_map/ppermute | solution.py:513
  539.1 556.9 %collective-permute-start.9 = (bf16[4,64,768]{2,1,0:T(8,128)(2,1)}, bf16[4,64,768]{2,1,0:T(8,128)(2,1)}, u32[]{:S(2)}, u32[]{:S(2)}) collective-permute-start(bf16[4,64,768]{2,1,0:T(8,128)(2,1)} %convert_element_type.1338), channel_id=1, source_target_pairs={{16,0},{17,1},{18,2},{19,3},{20,4},{21,5},{22,6},{23,7},{24,8},{25... | collective-permute-start | bytes 1179656 | tf_op jit(solution)/shard_map/ppermute | solution.py:513
  540.4 560.5 %collective-permute-start.7 = (bf16[4,64,768]{2,1,0:T(8,128)(2,1)}, bf16[4,64,768]{2,1,0:T(8,128)(2,1)}, u32[]{:S(2)}, u32[]{:S(2)}) collective-permute-start(bf16[4,64,768]{2,1,0:T(8,128)(2,1)} %convert_element_type.1334), channel_id=1, source_target_pairs={{16,0},{17,1},{18,2},{19,3},{20,4},{21,5},{22,6},{23,7},{24,8},{25... | collective-permute-start | bytes 1179656 | tf_op jit(solution)/shard_map/ppermute | solution.py:513
  560.7 763.8 %collective-permute-start.11 = (bf16[576,1536]{1,0:T(8,128)(2,1)}, bf16[576,1536]{1,0:T(8,128)(2,1)}, u32[]{:S(2)}, u32[]{:S(2)}) collective-permute-start(bf16[576,1536]{1,0:T(8,128)(2,1)} %get-tuple-element.2917), channel_id=1, source_target_pairs={{1,0},{2,1},{3,2},{4,3},{5,4},{6,5},{7,6},{8,7},{9,8},{10,9},{11,1... | collective-permute-start | bytes 5308424 | tf_op jit(solution)/shard_map/ppermute | solution.py:538
  561.0 763.5 %collective-permute-start.12 = (bf16[576,1536]{1,0:T(8,128)(2,1)}, bf16[576,1536]{1,0:T(8,128)(2,1)}, u32[]{:S(2)}, u32[]{:S(2)}) collective-permute-start(bf16[576,1536]{1,0:T(8,128)(2,1)} %get-tuple-element.2918), channel_id=1, source_target_pairs={{0,1},{1,2},{2,3},{3,4},{4,5},{5,6},{6,7},{7,8},{8,9},{9,10},{10,1... | collective-permute-start | bytes 5308424 | tf_op jit(solution)/shard_map/ppermute | solution.py:539
  1368.8 26.8 %collective-permute-start.14 = (bf16[48,6272]{1,0:T(8,128)(2,1)S(1)}, bf16[48,6272]{1,0:T(8,128)(2,1)S(1)}, u32[]{:S(2)}, u32[]{:S(2)}) collective-permute-start(bf16[48,6272]{1,0:T(8,128)(2,1)S(1)} %dynamic-slice_bitcast_fusion.1), channel_id=1, source_target_pairs={{17,16},{18,17},{19,18},{22,19},{23,22},{26,23},{27,26},{30,27},{3... | collective-permute-start | bytes 1806344 | tf_op jit(solution)/shard_map/ppermute | solution.py:360
  1387.4 24.2 %collective-permute-start.13 = (f32[288,768]{1,0:T(8,128)S(1)}, f32[288,768]{1,0:T(8,128)S(1)}, u32[]{:S(2)}, u32[]{:S(2)}) collective-permute-start(f32[288,768]{1,0:T(8,128)S(1)} %slice.296), channel_id=1, source_target_pairs={{16,0},{17,1},{18,2},{19,3},{20,4},{21,5},{22,6},{23,7},{24,8},{25... | collective-permute-start | bytes 2654216 | tf_op jit(solution)/shard_map/ppermute | solution.py:549
  1389.0 24.8 %collective-permute-start.30 = (bf16[48,4736]{1,0:T(8,128)(2,1)S(1)}, bf16[48,4736]{1,0:T(8,128)(2,1)S(1)}, u32[]{:S(2)}, u32[]{:S(2)}) collective-permute-start(bf16[48,4736]{1,0:T(8,128)(2,1)S(1)} %fusion.690), channel_id=1, source_target_pairs={{1,0},{2,1},{3,2},{6,3},{7,6},{10,7},{11,10},{14,11},{15,14},{12,1... | collective-permute-start | bytes 1363976 | tf_op jit(solution)/shard_map/ppermute | solution.py:360
  1393.6 22.2 %collective-permute-start.60 = (bf16[48,4736]{1,0:T(8,128)(2,1)S(1)}, bf16[48,4736]{1,0:T(8,128)(2,1)S(1)}, u32[]{:S(2)}, u32[]{:S(2)}) collective-permute-start(bf16[48,4736]{1,0:T(8,128)(2,1)S(1)} %fusion.676), channel_id=1, source_target_pairs={{0,1},{1,2},{2,3},{3,6},{6,7},{7,10},{10,11},{11,14},{14,15},{15,1... | collective-permute-start | bytes 1363976 | tf_op jit(solution)/shard_map/ppermute | solution.py:359
  1395.7 22.7 %collective-permute-start.15 = (bf16[48,6272]{1,0:T(8,128)(2,1)S(1)}, bf16[48,6272]{1,0:T(8,128)(2,1)S(1)}, u32[]{:S(2)}, u32[]{:S(2)}) collective-permute-start(bf16[48,6272]{1,0:T(8,128)(2,1)S(1)} %fusion.662), channel_id=1, source_target_pairs={{17,16},{18,17},{19,18},{22,19},{23,22},{26,23},{27,26},{30,27},{3... | collective-permute-start | bytes 1806344 | tf_op jit(solution)/shard_map/ppermute | solution.py:360
  1396.6 22.7 %collective-permute-start.45 = (bf16[48,6272]{1,0:T(8,128)(2,1)S(1)}, bf16[48,6272]{1,0:T(8,128)(2,1)S(1)}, u32[]{:S(2)}, u32[]{:S(2)}) collective-permute-start(bf16[48,6272]{1,0:T(8,128)(2,1)S(1)} %fusion.648), channel_id=1, source_target_pairs={{16,17},{17,18},{18,19},{19,22},{22,23},{23,26},{26,27},{27,30},{3... | collective-permute-start | bytes 1806344 | tf_op jit(solution)/shard_map/ppermute | solution.py:359
  1428.4 20.1 %collective-permute-start.17 = (bf16[48,6272]{1,0:T(8,128)(2,1)S(1)}, bf16[48,6272]{1,0:T(8,128)(2,1)S(1)}, u32[]{:S(2)}, u32[]{:S(2)}) collective-permute-start(bf16[48,6272]{1,0:T(8,128)(2,1)S(1)} %fusion.660), channel_id=1, source_target_pairs={{17,16},{18,17},{19,18},{22,19},{23,22},{26,23},{27,26},{30,27},{3... | collective-permute-start | bytes 1806344 | tf_op jit(solution)/shard_map/ppermute | solution.py:360
  1469.0 20.2 %collective-permute-start.20 = (bf16[48,6272]{1,0:T(8,128)(2,1)S(1)}, bf16[48,6272]{1,0:T(8,128)(2,1)S(1)}, u32[]{:S(2)}, u32[]{:S(2)}) collective-permute-start(bf16[48,6272]{1,0:T(8,128)(2,1)S(1)} %fusion.657), channel_id=1, source_target_pairs={{17,16},{18,17},{19,18},{22,19},{23,22},{26,23},{27,26},{30,27},{3... | collective-permute-start | bytes 1806344 | tf_op jit(solution)/shard_map/ppermute | solution.py:360
  1469.9 20.2 %collective-permute-start.50 = (bf16[48,6272]{1,0:T(8,128)(2,1)S(1)}, bf16[48,6272]{1,0:T(8,128)(2,1)S(1)}, u32[]{:S(2)}, u32[]{:S(2)}) collective-permute-start(bf16[48,6272]{1,0:T(8,128)(2,1)S(1)} %fusion.643), channel_id=1, source_target_pairs={{16,17},{17,18},{18,19},{19,22},{22,23},{23,26},{26,27},{27,30},{3... | collective-permute-start | bytes 1806344 | tf_op jit(solution)/shard_map/ppermute | solution.py:359
  1509.7 20.2 %collective-permute-start.23 = (bf16[48,6272]{1,0:T(8,128)(2,1)S(1)}, bf16[48,6272]{1,0:T(8,128)(2,1)S(1)}, u32[]{:S(2)}, u32[]{:S(2)}) collective-permute-start(bf16[48,6272]{1,0:T(8,128)(2,1)S(1)} %fusion.654), channel_id=1, source_target_pairs={{17,16},{18,17},{19,18},{22,19},{23,22},{26,23},{27,26},{30,27},{3... | collective-permute-start | bytes 1806344 | tf_op jit(solution)/shard_map/ppermute | solution.py:360
  1510.6 20.2 %collective-permute-start.53 = (bf16[48,6272]{1,0:T(8,128)(2,1)S(1)}, bf16[48,6272]{1,0:T(8,128)(2,1)S(1)}, u32[]{:S(2)}, u32[]{:S(2)}) collective-permute-start(bf16[48,6272]{1,0:T(8,128)(2,1)S(1)} %fusion.640), channel_id=1, source_target_pairs={{16,17},{17,18},{18,19},{19,22},{22,23},{23,26},{26,27},{27,30},{3... | collective-permute-start | bytes 1806344 | tf_op jit(solution)/shard_map/ppermute | solution.py:359
  1566.9 30.1 %collective-permute-start.77 = (f32[48,1536]{1,0:T(8,128)S(1)}, f32[48,1536]{1,0:T(8,128)S(1)}, u32[]{:S(2)}, u32[]{:S(2)}) collective-permute-start(f32[48,1536]{1,0:T(8,128)S(1)} %slice.375), channel_id=1, source_target_pairs={{16,0},{17,1},{18,2},{19,3},{20,4},{21,5},{22,6},{23,7},{24,8},{25... | collective-permute-start | bytes 884744 | tf_op jit(solution)/shard_map/ppermute | solution.py:596
  (155 other events, 2345.6 us)

commit v8 on v6

--- a/solution.py
+++ b/solution.py
@@ -122,10 +122,25 @@
     return lax.dot_general(a, b, (((1,), (0,)), ((), ())), preferred_element_type=F32)
 
 
+LO = 16
+HI = 48
+
+
+def _join(top, bottom, first):
+    t = first.shape[0]
+    mid = jnp.where(first[LO:HI], top[LO:HI], bottom[: HI - LO])
+    return jnp.concatenate([top[:LO], mid, bottom[HI - LO :]], 0)
+
+
+def _split(x, first):
+    zero = jnp.zeros_like(x)
+    return jnp.where(first, x, zero)[:HI], jnp.where(first, zero, x)[LO:]
+
+
 def _probs(q, ka, kb, first):
-    sa = _dot_nt(q, ka) * SCALE
-    sb = _dot_nt(q, kb) * SCALE
-    s = jnp.where(first, sa, sb)
+    sa = _dot_nt(q[:HI], ka) * SCALE
+    sb = _dot_nt(q[LO:], kb) * SCALE
+    s = _join(sa, sb, first)
     top = jnp.max(s, -1, keepdims=True)
     e = jnp.exp(s - top)
     return e / jnp.sum(e, -1, keepdims=True)
@@ -145,10 +160,10 @@
             vcols = pl.ds(d + h * HD, HD)
             q = q_ref[j, :, cols]
             p = _probs(q, pool_ref[a, :, cols], pool_ref[b, :, cols], first).astype(BF16)
-            zero = jnp.zeros_like(p)
-            o = _dot(jnp.where(first, p, zero), pool_ref[a, :, vcols]) + _dot(
-                jnp.where(first, zero, p), pool_ref[b, :, vcols]
-            )
+            pa, pb = _split(p, first)
+            oa = _dot(pa, pool_ref[a, :, vcols])
+            ob = _dot(pb, pool_ref[b, :, vcols])
+            o = jnp.concatenate([oa[:LO], oa[LO:] + ob[: HI - LO], ob[HI - LO :]], 0)
             o_ref[j, :, cols] = o.astype(o_ref.dtype)
 
 
@@ -176,20 +191,18 @@
             va = pool_ref[a, :, vcols]
             vb = pool_ref[b, :, vcols]
             p = _probs(q, ka, kb, first)
-            dp = jnp.where(first, _dot_nt(do, va), _dot_nt(do, vb))
+            dp = _join(_dot_nt(do[:HI], va), _dot_nt(do[LO:], vb), first)
             ds = (p * (dp - jnp.sum(p * dp, -1, keepdims=True))).astype(BF16)
-            zero = jnp.zeros_like(ds)
-            dsa = jnp.where(first, ds, zero)
-            dsb = jnp.where(first, zero, ds)
-            dq = (_dot(dsa, ka) + _dot(dsb, kb)) * SCALE
+            dsa, dsb = _split(ds, first)
+            dqa = _dot(dsa, ka)
+            dqb = _dot(dsb, kb)
+            dq = jnp.concatenate([dqa[:LO], dqa[LO:] + dqb[: HI - LO], dqb[HI - LO :]], 0) * SCALE
             dq_ref[j, :, cols] = dq.astype(dq_ref.dtype)
-            pb = p.astype(BF16)
-            pa_ = jnp.where(first, pb, zero)
-            pb_ = jnp.where(first, zero, pb)
-            dpool_ref[a, :, cols] += _dot_tn(dsa, q) * SCALE
-            dpool_ref[a, :, vcols] += _dot_tn(pa_, do)
-            dpool_ref[b, :, cols] += _dot_tn(dsb, q) * SCALE
-            dpool_ref[b, :, vcols] += _dot_tn(pb_, do)
+            pa, pb = _split(p.astype(BF16), first)
+            dpool_ref[a, :, cols] += _dot_tn(dsa, q[:HI]) * SCALE
+            dpool_ref[a, :, vcols] += _dot_tn(pa, do[:HI])
+            dpool_ref[b, :, cols] += _dot_tn(dsb, q[LO:]) * SCALE
+            dpool_ref[b, :, vcols] += _dot_tn(pb, do[LO:])
 
 
 def cross_attention_fwd(qc, pool, slots, cuts):

time: 1280 us -> 1250 us (0.977)
  waiting for transfers between devices: 428 us -> 405 us
    ppermute x2, waiting for transfers between devices: 300 us -> 277 us  [per_device(): returned.append(lax.ppermute(bf(dh), 'section', [(1, 0)]))]
  transfers between devices with their start and end apart: 75 -> 75, of which waited for: 24 -> 24; matrix products, arithmetic and copies ran while one was open for 42% -> 43% of each run, Pallas kernels for 0% -> 0%
where the time goes in v8:
time: 1250 us; the launch traced here: 1240 us
  waiting for transfers between devices  405 us (32%)
  local copies, waits for them, and re-layouts  281 us (22%)
  matrix products  192 us (15%)
  starting transfers between devices  134 us (11%)
  other arithmetic  114 us (9%)
  between operations  79.8 us (6%)
  loops' own time  35.1 us (3%)
    ppermute x2, waiting for transfers between devices, per_device(): returned.append(lax.ppermute(bf(dh), 'section', [(1, 0)]))  277 us
    another operation x81, local copies, waits for them, and re-layouts  91.4 us
    dot_general x8, matrix products, mm_t(): return jnp.einsum('...e,de->...d', g, w, preferred_element_type=F32)  69 us
    ppermute x30, starting transfers between devices, ring_reduce_scatter(): got_w = lax.ppermute(send_w, axes, bwd)  67.8 us
    dot_general x8, matrix products, mm(): return jnp.einsum('...d,de->...e', a, w, preferred_element_type=F32)  62.4 us
    ppermute x1, waiting for transfers between devices, per_device(): ig_first = lax.ppermute(image_grad_full[:half], 'section', [(1, 0)])  58.1 us
    convert_element_type x77, other arithmetic, bf(): return x.astype(BF16)  56.4 us
    concatenate x2, local copies, waits for them, and re-layouts, pack_rows(): return jnp.concatenate(pieces, -1)  53.6 us
  transfers between devices with their start and end apart: 75, of which 24 were waited for; matrix products, arithmetic and copies ran while one was open for 43% of the time, Pallas kernels for 0%

profile of v8, /device:TPU:0, one launch (start us, length us, event | category | flops | bytes accessed | tf_op | source)
XLA Modules:
  0.0 1240.2 jit_solution(14868470601770655262)
XLA Ops:
  5.6 9.7 collective-permute-done.2
  26.3 67.6 %conditional.12 = (f32[8,64,768]{2,1,0:T(8,128)}, bf16[8,64,12,64]{3,1,2,0:T(8,128)(2,1)}, bf16[8,64,768]{2,1,0:T(8,128)(2,1)}, f32[8,64,768]{2,1,0:T(8,128)}, f...) conditional(s32[]{:T(128)} %convert_element_type.1093, ...), branch_computations={%region_0.0_spmd, %region_1.8_spmd} | conditional | flops 7464489984 | bytes 124480776 | solution.py:31
  67.9 18.6 %fusion.85 = (bf16[8,64,3072]{2,1,0:T(8,128)(2,1)}, f32[8,64,3072]{2,1,0:T(8,128)}) fusion(f32[3072]{0:T(1024)S(1)} %bitcast.780, bf16[8,64,768]{2,1,0:T(8,128)(2,1)} %get-tuple-element.1595, bf16[768,3072]{1,0:T(8,128)(2,1)} %get-tuple-element.449), kind=kOutput, calls=%fused_computation.90 | convolution fusion | flops 2519728128 | bytes 14954496 | tf_op jit(solution)/shard_map/cond/branch_1_fun/...d,de->...e/dot_general | solution.py:58
  98.8 66.3 %conditional.13 = (f32[8,64,768]{2,1,0:T(8,128)}, bf16[8,64,12,64]{3,1,2,0:T(8,128)(2,1)S(1)}, bf16[8,64,768]{2,1,0:T(8,128)(2,1)}, f32[8,64,768]{2,1,0:T(8,128)...) conditional(s32[]{:T(128)} %convert_element_type.1093, ...), branch_computations={%region_8.9_spmd, %region_9.16_spmd} | conditional | flops 7464489984 | bytes 118189384 | solution.py:31
  139.2 18.5 %fusion.116 = (bf16[8,64,3072]{2,1,0:T(8,128)(2,1)}, f32[8,64,3072]{2,1,0:T(8,128)}) fusion(f32[3072]{0:T(1024)S(1)} %bitcast.781, bf16[8,64,768]{2,1,0:T(8,128)(2,1)} %get-tuple-element.1623, bf16[768,3072]{1,0:T(8,128)(2,1)} %get-tuple-element.461), kind=kOutput, calls=%fused_computation.148 | convolution fusion | flops 2519728128 | bytes 14954496 | tf_op jit(solution)/shard_map/cond/branch_1_fun/...d,de->...e/dot_general | solution.py:58
  211.8 29.2 %conditional.15 = (f32[8,64,768]{2,1,0:T(8,128)}, bf16[8,64,12,64]{3,1,2,0:T(8,128)(2,1)}, bf16[8,64,768]{2,1,0:T(8,128)(2,1)}, f32[8,64,768]{2,1,0:T(8,128)}, f...) conditional(s32[]{:T(128)} %convert_element_type.1096, ...), branch_computations={%region_19.20_spmd, %region_20.29_spmd} | conditional | flops 10490288128 | bytes 124310992 | solution.py:31
  241.0 23.9 %conditional.17 = (f32[8,64,768]{2,1,0:T(8,128)}, f32[768]{0:T(1024)S(1)}, f32[768]{0:T(1024)S(1)}, f32[768]{0:T(1024)S(1)}, f32[768]{0:T(1024)S(1)}, /*index=5*...) conditional(s32[]{:T(128)} %convert_element_type.1096, ...), branch_computations={%region_39.40_spmd, %region_40.54_spmd} | conditional | flops 13324111872 | bytes 152132064 | solution.py:31
  268.8 29.0 %conditional.16 = (bf16[8,64,12,64]{3,1,2,0:T(8,128)(2,1)}, bf16[8,64,768]{2,1,0:T(8,128)(2,1)}, f32[8,64,768]{2,1,0:T(8,128)}, f32[8,64,1]{1,0,2:T(8,128)S(1)},...) conditional(s32[]{:T(128)} %convert_element_type.1096, ...), branch_computations={%region_29.30_spmd, %region_30.39_spmd} | conditional | flops 10490288128 | bytes 124311000 | solution.py:31
  297.8 28.0 %conditional.18 = (f32[8,64,768]{2,1,0:T(8,128)}, f32[768]{0:T(1024)S(1)}, f32[768]{0:T(1024)S(1)}, f32[768]{0:T(1024)S(1)}, f32[768]{0:T(1024)S(1)}, /*index=5*...) conditional(s32[]{:T(128)} %convert_element_type.1096, ...), branch_computations={%region_54.55_spmd, %region_55.69_spmd} | conditional | flops 13324111872 | bytes 152132064 | solution.py:31
  390.6 19.2 %conditional.22 = (bf16[16,48,2304]{2,1,0:T(8,128)(2,1)}, bf16[16,48,768]{2,1,0:T(8,128)(2,1)}, bf16[16,48,3072]{2,1,0:T(8,128)(2,1)}, bf16[16,192]{1,0:T(8,128)...) conditional(s32[]{:T(128)} %convert_element_type.1096, ...), branch_computations={%region_93.94_spmd, %region_94.0_spmd} | conditional | flops 16939347968 | bytes 65327688 | solution.py:31
  410.9 41.9 %collective-permute-done.6 = bf16[8,64,768]{2,1,0:T(8,128)(2,1)} collective-permute-done((bf16[8,64,768]{2,1,0:T(8,128)(2,1)}, bf16[8,64,768]{2,1,0:T(8,128)(2,1)}, u32[]{:S(2)}, u32[]{:S(2)}) %collective-permute-start.6) | collective-permute-done | bytes 786464 | tf_op jit(solution)/shard_map/ppermute | solution.py:526
  454.0 74.3 %conditional.19 = (f32[8,64,768]{2,1,0:T(8,128)}, f32[768]{0:T(1024)S(1)}, f32[768]{0:T(1024)S(1)}, f32[768]{0:T(1024)S(1)}, f32[768]{0:T(1024)S(1)}, /*index=5*...) conditional(s32[]{:T(128)} %convert_element_type.1093, ...), branch_computations={%region_69.70_spmd, %region_70.80_spmd} | conditional | flops 7580802048 | bytes 129884416 | solution.py:31
  457.4 19.7 %fusion.278 = bf16[8,64,3072]{2,1,0:T(8,128)(2,1)} fusion(f32[8,64,3072]{2,1,0:T(8,128)} %get-tuple-element.574, bf16[8,64,768]{2,1,0:T(8,128)(2,1)} %get-tuple-element.1811, bf16[3072,768]{1,0:T(8,128)(2,1)S(1)} %copy-done.91), kind=kOutput, calls=%fused_computation.468 | convolution fusion | flops 2529165312 | bytes 14942208 | tf_op jit(solution)/shard_map/cond/branch_1_fun/...e,de->...d/dot_general | solution.py:62
  528.4 235.5 %collective-permute-done.5 = bf16[8,64,768]{2,1,0:T(8,128)(2,1)} collective-permute-done((bf16[8,64,768]{2,1,0:T(8,128)(2,1)}, bf16[8,64,768]{2,1,0:T(8,128)(2,1)}, u32[]{:S(2)}, u32[]{:S(2)}) %collective-permute-start.5) | collective-permute-done | bytes 786464 | tf_op jit(solution)/shard_map/ppermute | solution.py:526
  765.8 70.5 %conditional.20 = (f32[768]{0:T(1024)S(1)}, f32[768]{0:T(1024)S(1)}, f32[768]{0:T(1024)S(1)}, f32[768]{0:T(1024)S(1)}, bf16[8,64,2304]{2,1,0:T(8,128)(2,1)}, /*i...) conditional(s32[]{:T(128)} %convert_element_type.1093, ...), branch_computations={%region_80.81_spmd, %region_81.91_spmd} | conditional | flops 7580408832 | bytes 117301536 | solution.py:31
  766.8 19.1 %fusion.303 = bf16[8,64,3072]{2,1,0:T(8,128)(2,1)} fusion(f32[8,64,3072]{2,1,0:T(8,128)} %get-tuple-element.595, bf16[8,64,768]{2,1,0:T(8,128)(2,1)} %convert_element_type.812, bf16[3072,768]{1,0:T(8,128)(2,1)} %get-tuple-element.596), kind=kOutput, calls=%fused_computation.519 | convolution fusion | flops 2529165312 | bytes 14942208 | tf_op jit(solution)/shard_map/cond/branch_1_fun/...e,de->...d/dot_general | solution.py:62
  839.1 46.3 %conditional.23 = (bf16[16,48,2304]{2,1,0:T(8,128)(2,1)S(1)}, bf16[16,48,768]{2,1,0:T(8,128)(2,1)}, bf16[16,48,3072]{2,1,0:T(8,128)(2,1)}, bf16[16,192]{1,0:T(8,...) conditional(s32[]{:T(128)} %convert_element_type.1093, () %tuple.171, ...), branch_computations={%region_99.100_spmd, %region_100.0_spmd} | conditional | flops 14519103488 | bytes 56676920 | solution.py:31
  839.1 9.1 bitcast_convert_fusion.6
  856.6 9.6 bitcast_convert_fusion.7
  888.4 22.1 %concatenate.159 = bf16[16,48,9472]{2,1,0:T(8,128)(2,1)} concatenate(bf16[16,48,2304]{2,1,0:T(8,128)(2,1)S(1)} %get-tuple-element.977, bf16[16,48,768]{2,1,0:T(8,128)(2,1)} %get-tuple-element.978, bf16[16,48,3072]{2,1,0:T(8,128)(2,1)} %get-tuple-element.979, bf16[16,48,3072]{2,1,0:T(8,128)(2,1)} %get-tuple-element.980, bf16[16,48,9]{2,1,0:T(8,128)(2,1)} %reshape.1069, ...), dimensions={2} | concatenate | bytes 29097984 | tf_op jit(solution)/shard_map/concatenate | solution.py:389
  923.2 31.6 %concatenate.157 = bf16[16,48,12544]{2,1,0:T(8,128)(2,1)} concatenate(bf16[16,48,2304]{2,1,0:T(8,128)(2,1)} %get-tuple-element.940, bf16[16,48,768]{2,1,0:T(8,128)(2,1)} %get-tuple-element.941, bf16[16,48,3072]{2,1,0:T(8,128)(2,1)} %get-tuple-element.942, bf16[16,48,3072]{2,1,0:T(8,128)(2,1)} %get-tuple-element.943, bf16[16,48,768]{2,1,0:T(8,128)(2,1)} %get-tuple-element.944, ...), dimensions={2} | concatenate | bytes 38535168 | tf_op jit(solution)/shard_map/concatenate | solution.py:389
  963.2 11.5 fusion.419
  991.0 58.1 %collective-permute-done.9 = f32[288,768]{1,0:T(8,128)S(1)} collective-permute-done((f32[288,768]{1,0:T(8,128)S(1)}, f32[288,768]{1,0:T(8,128)S(1)}, u32[]{:S(2)}, u32[]{:S(2)}) %collective-permute-start.9) | collective-permute-done | bytes 884768 | tf_op jit(solution)/shard_map/ppermute | solution.py:562
  1207.8 14.8 %collective-permute-done.71 = f32[48]{0:T(128)S(1)} collective-permute-done((f32[48]{0:T(128)S(1)}, f32[48]{0:T(128)S(1)}, u32[]{:S(2)}, u32[]{:S(2)}) %collective-permute-start.71) | collective-permute-done | bytes 224 | tf_op jit(solution)/shard_map/ppermute | solution.py:609
  (622 shorter events, 609.9 us)
Async XLA Ops:
  0.7 14.6 %collective-permute-start.2 = (bf16[288,768]{1,0:T(8,128)(2,1)}, bf16[288,768]{1,0:T(8,128)(2,1)S(1)}, u32[]{:S(2)}, u32[]{:S(2)}) collective-permute-start(bf16[288,768]{1,0:T(8,128)(2,1)} %bitcast.743), channel_id=1, source_target_pairs={{0,16},{1,17},{2,18},{3,19},{4,20},{5,21},{6,22},{7,23},{8,24},{9,... | collective-permute-start | bytes 1327112 | tf_op jit(solution)/shard_map/ppermute | solution.py:448
  19.9 186.0 %collective-permute-start.3 = (bf16[576,1536]{1,0:T(8,128)(2,1)}, bf16[576,1536]{1,0:T(8,128)(2,1)}, u32[]{:S(2)}, u32[]{:S(2)}) collective-permute-start(bf16[576,1536]{1,0:T(8,128)(2,1)} %get-tuple-element.836), channel_id=1, source_target_pairs={{0,1},{1,2},{2,3},{3,4},{4,5},{5,6},{6,7},{7,8},{8,9},{9,10},{10,1... | collective-permute-start | bytes 5308424 | tf_op jit(solution)/shard_map/ppermute | solution.py:457
  20.0 185.9 %collective-permute-start.4 = (bf16[576,1536]{1,0:T(8,128)(2,1)}, bf16[576,1536]{1,0:T(8,128)(2,1)}, u32[]{:S(2)}, u32[]{:S(2)}) collective-permute-start(bf16[576,1536]{1,0:T(8,128)(2,1)} %get-tuple-element.836), channel_id=1, source_target_pairs={{1,0},{2,1},{3,2},{4,3},{5,4},{6,5},{7,6},{8,7},{9,8},{10,9},{11,1... | collective-permute-start | bytes 5308424 | tf_op jit(solution)/shard_map/ppermute | solution.py:458
  96.4 115.4 %collective-permute-start.1 = (bf16[8,64,768]{2,1,0:T(8,128)(2,1)}, bf16[8,64,768]{2,1,0:T(8,128)(2,1)}, u32[]{:S(2)}, u32[]{:S(2)}) collective-permute-start(bf16[8,64,768]{2,1,0:T(8,128)(2,1)} %convert_element_type.1097), channel_id=1, source_target_pairs={{0,16},{1,17},{2,18},{3,19},{4,20},{5,21},{6,22},{7,23},{8,24},{9,... | collective-permute-start | bytes 2359304 | tf_op jit(solution)/shard_map/ppermute | solution.py:491
  168.2 100.5 %collective-permute-start = (bf16[8,64,768]{2,1,0:T(8,128)(2,1)}, bf16[8,64,768]{2,1,0:T(8,128)(2,1)}, u32[]{:S(2)}, u32[]{:S(2)}) collective-permute-start(bf16[8,64,768]{2,1,0:T(8,128)(2,1)} %convert_element_type.1095), channel_id=1, source_target_pairs={{0,16},{1,17},{2,18},{3,19},{4,20},{5,21},{6,22},{7,23},{8,24},{9,... | collective-permute-start | bytes 2359304 | tf_op jit(solution)/shard_map/ppermute | solution.py:491
  267.4 185.3 %collective-permute-start.6 = (bf16[8,64,768]{2,1,0:T(8,128)(2,1)}, bf16[8,64,768]{2,1,0:T(8,128)(2,1)}, u32[]{:S(2)}, u32[]{:S(2)}) collective-permute-start(bf16[8,64,768]{2,1,0:T(8,128)(2,1)} %convert_element_type.1102), channel_id=1, source_target_pairs={{16,0},{17,1},{18,2},{19,3},{20,4},{21,5},{22,6},{23,7},{24,8},{25... | collective-permute-start | bytes 2359304 | tf_op jit(solution)/shard_map/ppermute | solution.py:526
  328.2 435.7 %collective-permute-start.5 = (bf16[8,64,768]{2,1,0:T(8,128)(2,1)}, bf16[8,64,768]{2,1,0:T(8,128)(2,1)}, u32[]{:S(2)}, u32[]{:S(2)}) collective-permute-start(bf16[8,64,768]{2,1,0:T(8,128)(2,1)} %convert_element_type.1100), channel_id=1, source_target_pairs={{16,0},{17,1},{18,2},{19,3},{20,4},{21,5},{22,6},{23,7},{24,8},{25... | collective-permute-start | bytes 2359304 | tf_op jit(solution)/shard_map/ppermute | solution.py:526
  340.7 577.4 %collective-permute-start.7 = (bf16[576,1536]{1,0:T(8,128)(2,1)}, bf16[576,1536]{1,0:T(8,128)(2,1)}, u32[]{:S(2)}, u32[]{:S(2)}) collective-permute-start(bf16[576,1536]{1,0:T(8,128)(2,1)} %get-tuple-element.1503), channel_id=1, source_target_pairs={{1,0},{2,1},{3,2},{4,3},{5,4},{6,5},{7,6},{8,7},{9,8},{10,9},{11,1... | collective-permute-start | bytes 5308424 | tf_op jit(solution)/shard_map/ppermute | solution.py:551
  341.0 577.2 %collective-permute-start.8 = (bf16[576,1536]{1,0:T(8,128)(2,1)}, bf16[576,1536]{1,0:T(8,128)(2,1)}, u32[]{:S(2)}, u32[]{:S(2)}) collective-permute-start(bf16[576,1536]{1,0:T(8,128)(2,1)} %get-tuple-element.1504), channel_id=1, source_target_pairs={{0,1},{1,2},{2,3},{3,4},{4,5},{5,6},{6,7},{7,8},{8,9},{9,10},{10,1... | collective-permute-start | bytes 5308424 | tf_op jit(solution)/shard_map/ppermute | solution.py:552
  962.5 26.8 %collective-permute-start.10 = (bf16[48,6272]{1,0:T(8,128)(2,1)S(1)}, bf16[48,6272]{1,0:T(8,128)(2,1)S(1)}, u32[]{:S(2)}, u32[]{:S(2)}) collective-permute-start(bf16[48,6272]{1,0:T(8,128)(2,1)S(1)} %dynamic-slice_bitcast_fusion.1), channel_id=1, source_target_pairs={{17,16},{18,17},{19,18},{22,19},{23,22},{26,23},{27,26},{30,27},{3... | collective-permute-start | bytes 1806344 | tf_op jit(solution)/shard_map/ppermute | solution.py:373
  976.7 13.4 %collective-permute-start.40 = (bf16[48,6272]{1,0:T(8,128)(2,1)S(1)}, bf16[48,6272]{1,0:T(8,128)(2,1)S(1)}, u32[]{:S(2)}, u32[]{:S(2)}) collective-permute-start(bf16[48,6272]{1,0:T(8,128)(2,1)S(1)} %dynamic-slice_bitcast_fusion), channel_id=1, source_target_pairs={{16,17},{17,18},{18,19},{19,22},{22,23},{23,26},{26,27},{27,30},{3... | collective-permute-start | bytes 1806344 | tf_op jit(solution)/shard_map/ppermute | solution.py:372
  981.1 68.0 %collective-permute-start.9 = (f32[288,768]{1,0:T(8,128)S(1)}, f32[288,768]{1,0:T(8,128)S(1)}, u32[]{:S(2)}, u32[]{:S(2)}) collective-permute-start(f32[288,768]{1,0:T(8,128)S(1)} %slice.204), channel_id=1, source_target_pairs={{16,0},{17,1},{18,2},{19,3},{20,4},{21,5},{22,6},{23,7},{24,8},{25... | collective-permute-start | bytes 2654216 | tf_op jit(solution)/shard_map/ppermute | solution.py:562
  982.7 68.6 %collective-permute-start.26 = (bf16[48,4736]{1,0:T(8,128)(2,1)S(1)}, bf16[48,4736]{1,0:T(8,128)(2,1)S(1)}, u32[]{:S(2)}, u32[]{:S(2)}) collective-permute-start(bf16[48,4736]{1,0:T(8,128)(2,1)S(1)} %fusion.381), channel_id=1, source_target_pairs={{1,0},{2,1},{3,2},{6,3},{7,6},{10,7},{11,10},{14,11},{15,14},{12,1... | collective-permute-start | bytes 1363976 | tf_op jit(solution)/shard_map/ppermute | solution.py:373
  987.4 66.1 %collective-permute-start.56 = (bf16[48,4736]{1,0:T(8,128)(2,1)S(1)}, bf16[48,4736]{1,0:T(8,128)(2,1)S(1)}, u32[]{:S(2)}, u32[]{:S(2)}) collective-permute-start(bf16[48,4736]{1,0:T(8,128)(2,1)S(1)} %fusion.367), channel_id=1, source_target_pairs={{0,1},{1,2},{2,3},{3,6},{6,7},{7,10},{10,11},{11,14},{14,15},{15,1... | collective-permute-start | bytes 1363976 | tf_op jit(solution)/shard_map/ppermute | solution.py:372
  989.4 66.4 %collective-permute-start.11 = (bf16[48,6272]{1,0:T(8,128)(2,1)S(1)}, bf16[48,6272]{1,0:T(8,128)(2,1)S(1)}, u32[]{:S(2)}, u32[]{:S(2)}) collective-permute-start(bf16[48,6272]{1,0:T(8,128)(2,1)S(1)} %fusion.353), channel_id=1, source_target_pairs={{17,16},{18,17},{19,18},{22,19},{23,22},{26,23},{27,26},{30,27},{3... | collective-permute-start | bytes 1806344 | tf_op jit(solution)/shard_map/ppermute | solution.py:373
  990.3 66.4 %collective-permute-start.41 = (bf16[48,6272]{1,0:T(8,128)(2,1)S(1)}, bf16[48,6272]{1,0:T(8,128)(2,1)S(1)}, u32[]{:S(2)}, u32[]{:S(2)}) collective-permute-start(bf16[48,6272]{1,0:T(8,128)(2,1)S(1)} %fusion.339), channel_id=1, source_target_pairs={{16,17},{17,18},{18,19},{19,22},{22,23},{23,26},{26,27},{27,30},{3... | collective-permute-start | bytes 1806344 | tf_op jit(solution)/shard_map/ppermute | solution.py:372
  1065.8 20.2 %collective-permute-start.13 = (bf16[48,6272]{1,0:T(8,128)(2,1)S(1)}, bf16[48,6272]{1,0:T(8,128)(2,1)S(1)}, u32[]{:S(2)}, u32[]{:S(2)}) collective-permute-start(bf16[48,6272]{1,0:T(8,128)(2,1)S(1)} %fusion.351), channel_id=1, source_target_pairs={{17,16},{18,17},{19,18},{22,19},{23,22},{26,23},{27,26},{30,27},{3... | collective-permute-start | bytes 1806344 | tf_op jit(solution)/shard_map/ppermute | solution.py:373
  1066.7 20.2 %collective-permute-start.43 = (bf16[48,6272]{1,0:T(8,128)(2,1)S(1)}, bf16[48,6272]{1,0:T(8,128)(2,1)S(1)}, u32[]{:S(2)}, u32[]{:S(2)}) collective-permute-start(bf16[48,6272]{1,0:T(8,128)(2,1)S(1)} %fusion.337), channel_id=1, source_target_pairs={{16,17},{17,18},{18,19},{19,22},{22,23},{23,26},{26,27},{27,30},{3... | collective-permute-start | bytes 1806344 | tf_op jit(solution)/shard_map/ppermute | solution.py:372
  1106.5 20.2 %collective-permute-start.16 = (bf16[48,6272]{1,0:T(8,128)(2,1)S(1)}, bf16[48,6272]{1,0:T(8,128)(2,1)S(1)}, u32[]{:S(2)}, u32[]{:S(2)}) collective-permute-start(bf16[48,6272]{1,0:T(8,128)(2,1)S(1)} %fusion.348), channel_id=1, source_target_pairs={{17,16},{18,17},{19,18},{22,19},{23,22},{26,23},{27,26},{30,27},{3... | collective-permute-start | bytes 1806344 | tf_op jit(solution)/shard_map/ppermute | solution.py:373
  1107.4 20.2 %collective-permute-start.46 = (bf16[48,6272]{1,0:T(8,128)(2,1)S(1)}, bf16[48,6272]{1,0:T(8,128)(2,1)S(1)}, u32[]{:S(2)}, u32[]{:S(2)}) collective-permute-start(bf16[48,6272]{1,0:T(8,128)(2,1)S(1)} %fusion.334), channel_id=1, source_target_pairs={{16,17},{17,18},{18,19},{19,22},{22,23},{23,26},{26,27},{27,30},{3... | collective-permute-start | bytes 1806344 | tf_op jit(solution)/shard_map/ppermute | solution.py:372
  1147.2 20.2 %collective-permute-start.19 = (bf16[48,6272]{1,0:T(8,128)(2,1)S(1)}, bf16[48,6272]{1,0:T(8,128)(2,1)S(1)}, u32[]{:S(2)}, u32[]{:S(2)}) collective-permute-start(bf16[48,6272]{1,0:T(8,128)(2,1)S(1)} %fusion.345), channel_id=1, source_target_pairs={{17,16},{18,17},{19,18},{22,19},{23,22},{26,23},{27,26},{30,27},{3... | collective-permute-start | bytes 1806344 | tf_op jit(solution)/shard_map/ppermute | solution.py:373
  1148.0 20.2 %collective-permute-start.49 = (bf16[48,6272]{1,0:T(8,128)(2,1)S(1)}, bf16[48,6272]{1,0:T(8,128)(2,1)S(1)}, u32[]{:S(2)}, u32[]{:S(2)}) collective-permute-start(bf16[48,6272]{1,0:T(8,128)(2,1)S(1)} %fusion.331), channel_id=1, source_target_pairs={{16,17},{17,18},{18,19},{19,22},{22,23},{23,26},{26,27},{27,30},{3... | collective-permute-start | bytes 1806344 | tf_op jit(solution)/shard_map/ppermute | solution.py:372
  1204.4 29.2 %collective-permute-start.73 = (f32[48,1536]{1,0:T(8,128)S(1)}, f32[48,1536]{1,0:T(8,128)S(1)}, u32[]{:S(2)}, u32[]{:S(2)}) collective-permute-start(f32[48,1536]{1,0:T(8,128)S(1)} %slice.265), channel_id=1, source_target_pairs={{16,0},{17,1},{18,2},{19,3},{20,4},{21,5},{22,6},{23,7},{24,8},{25... | collective-permute-start | bytes 884744 | tf_op jit(solution)/shard_map/ppermute | solution.py:609
  1205.9 16.8 %collective-permute-start.71 = (f32[48]{0:T(128)S(1)}, f32[48]{0:T(128)S(1)}, u32[]{:S(2)}, u32[]{:S(2)}) collective-permute-start(f32[48]{0:T(128)S(1)} %slice.232), channel_id=1, source_target_pairs={{16,0},{17,1},{18,2},{19,3},{20,4},{21,5},{22,6},{23,7},{24,8},{25... | collective-permute-start | bytes 584 | tf_op jit(solution)/shard_map/ppermute | solution.py:609
  (126 other events, 3119.3 us)

commit v9 on v8

--- a/solution.py
+++ b/solution.py
@@ -596,10 +596,10 @@
         low_pairs.append(pairs)
 
     low_w = run_on(low, layer_weight_grads, low_pairs)
+    a_packed, low_w = lax.optimization_barrier((a_packed, low_w))
     low_sm = tree_sum(low_small)
     b_list = layer_list(low_w, low_sm)
     b_packed = pack_rows(b_list, n_dp, block_rows)
-    a_packed, b_packed = lax.optimization_barrier((a_packed, b_packed))
     a_row = ring_reduce_scatter(a_packed, 1, cycle, dp_index)
     b_row = ring_reduce_scatter(b_packed, 0, cycle, dp_index)
     a_got = unpack_row(a_row, a_list, n_dp, block_rows)

time: 1250 us -> 1280 us (1.024)
  other arithmetic: 114 us -> 127 us
  transfers between devices with their start and end apart: 75 -> 75, of which waited for: 24 -> 23; matrix products, arithmetic and copies ran while one was open for 43% -> 42% of each run, Pallas kernels for 0% -> 0%
where the time goes in v9:
time: 1280 us; the launch traced here: 1260 us
  waiting for transfers between devices  416 us (32%)
  local copies, waits for them, and re-layouts  287 us (22%)
  matrix products  186 us (15%)
  starting transfers between devices  133 us (10%)
  other arithmetic  127 us (10%)
  between operations  79.9 us (6%)
  loops' own time  35.2 us (3%)
    ppermute x2, waiting for transfers between devices, per_device(): returned.append(lax.ppermute(bf(dh), 'section', [(1, 0)]))  276 us
    another operation x81, local copies, waits for them, and re-layouts  91.3 us
    dot_general x8, matrix products, mm_t(): return jnp.einsum('...e,de->...d', g, w, preferred_element_type=F32)  69 us
    ppermute x30, starting transfers between devices, ring_reduce_scatter(): got_w = lax.ppermute(send_w, axes, bwd)  68.7 us
    convert_element_type x77, other arithmetic, bf(): return x.astype(BF16)  68.2 us
    ppermute x1, waiting for transfers between devices, per_device(): ig_first = lax.ppermute(image_grad_full[:half], 'section', [(1, 0)])  67.7 us
    dot_general x8, matrix products, mm(): return jnp.einsum('...d,de->...e', a, w, preferred_element_type=F32)  62.4 us
    concatenate x2, local copies, waits for them, and re-layouts, pack_rows(): return jnp.concatenate(pieces, -1)  47 us
  transfers between devices with their start and end apart: 75, of which 23 were waited for; matrix products, arithmetic and copies ran while one was open for 42% of the time, Pallas kernels for 0%

profile of v9, /device:TPU:0, one launch (start us, length us, event | category | flops | bytes accessed | tf_op | source)
XLA Modules:
  0.0 1263.7 jit_solution(4234283333301645231)
XLA Ops:
  5.6 9.7 collective-permute-done.2
  26.3 67.6 %conditional.12 = (f32[8,64,768]{2,1,0:T(8,128)}, bf16[8,64,12,64]{3,1,2,0:T(8,128)(2,1)}, bf16[8,64,768]{2,1,0:T(8,128)(2,1)}, f32[8,64,768]{2,1,0:T(8,128)}, f...) conditional(s32[]{:T(128)} %convert_element_type.1083, ...), branch_computations={%region_0.0_spmd, %region_1.8_spmd} | conditional | flops 7464489984 | bytes 124480776 | solution.py:31
  68.1 18.6 %fusion.77 = (bf16[8,64,3072]{2,1,0:T(8,128)(2,1)}, f32[8,64,3072]{2,1,0:T(8,128)}) fusion(f32[3072]{0:T(1024)S(1)} %bitcast.786, bf16[8,64,768]{2,1,0:T(8,128)(2,1)} %get-tuple-element.1597, bf16[768,3072]{1,0:T(8,128)(2,1)} %get-tuple-element.443), kind=kOutput, calls=%fused_computation.89 | convolution fusion | flops 2519728128 | bytes 14954496 | tf_op jit(solution)/shard_map/cond/branch_1_fun/...d,de->...e/dot_general | solution.py:58
  98.9 66.4 %conditional.13 = (f32[8,64,768]{2,1,0:T(8,128)}, bf16[8,64,12,64]{3,1,2,0:T(8,128)(2,1)S(1)}, bf16[8,64,768]{2,1,0:T(8,128)(2,1)}, f32[8,64,768]{2,1,0:T(8,128)...) conditional(s32[]{:T(128)} %convert_element_type.1083, ...), branch_computations={%region_8.9_spmd, %region_9.16_spmd} | conditional | flops 7464489984 | bytes 118189384 | solution.py:31
  139.3 18.5 %fusion.108 = (bf16[8,64,3072]{2,1,0:T(8,128)(2,1)}, f32[8,64,3072]{2,1,0:T(8,128)}) fusion(f32[3072]{0:T(1024)S(1)} %bitcast.787, bf16[8,64,768]{2,1,0:T(8,128)(2,1)} %get-tuple-element.1625, bf16[768,3072]{1,0:T(8,128)(2,1)} %get-tuple-element.455), kind=kOutput, calls=%fused_computation.147 | convolution fusion | flops 2519728128 | bytes 14954496 | tf_op jit(solution)/shard_map/cond/branch_1_fun/...d,de->...e/dot_general | solution.py:58
  211.5 29.2 %conditional.15 = (f32[8,64,768]{2,1,0:T(8,128)}, bf16[8,64,12,64]{3,1,2,0:T(8,128)(2,1)}, bf16[8,64,768]{2,1,0:T(8,128)(2,1)}, f32[8,64,768]{2,1,0:T(8,128)}, f...) conditional(s32[]{:T(128)} %convert_element_type.1086, ...), branch_computations={%region_19.20_spmd, %region_20.29_spmd} | conditional | flops 10490288128 | bytes 124310992 | solution.py:31
  240.7 23.9 %conditional.17 = (f32[8,64,768]{2,1,0:T(8,128)}, f32[768]{0:T(1024)S(1)}, f32[768]{0:T(1024)S(1)}, f32[768]{0:T(1024)S(1)}, f32[768]{0:T(1024)S(1)}, /*index=5*...) conditional(s32[]{:T(128)} %convert_element_type.1086, ...), branch_computations={%region_39.40_spmd, %region_40.54_spmd} | conditional | flops 13324111872 | bytes 152132064 | solution.py:31
  268.5 29.1 %conditional.16 = (bf16[8,64,12,64]{3,1,2,0:T(8,128)(2,1)}, bf16[8,64,768]{2,1,0:T(8,128)(2,1)}, f32[8,64,768]{2,1,0:T(8,128)}, f32[8,64,1]{1,0,2:T(8,128)S(1)},...) conditional(s32[]{:T(128)} %convert_element_type.1086, ...), branch_computations={%region_29.30_spmd, %region_30.39_spmd} | conditional | flops 10490288128 | bytes 124311000 | solution.py:31
  297.6 27.8 %conditional.18 = (f32[8,64,768]{2,1,0:T(8,128)}, f32[768]{0:T(1024)S(1)}, f32[768]{0:T(1024)S(1)}, f32[768]{0:T(1024)S(1)}, f32[768]{0:T(1024)S(1)}, /*index=5*...) conditional(s32[]{:T(128)} %convert_element_type.1086, ...), branch_computations={%region_54.55_spmd, %region_55.69_spmd} | conditional | flops 13324111872 | bytes 152132064 | solution.py:31
  391.2 19.3 %conditional.22 = (bf16[16,48,2304]{2,1,0:T(8,128)(2,1)}, bf16[16,48,768]{2,1,0:T(8,128)(2,1)}, bf16[16,48,3072]{2,1,0:T(8,128)(2,1)}, bf16[16,192]{1,0:T(8,128)...) conditional(s32[]{:T(128)} %convert_element_type.1086, ...), branch_computations={%region_93.94_spmd, %region_94.0_spmd} | conditional | flops 16939347968 | bytes 65327688 | solution.py:31
  411.5 40.4 %collective-permute-done.6 = bf16[8,64,768]{2,1,0:T(8,128)(2,1)} collective-permute-done((bf16[8,64,768]{2,1,0:T(8,128)(2,1)}, bf16[8,64,768]{2,1,0:T(8,128)(2,1)}, u32[]{:S(2)}, u32[]{:S(2)}) %collective-permute-start.6) | collective-permute-done | bytes 786464 | tf_op jit(solution)/shard_map/ppermute | solution.py:526
  453.3 74.5 %conditional.19 = (f32[8,64,768]{2,1,0:T(8,128)}, f32[768]{0:T(1024)S(1)}, f32[768]{0:T(1024)S(1)}, f32[768]{0:T(1024)S(1)}, f32[768]{0:T(1024)S(1)}, /*index=5*...) conditional(s32[]{:T(128)} %convert_element_type.1083, ...), branch_computations={%region_69.70_spmd, %region_70.80_spmd} | conditional | flops 7580802048 | bytes 129884416 | solution.py:31
  456.6 19.6 %fusion.270 = bf16[8,64,3072]{2,1,0:T(8,128)(2,1)} fusion(f32[8,64,3072]{2,1,0:T(8,128)} %get-tuple-element.568, bf16[8,64,768]{2,1,0:T(8,128)(2,1)} %get-tuple-element.1813, bf16[3072,768]{1,0:T(8,128)(2,1)S(1)} %copy-done.90), kind=kOutput, calls=%fused_computation.467 | convolution fusion | flops 2529165312 | bytes 14942208 | tf_op jit(solution)/shard_map/cond/branch_1_fun/...e,de->...d/dot_general | solution.py:62
  527.8 235.4 %collective-permute-done.5 = bf16[8,64,768]{2,1,0:T(8,128)(2,1)} collective-permute-done((bf16[8,64,768]{2,1,0:T(8,128)(2,1)}, bf16[8,64,768]{2,1,0:T(8,128)(2,1)}, u32[]{:S(2)}, u32[]{:S(2)}) %collective-permute-start.5) | collective-permute-done | bytes 786464 | tf_op jit(solution)/shard_map/ppermute | solution.py:526
  765.0 70.9 %conditional.20 = (f32[768]{0:T(1024)S(1)}, f32[768]{0:T(1024)S(1)}, f32[768]{0:T(1024)S(1)}, f32[768]{0:T(1024)S(1)}, bf16[8,64,2304]{2,1,0:T(8,128)(2,1)}, /*i...) conditional(s32[]{:T(128)} %convert_element_type.1083, ...), branch_computations={%region_80.81_spmd, %region_81.91_spmd} | conditional | flops 7580408832 | bytes 117301536 | solution.py:31
  766.1 19.1 %fusion.295 = bf16[8,64,3072]{2,1,0:T(8,128)(2,1)} fusion(f32[8,64,3072]{2,1,0:T(8,128)} %get-tuple-element.589, bf16[8,64,768]{2,1,0:T(8,128)(2,1)} %convert_element_type.798, bf16[3072,768]{1,0:T(8,128)(2,1)} %get-tuple-element.590), kind=kOutput, calls=%fused_computation.518 | convolution fusion | flops 2529165312 | bytes 14942208 | tf_op jit(solution)/shard_map/cond/branch_1_fun/...e,de->...d/dot_general | solution.py:62
  838.7 32.3 %conditional.23 = (bf16[768,2304]{1,0:T(8,128)(2,1)S(1)}, bf16[768,768]{1,0:T(8,128)(2,1)S(1)}, bf16[768,3072]{1,0:T(8,128)(2,1)S(1)}, bf16[3072]{0:T(1024)(128)...) conditional(s32[]{:T(128)} %convert_element_type.1083, () %tuple.159, ...), branch_computations={%region_99.100_spmd, %region_100.103_spmd} | conditional | flops 14512025600 | bytes 62922288 | solution.py:31
  871.0 11.3 maximum_select_fusion
  889.5 32.1 %concatenate.161 = bf16[16,48,12544]{2,1,0:T(8,128)(2,1)} concatenate(bf16[16,48,2304]{2,1,0:T(8,128)(2,1)} %get-tuple-element.939, bf16[16,48,768]{2,1,0:T(8,128)(2,1)} %get-tuple-element.940, bf16[16,48,3072]{2,1,0:T(8,128)(2,1)} %get-tuple-element.941, bf16[16,48,3072]{2,1,0:T(8,128)(2,1)} %get-tuple-element.942, bf16[16,48,768]{2,1,0:T(8,128)(2,1)} %get-tuple-element.943, ...), dimensions={2} | concatenate | bytes 38535168 | tf_op jit(solution)/shard_map/concatenate | solution.py:389
  921.6 14.8 %fusion.410 = (bf16[16,48,6272]{2,1,0:T(8,128)(2,1)}, bf16[16,48,6272]{2,1,0:T(8,128)(2,1)}) fusion(bf16[16,48,12544]{2,1,0:T(8,128)(2,1)} %concatenate.161), kind=kLoop, calls=%fused_computation.768 | loop fusion | bytes 38535168 | tf_op jit(solution)/shard_map/slice | solution.py:364
  943.0 8.5 reshape.1043
  952.3 14.9 %concatenate.163 = bf16[16,48,6400]{2,1,0:T(8,128)(2,1)} concatenate(bf16[16,48,3072]{2,1,0:T(8,128)(2,1)} %bitcast.727, bf16[16,48,3072]{2,1,0:T(8,128)(2,1)} %reshape.1043, bf16[16,48,9]{2,1,0:T(8,128)(2,1)} %reshape.1050, bf16[16,48,247]{2,1,0:T(8,128)(2,1)} %broadcast_in_dim.102), dimensions={2} | concatenate | bytes 19660800 | tf_op jit(solution)/shard_map/concatenate | solution.py:389
  993.1 67.7 %collective-permute-done.9 = f32[288,768]{1,0:T(8,128)S(1)} collective-permute-done((f32[288,768]{1,0:T(8,128)S(1)}, f32[288,768]{1,0:T(8,128)S(1)}, u32[]{:S(2)}, u32[]{:S(2)}) %collective-permute-start.9) | collective-permute-done | bytes 884768 | tf_op jit(solution)/shard_map/ppermute | solution.py:562
  1220.0 26.2 %collective-permute-done.71 = f32[48]{0:T(128)S(1)} collective-permute-done((f32[48]{0:T(128)S(1)}, f32[48]{0:T(128)S(1)}, u32[]{:S(2)}, u32[]{:S(2)}) %collective-permute-start.71) | collective-permute-done | bytes 224 | tf_op jit(solution)/shard_map/ppermute | solution.py:609
  (628 shorter events, 617.5 us)
Async XLA Ops:
  0.7 14.6 %collective-permute-start.2 = (bf16[288,768]{1,0:T(8,128)(2,1)}, bf16[288,768]{1,0:T(8,128)(2,1)S(1)}, u32[]{:S(2)}, u32[]{:S(2)}) collective-permute-start(bf16[288,768]{1,0:T(8,128)(2,1)} %bitcast.749), channel_id=1, source_target_pairs={{0,16},{1,17},{2,18},{3,19},{4,20},{5,21},{6,22},{7,23},{8,24},{9,... | collective-permute-start | bytes 1327112 | tf_op jit(solution)/shard_map/ppermute | solution.py:448
  19.9 185.6 %collective-permute-start.3 = (bf16[576,1536]{1,0:T(8,128)(2,1)}, bf16[576,1536]{1,0:T(8,128)(2,1)}, u32[]{:S(2)}, u32[]{:S(2)}) collective-permute-start(bf16[576,1536]{1,0:T(8,128)(2,1)} %get-tuple-element.835), channel_id=1, source_target_pairs={{0,1},{1,2},{2,3},{3,4},{4,5},{5,6},{6,7},{7,8},{8,9},{9,10},{10,1... | collective-permute-start | bytes 5308424 | tf_op jit(solution)/shard_map/ppermute | solution.py:457
  20.0 185.5 %collective-permute-start.4 = (bf16[576,1536]{1,0:T(8,128)(2,1)}, bf16[576,1536]{1,0:T(8,128)(2,1)}, u32[]{:S(2)}, u32[]{:S(2)}) collective-permute-start(bf16[576,1536]{1,0:T(8,128)(2,1)} %get-tuple-element.835), channel_id=1, source_target_pairs={{1,0},{2,1},{3,2},{4,3},{5,4},{6,5},{7,6},{8,7},{9,8},{10,9},{11,1... | collective-permute-start | bytes 5308424 | tf_op jit(solution)/shard_map/ppermute | solution.py:458
  96.5 115.0 %collective-permute-start.1 = (bf16[8,64,768]{2,1,0:T(8,128)(2,1)}, bf16[8,64,768]{2,1,0:T(8,128)(2,1)}, u32[]{:S(2)}, u32[]{:S(2)}) collective-permute-start(bf16[8,64,768]{2,1,0:T(8,128)(2,1)} %convert_element_type.1087), channel_id=1, source_target_pairs={{0,16},{1,17},{2,18},{3,19},{4,20},{5,21},{6,22},{7,23},{8,24},{9,... | collective-permute-start | bytes 2359304 | tf_op jit(solution)/shard_map/ppermute | solution.py:491
  168.2 100.1 %collective-permute-start = (bf16[8,64,768]{2,1,0:T(8,128)(2,1)}, bf16[8,64,768]{2,1,0:T(8,128)(2,1)}, u32[]{:S(2)}, u32[]{:S(2)}) collective-permute-start(bf16[8,64,768]{2,1,0:T(8,128)(2,1)} %convert_element_type.1085), channel_id=1, source_target_pairs={{0,16},{1,17},{2,18},{3,19},{4,20},{5,21},{6,22},{7,23},{8,24},{9,... | collective-permute-start | bytes 2359304 | tf_op jit(solution)/shard_map/ppermute | solution.py:491
  267.1 184.9 %collective-permute-start.6 = (bf16[8,64,768]{2,1,0:T(8,128)(2,1)}, bf16[8,64,768]{2,1,0:T(8,128)(2,1)}, u32[]{:S(2)}, u32[]{:S(2)}) collective-permute-start(bf16[8,64,768]{2,1,0:T(8,128)(2,1)} %convert_element_type.1092), channel_id=1, source_target_pairs={{16,0},{17,1},{18,2},{19,3},{20,4},{21,5},{22,6},{23,7},{24,8},{25... | collective-permute-start | bytes 2359304 | tf_op jit(solution)/shard_map/ppermute | solution.py:526
  327.9 435.2 %collective-permute-start.5 = (bf16[8,64,768]{2,1,0:T(8,128)(2,1)}, bf16[8,64,768]{2,1,0:T(8,128)(2,1)}, u32[]{:S(2)}, u32[]{:S(2)}) collective-permute-start(bf16[8,64,768]{2,1,0:T(8,128)(2,1)} %convert_element_type.1090), channel_id=1, source_target_pairs={{16,0},{17,1},{18,2},{19,3},{20,4},{21,5},{22,6},{23,7},{24,8},{25... | collective-permute-start | bytes 2359304 | tf_op jit(solution)/shard_map/ppermute | solution.py:526
  340.5 541.8 %collective-permute-start.7 = (bf16[576,1536]{1,0:T(8,128)(2,1)}, bf16[576,1536]{1,0:T(8,128)(2,1)}, u32[]{:S(2)}, u32[]{:S(2)}) collective-permute-start(bf16[576,1536]{1,0:T(8,128)(2,1)} %get-tuple-element.1505), channel_id=1, source_target_pairs={{1,0},{2,1},{3,2},{4,3},{5,4},{6,5},{7,6},{8,7},{9,8},{10,9},{11,1... | collective-permute-start | bytes 5308424 | tf_op jit(solution)/shard_map/ppermute | solution.py:551
  340.8 541.5 %collective-permute-start.8 = (bf16[576,1536]{1,0:T(8,128)(2,1)}, bf16[576,1536]{1,0:T(8,128)(2,1)}, u32[]{:S(2)}, u32[]{:S(2)}) collective-permute-start(bf16[576,1536]{1,0:T(8,128)(2,1)} %get-tuple-element.1506), channel_id=1, source_target_pairs={{0,1},{1,2},{2,3},{3,4},{4,5},{5,6},{6,7},{7,8},{8,9},{9,10},{10,1... | collective-permute-start | bytes 5308424 | tf_op jit(solution)/shard_map/ppermute | solution.py:552
  938.4 51.6 %collective-permute-start.10 = (bf16[48,6272]{1,0:T(8,128)(2,1)}, bf16[48,6272]{1,0:T(8,128)(2,1)}, u32[]{:S(2)}, u32[]{:S(2)}) collective-permute-start(bf16[48,6272]{1,0:T(8,128)(2,1)} %dynamic-slice_bitcast_fusion.1), channel_id=1, source_target_pairs={{17,16},{18,17},{19,18},{22,19},{23,22},{26,23},{27,26},{30,27},{3... | collective-permute-start | bytes 1806344 | tf_op jit(solution)/shard_map/ppermute | solution.py:373
  973.9 18.3 %collective-permute-start.40 = (bf16[48,6272]{1,0:T(8,128)(2,1)S(1)}, bf16[48,6272]{1,0:T(8,128)(2,1)S(1)}, u32[]{:S(2)}, u32[]{:S(2)}) collective-permute-start(bf16[48,6272]{1,0:T(8,128)(2,1)S(1)} %dynamic-slice_bitcast_fusion), channel_id=1, source_target_pairs={{16,17},{17,18},{18,19},{19,22},{22,23},{23,26},{26,27},{27,30},{3... | collective-permute-start | bytes 1806344 | tf_op jit(solution)/shard_map/ppermute | solution.py:372
  981.9 78.9 %collective-permute-start.9 = (f32[288,768]{1,0:T(8,128)S(1)}, f32[288,768]{1,0:T(8,128)S(1)}, u32[]{:S(2)}, u32[]{:S(2)}) collective-permute-start(f32[288,768]{1,0:T(8,128)S(1)} %slice.206), channel_id=1, source_target_pairs={{16,0},{17,1},{18,2},{19,3},{20,4},{21,5},{22,6},{23,7},{24,8},{25... | collective-permute-start | bytes 2654216 | tf_op jit(solution)/shard_map/ppermute | solution.py:562
  983.3 79.7 %collective-permute-start.26 = (bf16[48,4736]{1,0:T(8,128)(2,1)S(1)}, bf16[48,4736]{1,0:T(8,128)(2,1)S(1)}, u32[]{:S(2)}, u32[]{:S(2)}) collective-permute-start(bf16[48,4736]{1,0:T(8,128)(2,1)S(1)} %fusion.373), channel_id=1, source_target_pairs={{1,0},{2,1},{3,2},{6,3},{7,6},{10,7},{11,10},{14,11},{15,14},{12,1... | collective-permute-start | bytes 1363976 | tf_op jit(solution)/shard_map/ppermute | solution.py:373
  988.1 77.6 %collective-permute-start.56 = (bf16[48,4736]{1,0:T(8,128)(2,1)S(1)}, bf16[48,4736]{1,0:T(8,128)(2,1)S(1)}, u32[]{:S(2)}, u32[]{:S(2)}) collective-permute-start(bf16[48,4736]{1,0:T(8,128)(2,1)S(1)} %fusion.359), channel_id=1, source_target_pairs={{0,1},{1,2},{2,3},{3,6},{6,7},{7,10},{10,11},{11,14},{14,15},{15,1... | collective-permute-start | bytes 1363976 | tf_op jit(solution)/shard_map/ppermute | solution.py:372
  991.5 76.3 %collective-permute-start.11 = (bf16[48,6272]{1,0:T(8,128)(2,1)S(1)}, bf16[48,6272]{1,0:T(8,128)(2,1)S(1)}, u32[]{:S(2)}, u32[]{:S(2)}) collective-permute-start(bf16[48,6272]{1,0:T(8,128)(2,1)S(1)} %fusion.345), channel_id=1, source_target_pairs={{17,16},{18,17},{19,18},{22,19},{23,22},{26,23},{27,26},{30,27},{3... | collective-permute-start | bytes 1806344 | tf_op jit(solution)/shard_map/ppermute | solution.py:373
  992.4 77.3 %collective-permute-start.41 = (bf16[48,6272]{1,0:T(8,128)(2,1)S(1)}, bf16[48,6272]{1,0:T(8,128)(2,1)S(1)}, u32[]{:S(2)}, u32[]{:S(2)}) collective-permute-start(bf16[48,6272]{1,0:T(8,128)(2,1)S(1)} %fusion.331), channel_id=1, source_target_pairs={{16,17},{17,18},{18,19},{19,22},{22,23},{23,26},{26,27},{27,30},{3... | collective-permute-start | bytes 1806344 | tf_op jit(solution)/shard_map/ppermute | solution.py:372
  1079.1 19.1 %collective-permute-start.13 = (bf16[48,6272]{1,0:T(8,128)(2,1)S(1)}, bf16[48,6272]{1,0:T(8,128)(2,1)S(1)}, u32[]{:S(2)}, u32[]{:S(2)}) collective-permute-start(bf16[48,6272]{1,0:T(8,128)(2,1)S(1)} %fusion.343), channel_id=1, source_target_pairs={{17,16},{18,17},{19,18},{22,19},{23,22},{26,23},{27,26},{30,27},{3... | collective-permute-start | bytes 1806344 | tf_op jit(solution)/shard_map/ppermute | solution.py:373
  1080.0 20.2 %collective-permute-start.43 = (bf16[48,6272]{1,0:T(8,128)(2,1)S(1)}, bf16[48,6272]{1,0:T(8,128)(2,1)S(1)}, u32[]{:S(2)}, u32[]{:S(2)}) collective-permute-start(bf16[48,6272]{1,0:T(8,128)(2,1)S(1)} %fusion.329), channel_id=1, source_target_pairs={{16,17},{17,18},{18,19},{19,22},{22,23},{23,26},{26,27},{27,30},{3... | collective-permute-start | bytes 1806344 | tf_op jit(solution)/shard_map/ppermute | solution.py:372
  1119.8 19.1 %collective-permute-start.16 = (bf16[48,6272]{1,0:T(8,128)(2,1)S(1)}, bf16[48,6272]{1,0:T(8,128)(2,1)S(1)}, u32[]{:S(2)}, u32[]{:S(2)}) collective-permute-start(bf16[48,6272]{1,0:T(8,128)(2,1)S(1)} %fusion.340), channel_id=1, source_target_pairs={{17,16},{18,17},{19,18},{22,19},{23,22},{26,23},{27,26},{30,27},{3... | collective-permute-start | bytes 1806344 | tf_op jit(solution)/shard_map/ppermute | solution.py:373
  1120.7 20.2 %collective-permute-start.46 = (bf16[48,6272]{1,0:T(8,128)(2,1)S(1)}, bf16[48,6272]{1,0:T(8,128)(2,1)S(1)}, u32[]{:S(2)}, u32[]{:S(2)}) collective-permute-start(bf16[48,6272]{1,0:T(8,128)(2,1)S(1)} %fusion.326), channel_id=1, source_target_pairs={{16,17},{17,18},{18,19},{19,22},{22,23},{23,26},{26,27},{27,30},{3... | collective-permute-start | bytes 1806344 | tf_op jit(solution)/shard_map/ppermute | solution.py:372
  1160.5 19.1 %collective-permute-start.19 = (bf16[48,6272]{1,0:T(8,128)(2,1)S(1)}, bf16[48,6272]{1,0:T(8,128)(2,1)S(1)}, u32[]{:S(2)}, u32[]{:S(2)}) collective-permute-start(bf16[48,6272]{1,0:T(8,128)(2,1)S(1)} %fusion.337), channel_id=1, source_target_pairs={{17,16},{18,17},{19,18},{22,19},{23,22},{26,23},{27,26},{30,27},{3... | collective-permute-start | bytes 1806344 | tf_op jit(solution)/shard_map/ppermute | solution.py:373
  1161.4 20.2 %collective-permute-start.49 = (bf16[48,6272]{1,0:T(8,128)(2,1)S(1)}, bf16[48,6272]{1,0:T(8,128)(2,1)S(1)}, u32[]{:S(2)}, u32[]{:S(2)}) collective-permute-start(bf16[48,6272]{1,0:T(8,128)(2,1)S(1)} %fusion.323), channel_id=1, source_target_pairs={{16,17},{17,18},{18,19},{19,22},{22,23},{23,26},{26,27},{27,30},{3... | collective-permute-start | bytes 1806344 | tf_op jit(solution)/shard_map/ppermute | solution.py:372
  1216.5 40.5 %collective-permute-start.73 = (f32[48,1536]{1,0:T(8,128)S(1)}, f32[48,1536]{1,0:T(8,128)S(1)}, u32[]{:S(2)}, u32[]{:S(2)}) collective-permute-start(f32[48,1536]{1,0:T(8,128)S(1)} %slice.268), channel_id=1, source_target_pairs={{16,0},{17,1},{18,2},{19,3},{20,4},{21,5},{22,6},{23,7},{24,8},{25... | collective-permute-start | bytes 884744 | tf_op jit(solution)/shard_map/ppermute | solution.py:609
  1218.0 28.1 %collective-permute-start.71 = (f32[48]{0:T(128)S(1)}, f32[48]{0:T(128)S(1)}, u32[]{:S(2)}, u32[]{:S(2)}) collective-permute-start(f32[48]{0:T(128)S(1)} %slice.234), channel_id=1, source_target_pairs={{16,0},{17,1},{18,2},{19,3},{20,4},{21,5},{22,6},{23,7},{24,8},{25... | collective-permute-start | bytes 584 | tf_op jit(solution)/shard_map/ppermute | solution.py:609
  (128 other events, 2784.7 us)
